TPU v7x, 32 devices: a whole 2x2x4 slice. The times are simulated.
32 devices in a mesh: dp: 8 (over z, x), rep: 4 (over y, core).
Axes of the slice: x: 2, y: 2, z: 4, core: 2. Of those that a mesh axis runs over, the one named last changes fastest.
Arguments:
- latents: bfloat16 [8192, 16], P(('dp', 'rep')), may hold values from -6 to 6
- route: int32 [8192], P(('dp', 'rep')), may hold values from 0 to 256, as said below
- labels: int32 [32], P(('dp', 'rep')), may hold values from 0 to 999
- timesteps: int32 [4, 8192], P(None, ('dp', 'rep')), may hold values from 0 to 999
- noise: float32 [4, 8192, 16], P(None, ('dp', 'rep')), may hold values from -6 to 6
- image_weight: float32 [32], P(('dp', 'rep')), may hold values from 0.5 to 1.5
- weights: float32 [22573056], P(('dp', 'rep')), as said below
- momentum: float32 [22573056], P(('dp', 'rep')), as said below
- average: float32 [22573056], P(('dp', 'rep')), as said below
Outputs:
- new_weights: float32 [22573056], P(('dp', 'rep'))
- new_momentum: float32 [22573056], P(('dp', 'rep'))
- new_average: float32 [22573056], P(('dp', 'rep'))
- loss: float32 [], replicated
Inputs may be any that keep to these rules, and one draw needn't show every extreme that they name: For each device's 1 * 256 tokens, images in order: a masked token has route = d * 32 + s, and the masked tokens of one device have distinct values; a visible token has route = 256. Each image has 179 or more masked tokens and at least one visible one. Some destination gets all 32 slots of a sender. `weights`: parameters in the layout of the first step. `momentum`: momentum of each parameter. `average`: average of each parameter.
All inputs are finite; a program needn't handle non-finite values.
Results may differ from a plain program's by a relative error of at most 0.00075.
The roundings to bfloat16 on the way count: a program that leaves them out, or rounds other values in their place, can miss the bound.
Values may be sent and summed in bfloat16 or wider, within the bound.
A program may use at most 384 MiB of HBM per device.

v0:
```python
import functools
import heapq
import math
import types

import jax
import jax.numpy as jnp
from jax import lax
from jax.experimental import pallas as pl
from jax.experimental.pallas import tpu as pltpu
from jax.sharding import PartitionSpec as P

D = 768
HEADS = 12
HEAD_DIM = 64
MLP = 3072
HW = 1024
TOK_CH = 16
FREQ = 256
CLASSES = 1000
BUF = 64
SEQ = 256
COPIES = 4
STEPS_T = 1000
LANES = 128
WIDE = jnp.float32
NARROW = jnp.bfloat16
NORM_EPS = 1e-06
MESH = pl.DeviceIdType.MESH
ANY = pl.BlockSpec(memory_space=pl.ANY)
DMA = pltpu.SemaphoreType.DMA
BOTH = ("dp", "rep")


def block_shapes():
    return dict(
        norm_one_gain=(D,), norm_one_shift=(D,), attn_weight=(D, 3 * D), attn_bias=(2 * D,),
        proj_weight=(D, D), proj_bias=(D,), norm_two_gain=(D,), norm_two_shift=(D,),
        fc_one_weight=(D, MLP), fc_one_bias=(MLP,), fc_two_weight=(MLP, D), fc_two_bias=(D,),
    )


ENC, DEC = 1, 3
GROUPS = (
    dict(embed_weight=(TOK_CH, D), embed_bias=(D,), class_table=(CLASSES, D), encoder_pos=(BUF + SEQ, D)),
    block_shapes(),
    dict(enc_gain=(D,), enc_shift=(D,), dec_weight=(D, D), dec_bias=(D,), mask_token=(D,), decoder_pos=(BUF + SEQ, D)),
    block_shapes(),
    dict(
        dec_gain=(D,), dec_shift=(D,), diffusion_pos=(SEQ, D), input_weight=(TOK_CH, HW), input_bias=(HW,),
        time_weight=(FREQ, HW), time_bias=(HW,), cond_weight=(D, HW), cond_bias=(HW,), head_gain=(HW,),
        head_shift=(HW,), ada_weight=(HW, 3 * HW), ada_bias=(3 * HW,), inner_weight=(HW, HW), inner_bias=(HW,),
        outer_weight=(HW, HW), outer_bias=(HW,), final_weight=(HW, TOK_CH), final_bias=(TOK_CH,),
    ),
)


class Entry:
    def __init__(self, group, name, shape, start):
        self.group, self.name, self.shape, self.start = group, name, shape, start
        self.rows = -(-math.prod(shape) // LANES)
        self.matrix = len(shape) == 2 and shape[1] % LANES == 0
        self.across = shape[1] // LANES if self.matrix else 1
        self.sparse = name == GROUP_SPARSE


GROUP_SPARSE = next(name for name, shape in GROUPS[0].items() if shape[0] == CLASSES)


def entries():
    found, start = [], 0
    for group, shapes in enumerate(GROUPS):
        for name, shape in shapes.items():
            found.append(Entry(group, name, shape, start))
            start += found[-1].rows
    return found


ENTRIES = entries()
USED = ENTRIES[-1].start + ENTRIES[-1].rows


def block_height(entry, limit):
    best = 0
    for height in range(8, entry.shape[0] + 1, 8):
        if entry.shape[0] % height == 0 and height * entry.across <= limit:
            best = height
    return best


SLOTS = 4


def unfold_kernel(rows, padded, items, g_ref, *refs):
    count = len(items)
    outs = refs[:count]
    first, second, wide, first_sem, second_sem, out_sem = refs[count : count + 6]
    stages = dict(zip(sorted({(h, e.across) for e, h in items}), refs[count + 6 :]))
    place = 0
    for t, (entry, height) in enumerate(items):
        span = height * entry.across
        window = span + 8
        blocks = entry.shape[0] // height
        stage = stages[(height, entry.across)]

        def spot(b, entry=entry, span=span, window=window):
            start = entry.start + b * span
            dev = start // rows
            row = start - dev * rows
            low = jnp.minimum(row // 8 * 8, padded - window)
            return dev, row, low, row + span > rows

        def copies(b, spot=spot, window=window):
            dev, row, low, more = spot(b)
            slot = b % SLOTS
            one = pltpu.make_async_copy(
                g_ref.at[dev, pl.ds(pl.multiple_of(low, 8), window)], first.at[slot, pl.ds(0, window)], first_sem.at[slot]
            )
            two = pltpu.make_async_copy(
                g_ref.at[jnp.minimum(dev + 1, g_ref.shape[0] - 1), pl.ds(0, window)],
                second.at[slot, pl.ds(0, window)], second_sem.at[slot],
            )
            return one, two, more

        def fetch(b, copies=copies):
            one, two, more = copies(b)
            one.start()

            @pl.when(more)
            def _():
                two.start()

        def put(b, t=t, stage=stage, height=height):
            return pltpu.make_async_copy(
                stage.at[b % 2], outs[t].at[pl.ds(pl.multiple_of(b * height, 8), height)], out_sem.at[b % 2]
            )

        for b in range(min(SLOTS - 1, blocks)):
            fetch(b)

        def body(b, carry, entry=entry, height=height, span=span, window=window, blocks=blocks, stage=stage,
                 spot=spot, copies=copies, fetch=fetch, put=put):
            @pl.when(b + SLOTS - 1 < blocks)
            def _():
                fetch(b + SLOTS - 1)

            dev, row, low, _ = spot(b)
            slot = b % SLOTS
            one, two, more = copies(b)
            one.wait()
            wide[pl.ds(0, window), :] = first[slot, pl.ds(0, window), :].astype(WIDE)

            @pl.when(more)
            def _():
                two.wait()
                wide[pl.ds(rows - low, window), :] = second[slot, pl.ds(0, window), :].astype(WIDE)

            @pl.when(b >= 2)
            def _():
                put(b - 2).wait()

            off = row - low
            for j in range(entry.across):
                stage[b % 2, :, j * LANES : (j + 1) * LANES] = wide[pl.ds(off + j, height, stride=entry.across), :].astype(NARROW)
            put(b).start()
            return carry

        lax.fori_loop(0, blocks, body, 0)
        for b in range(max(0, blocks - 2), blocks):
            put(b).wait()


def unfold(gathered, rows):
    padded = gathered.shape[1]
    items = [(e, block_height(e, min(2304, rows - 16))) for e in ENTRIES if e.matrix and not e.sparse]
    tall = max(e.across * h for e, h in items) + 8
    kinds = sorted({(h, e.across) for e, h in items})
    total = sum(math.prod(e.shape) for e, _ in items)
    outs = pl.pallas_call(
        functools.partial(unfold_kernel, rows, padded, items),
        out_shape=[jax.ShapeDtypeStruct(e.shape, NARROW) for e, _ in items],
        in_specs=[ANY],
        out_specs=[ANY] * len(items),
        scratch_shapes=[
            pltpu.VMEM((SLOTS, tall, LANES), NARROW), pltpu.VMEM((SLOTS, tall, LANES), NARROW),
            pltpu.VMEM((2 * tall, LANES), WIDE), DMA((SLOTS,)), DMA((SLOTS,)), DMA((2,)),
        ]
        + [pltpu.VMEM((2, h, n * LANES), NARROW) for h, n in kinds],
        compiler_params=pltpu.CompilerParams(vmem_limit_bytes=48 * 1000 * 1000),
        cost_estimate=pl.CostEstimate(flops=total, bytes_accessed=4 * total, transcendentals=0),
    )(gathered)
    return {(e.group, e.name): out for (e, _), out in zip(items, outs)}


def rows_at(gathered, rows, start, number):
    pieces = []
    while number > 0:
        dev, row = divmod(start, rows)
        take = min(number, rows - row)
        pieces.append(gathered[dev, row : row + take])
        start, number = start + take, number - take
    return pieces[0] if len(pieces) == 1 else jnp.concatenate(pieces, 0)


def unpack(gathered, rows):
    matrices = unfold(gathered, rows)
    groups = [types.SimpleNamespace() for _ in GROUPS]
    for e in ENTRIES:
        if e.sparse:
            continue
        if e.matrix:
            value = matrices[(e.group, e.name)]
        else:
            value = rows_at(gathered, rows, e.start, e.rows).reshape(-1)[: math.prod(e.shape)].reshape(e.shape)
        setattr(groups[e.group], e.name, value)
    return groups


DEPTH = 3


def fold_kernel(items, plain, *refs):
    count = len(items) + len(plain)
    ins, full = refs[:count], refs[count]
    plain_sem, in_sem, out_sem = refs[count + 1 : count + 4]
    kinds = sorted({(h, e.across) for e, h in items})
    loads = dict(zip(kinds, refs[count + 4 : count + 4 + len(kinds)]))
    stage = refs[count + 4 + len(kinds)]
    moves = []
    for i, (start, number) in enumerate(plain):
        move = pltpu.make_async_copy(ins[len(items) + i].at[pl.ds(0, number)], full.at[pl.ds(start, number)], plain_sem.at[i])
        move.start()
        moves.append(move)
    for t, (entry, height) in enumerate(items):
        span = height * entry.across
        blocks = entry.shape[0] // height
        load = loads[(height, entry.across)]

        def get(b, t=t, load=load, height=height):
            return pltpu.make_async_copy(
                ins[t].at[pl.ds(pl.multiple_of(b * height, 8), height)], load.at[b % DEPTH], in_sem.at[b % DEPTH]
            )

        def put(b, entry=entry, span=span):
            return pltpu.make_async_copy(
                stage.at[b % DEPTH, pl.ds(0, span)], full.at[pl.ds(entry.start + b * span, span)], out_sem.at[b % DEPTH]
            )

        for b in range(min(DEPTH - 1, blocks)):
            get(b).start()

        def body(b, carry, entry=entry, height=height, blocks=blocks, load=load, get=get, put=put):
            @pl.when(b + DEPTH - 1 < blocks)
            def _():
                get(b + DEPTH - 1).start()

            get(b).wait()

            @pl.when(b >= DEPTH)
            def _():
                put(b - DEPTH).wait()

            slot = b % DEPTH
            for j in range(entry.across):
                stage[slot, pl.ds(j, height, stride=entry.across), :] = load[slot, :, j * LANES : (j + 1) * LANES]
            put(b).start()
            return carry

        lax.fori_loop(0, blocks, body, 0)
        for b in range(max(0, blocks - DEPTH), blocks):
            put(b).wait()
    for move in moves:
        move.wait()


def fold(grads, height_total):
    items = [(e, block_height(e, 2304)) for e in ENTRIES if e.matrix]
    matrices = [grads[(e.group, e.name)] for e, _ in items]
    plain, values = [], []
    for e in ENTRIES:
        if e.matrix:
            continue
        value = grads[(e.group, e.name)].reshape(-1)
        value = jnp.pad(value, (0, e.rows * LANES - value.shape[0]))
        plain.append((e.start, e.rows))
        values.append(value.reshape(e.rows, LANES))
    if height_total > USED:
        plain.append((USED, height_total - USED))
        values.append(jnp.zeros((height_total - USED, LANES), WIDE))
    kinds = sorted({(h, e.across) for e, h in items})
    tall = max(e.across * h for e, h in items)
    total = height_total * LANES
    return pl.pallas_call(
        functools.partial(fold_kernel, items, plain),
        out_shape=jax.ShapeDtypeStruct((height_total, LANES), WIDE),
        in_specs=[ANY] * (len(items) + len(plain)),
        out_specs=ANY,
        scratch_shapes=[DMA((len(plain),)), DMA((DEPTH,)), DMA((DEPTH,))]
        + [pltpu.VMEM((DEPTH, h, n * LANES), WIDE) for h, n in kinds]
        + [pltpu.VMEM((DEPTH, tall, LANES), WIDE)],
        compiler_params=pltpu.CompilerParams(vmem_limit_bytes=48 * 1000 * 1000),
        cost_estimate=pl.CostEstimate(flops=total, bytes_accessed=8 * total, transcendentals=0),
    )(*matrices, *values)


X, Y, Z = 0, 1, 2
TREES = ((Z, X, Y), (Z, Y, X), (X, Z, Y), (X, Z, Y), (Y, Z, X), (Y, Z, X))
SHARES = len(TREES)
FAR = 3


def onward(order, arrived, way, p):
    z, x, y = p
    found = []
    if arrived >= 0 and order[arrived] == Z and 0 <= z + way <= FAR:
        found.append(((z + way, x, y), arrived, way))
    for j in range(arrived + 1, 3):
        if order[j] == X:
            found.append(((z, 1 - x, y), j, 0))
        elif order[j] == Y:
            found.append(((z, x, 1 - y), j, 0))
        else:
            found += [((z + s, x, y), j, s) for s in (1, -1) if 0 <= z + s <= FAR]
    return found


@functools.cache
def flow(lag=0.4):
    chips = [(z, x, y) for z in range(FAR + 1) for x in range(2) for y in range(2)]
    events, queues, busy, come, sent = [], {}, set(), {}, []
    number = iter(range(10**9))
    for u in range(SHARES):
        for p in chips:
            heapq.heappush(events, (0.0, next(number), 0, (p, p, u, -1, 0)))

    def pump(link, t):
        if link in busy or not queues.get(link):
            return
        what = heapq.heappop(queues[link])[2]
        busy.add(link)
        sent.append((t, link, what[1], what[2]))
        heapq.heappush(events, (t + 1.0, next(number), 1, (link, what)))

    while events:
        t, _, kind, what = heapq.heappop(events)
        if kind == 1:
            link, piece = what
            busy.discard(link)
            heapq.heappush(events, (t + lag, next(number), 0, piece))
            pump(link, t)
            continue
        p, q, u, k, way = what
        come[(u, p, q)] = t
        for to, k2, way2 in onward(TREES[u], k, way, p):
            left = len(onward(TREES[u], k2, way2, to))
            heapq.heappush(queues.setdefault((p, to), []), ((-left, t), next(number), (to, q, u, k2, way2)))
            pump((p, to), t)
    return come, sent


def spread_order():
    keyed = {}
    for (u, p, q), t in flow()[0].items():
        keyed.setdefault((u, q[0] - p[0], (q[1] - p[1]) % 2, (q[2] - p[2]) % 2), []).append(t)
    return sorted(keyed, key=lambda k: (sum(keyed[k]) / len(keyed[k]), k))


def last_hop(u, dz, dx, dy):
    apart = [k for k in range(3) if (dx, dy, dz)[TREES[u][k]] != 0]
    return apart[-1] if apart else -1


def hops(u, dz, dx, dy):
    order, arrived = TREES[u], last_hop(u, dz, dx, dy)
    found = []
    if arrived >= 0 and order[arrived] == Z:
        found.append((1, 0, 0) if dz < 0 else (-1, 0, 0))
    for k in range(arrived + 1, 3):
        found += [[(0, 1, 0)], [(0, 0, 1)], [(1, 0, 0), (-1, 0, 0)]][order[k]]
    return found


def only(condition, action):
    if condition is None:
        action()
    else:
        pl.when(condition)(action)


def spread_kernel(own, out, keep_sem, send_sem, link_sem, core_send, core_sem):
    dp, rep = lax.axis_index("dp"), lax.axis_index("rep")
    z, x, y, c = dp // 2, dp % 2, rep // 2, rep % 2
    unit = own.shape[0] // SHARES
    sibling = (dp, y * 2 + 1 - c)

    def device(dz, dx, dy):
        return ((z + dz) * 2 + (x + dx) % 2, (y + dy) % 2 * 2 + c)

    def exists(dz):
        return None if dz == 0 else (z + dz >= 0 if dz < 0 else z + dz <= FAR)

    barrier = pltpu.get_barrier_semaphore()
    near = ((0, 1, 0), (0, 0, 1), (1, 0, 0), (-1, 0, 0))
    for hop in near:
        only(exists(hop[0]), lambda: pl.semaphore_signal(barrier, inc=1, device_id=device(*hop), device_id_type=MESH))
    pl.semaphore_signal(barrier, inc=1, device_id=sibling, device_id_type=MESH)
    inner = z * (FAR - z)
    only(inner == 0, lambda: pl.semaphore_wait(barrier, len(near)))
    only(inner > 0, lambda: pl.semaphore_wait(barrier, len(near) + 1))
    keep = pltpu.make_async_copy(own, out.at[dp * 4 + rep], keep_sem)
    keep.start()
    ends, number = [], 0
    for u, dz, dx, dy in spread_order():
        part = pl.ds(u * unit, unit)
        q = ((z + dz) * 2 + (x + dx) % 2) * 2 + (y + dy) % 2
        mine = dz == 0 and dx == 0 and dy == 0
        i = u * 16 + q

        def copy(to, send, come, part=part, q=q, mine=mine):
            here = out.at[q * 2 + c, part]
            return pltpu.make_async_remote_copy(
                own.at[part] if mine else here, here, send, come, device_id=to, device_id_type=MESH
            )

        goes = [(hop, number + k) for k, hop in enumerate(hops(u, dz, dx, dy))]
        number += len(goes)

        def run(i=i, copy=copy, goes=goes, mine=mine):
            if not mine:
                copy(sibling, send_sem.at[0], link_sem.at[i]).wait_recv()
            for hop, n in goes:
                only(exists(hop[0]), lambda: copy(device(*hop), send_sem.at[n], link_sem.at[i]).start())
            copy(sibling, core_send.at[i], core_sem.at[i]).start()

        def finish(i=i, copy=copy, goes=goes):
            for hop, n in goes:
                only(exists(hop[0]), lambda: copy(device(*hop), send_sem.at[n], link_sem.at[i]).wait_send())
            copy(sibling, core_send.at[i], core_sem.at[i]).wait()

        there = None if dz == 0 else jnp.logical_and(z + dz >= 0, z + dz <= FAR)
        only(there, run)
        ends.append((there, finish))
    for there, finish in ends:
        only(there, finish)
    keep.wait()


def spread(own):
    pieces = SHARES * 16
    sends = sum(len(hops(*key)) for key in spread_order())
    return pl.pallas_call(
        spread_kernel,
        out_shape=jax.ShapeDtypeStruct((32,) + own.shape, own.dtype),
        in_specs=[ANY],
        out_specs=ANY,
        scratch_shapes=[DMA, DMA((sends,)), DMA((pieces,)), DMA((pieces,)), DMA((pieces,))],
        compiler_params=pltpu.CompilerParams(collective_id=0, has_side_effects=True),
    )(own)


class Chip:
    def __init__(self, low):
        dp, rep = lax.axis_index("dp"), lax.axis_index("rep")
        self.low = low
        self.z, self.x, self.y, self.c = dp // 2, dp % 2, rep // 2, rep % 2
        self.way = 1 - 2 * (self.z // 2)

    def device(self, q, other=0):
        z = self.z + self.way * (q[0] - self.low)
        return z * 2 + (self.x + q[1]) % 2, (self.y + q[2]) % 2 * 2 + (self.c + other) % 2

    def block(self, q, other=0):
        dp, rep = self.device(q, other)
        return dp * 4 + rep

    def greet(self):
        low = self.low
        near = [(low, 1, 0), (low, 0, 1), (low + 1, 0, 0)] + ([(low - 1, 0, 0)] if low else [])
        barrier = pltpu.get_barrier_semaphore()
        for q in near:
            pl.semaphore_signal(barrier, inc=1, device_id=self.device(q), device_id_type=MESH)
        pl.semaphore_signal(barrier, inc=1, device_id=self.device((low, 0, 0), 1), device_id_type=MESH)
        pl.semaphore_wait(barrier, len(near) + 1)


def seen_from(p, r):
    low, way = min(p[0], FAR - p[0]), 1 if p[0] < 2 else -1
    return low + way * (r[0] - p[0]), (r[1] - p[1]) % 2, (r[2] - p[2]) % 2


@functools.cache
def sum_programs():
    come, sent = flow()
    last = max(come.values())
    found = []
    for z in (0, 1):
        p = (z, 0, 0)
        kids, parent, when = {}, {}, {}
        for t, link, q, u in sent:
            if link[0] == p:
                kids.setdefault((u, q), []).append(link[1])
                if q == p:
                    when[(u, p)] = max(when.get((u, p), 0.0), last - t)
            if link[1] == p:
                parent[(u, q)] = link[0]
                when[(u, q)] = last - t - 1.0
        tasks = sorted(when, key=lambda k: (when[k], k))
        found.append([(u, q, sorted(kids.get((u, q), [])), parent.get((u, q))) for u, q in tasks])
    return found


@functools.cache
def landing():
    return [{key: i for i, key in enumerate((u, q, k) for u, q, kids, _ in tasks for k in kids)} for tasks in sum_programs()]


RING = 12
SIDE = 4
EARLY = 12
STEP = 40


def add_rows(into, terms):
    def body(i, carry):
        at = pl.ds(pl.multiple_of(i * STEP, 8), STEP)
        total = into[at, :]
        for term in terms:
            total = total + term[at, :]
        into[at, :] = total
        return carry

    lax.fori_loop(0, into.shape[0] // STEP, body, 0)


def collect_at(low, size, full, out, aside, store, ring, side, ring_sem, side_sem, send_sem, link_sem, core_send, core_sem, out_sem):
    chip = Chip(low)
    me = (low, 0, 0)
    tasks, spots = sum_programs()[low], landing()
    count, unit = len(tasks), ring.shape[1]
    chip.greet()

    def part(i, other=0):
        return full.at[pl.ds(chip.block(tasks[i][1], other) * size + tasks[i][0] * unit, unit)]

    def across(i):
        return pltpu.make_async_remote_copy(
            part(i, 1), aside.at[i], core_send.at[i], core_sem.at[i], device_id=chip.device(me, 1), device_id_type=MESH
        )

    def ours(i):
        return pltpu.make_async_copy(part(i), ring.at[i % RING], ring_sem.at[i % RING])

    def theirs(i):
        return pltpu.make_async_copy(aside.at[i], side.at[i % SIDE], side_sem.at[i % SIDE])

    def along(i, spot, to):
        return pltpu.make_async_remote_copy(
            ring.at[i % RING], store.at[spot], send_sem.at[i], link_sem.at[spot], device_id=chip.device(to), device_id_type=MESH
        )

    leaving = {}

    def fetch(i):
        if i - RING in leaving:
            leaving.pop(i - RING)()
        ours(i).start()
        across(i).wait_recv()
        theirs(i).start()

    for i in range(EARLY):
        across(i).start()
    for i in range(SIDE - 1):
        fetch(i)
    for i, (u, q, kids, to) in enumerate(tasks):
        if i + EARLY < count:
            across(i + EARLY).start()
        if i + SIDE - 1 < count:
            fetch(i + SIDE - 1)
        ours(i).wait()
        theirs(i).wait()
        terms = [side.at[i % SIDE]]
        for kid in kids:
            spot = spots[low][(u, q, kid)]
            along(i, spot, kid).wait_recv()
            terms.append(store.at[spot])
        add_rows(ring.at[i % RING], terms)
        if to is None:
            move = pltpu.make_async_copy(ring.at[i % RING], out.at[pl.ds(u * unit, unit)], out_sem.at[u])
            move.start()
            leaving[i] = move.wait
        else:
            move = along(i, spots[min(to[0], FAR - to[0])][(u, seen_from(to, q), seen_from(to, me))], to)
            move.start()
            leaving[i] = move.wait_send
    for i in list(leaving):
        leaving.pop(i)()
    for i in range(count):
        across(i).wait_send()


def collect_kernel(size, *refs):
    z = lax.axis_index("dp") // 2
    inner = z * (FAR - z)

    @pl.when(inner == 0)
    def _():
        collect_at(0, size, *refs)

    @pl.when(inner > 0)
    def _():
        collect_at(1, size, *refs)


def collect(full, size, rows):
    slots = max(len(spots) for spots in landing())
    count, unit = len(sum_programs()[0]), rows // SHARES
    return pl.pallas_call(
        functools.partial(collect_kernel, size),
        out_shape=(jax.ShapeDtypeStruct((rows, LANES), WIDE), jax.ShapeDtypeStruct((count, unit, LANES), WIDE)),
        in_specs=[ANY],
        out_specs=(ANY, ANY),
        scratch_shapes=[
            pltpu.VMEM((slots, unit, LANES), WIDE), pltpu.VMEM((RING, unit, LANES), WIDE), pltpu.VMEM((SIDE, unit, LANES), WIDE),
            DMA((RING,)), DMA((SIDE,)), DMA((count,)), DMA((slots,)), DMA((count,)), DMA((count,)), DMA((SHARES,)),
        ],
        compiler_params=pltpu.CompilerParams(collective_id=1, has_side_effects=True, vmem_limit_bytes=62 * 1000 * 1000),
    )(full)[0]


def layer_norm(value, gain, shift):
    centered = value - jnp.mean(value, -1, keepdims=True)
    scaled = centered * lax.rsqrt(jnp.mean(centered * centered, -1, keepdims=True) + NORM_EPS)
    return scaled * gain + shift


def dense(inputs, weight):
    return lax.dot_general(inputs, weight, (((inputs.ndim - 1,), (0,)), ((), ())), preferred_element_type=WIDE)


def back_input(grads_low, weight):
    return lax.dot_general(grads_low, weight, (((grads_low.ndim - 1,), (1,)), ((), ())), preferred_element_type=WIDE)


def weight_grad(inputs, grads_low):
    flat_in = inputs.reshape(-1, inputs.shape[-1])
    flat_grad = grads_low.reshape(-1, grads_low.shape[-1])
    return lax.dot_general(flat_in, flat_grad, (((0,), (0,)), ((), ())), preferred_element_type=WIDE)


def rows_sum(values):
    return jnp.sum(values.reshape(-1, values.shape[-1]), 0)


def norm_pull(value, gain, shift):
    return jax.vjp(layer_norm, value, gain.astype(WIDE), shift.astype(WIDE))[1]


def split_heads(mixed):
    return [mixed[:, part * D : (part + 1) * D].reshape(-1, HEADS, HEAD_DIM) for part in range(3)]


def masked_scores(queries, keys, keep):
    scores = jnp.einsum("qhe,khe->hqk", queries, keys, preferred_element_type=WIDE) * HEAD_DIM ** (-0.5)
    return scores if keep is None else jnp.where(keep[None, None, :], scores, -1e30)


def block_forward(stream, keep, p):
    normed = layer_norm(stream, p.norm_one_gain.astype(WIDE), p.norm_one_shift.astype(WIDE)).astype(NARROW)
    bias = jnp.concatenate([p.attn_bias[:D].astype(WIDE), jnp.zeros((D,), WIDE), p.attn_bias[D:].astype(WIDE)])
    mixed = (dense(normed, p.attn_weight) + bias).astype(NARROW)
    queries, keys, values = split_heads(mixed)
    scores = masked_scores(queries, keys, keep)
    totals = jax.nn.logsumexp(scores, axis=-1)
    probs = jnp.exp(scores - totals[..., None]).astype(NARROW)
    attended = jnp.einsum("hqk,khe->qhe", probs, values, preferred_element_type=WIDE)
    attended = attended.reshape(-1, D).astype(NARROW)
    middle = stream + dense(attended, p.proj_weight) + p.proj_bias.astype(WIDE)
    second = layer_norm(middle, p.norm_two_gain.astype(WIDE), p.norm_two_shift.astype(WIDE)).astype(NARROW)
    inner = dense(second, p.fc_one_weight) + p.fc_one_bias.astype(WIDE)
    active = jax.nn.gelu(inner, approximate=False).astype(NARROW)
    output = middle + dense(active, p.fc_two_weight) + p.fc_two_bias.astype(WIDE)
    return output, (stream, normed, mixed, totals, attended, middle, second, inner, active)


def block_backward(grad_out, keep, p, saved):
    stream, normed, mixed, totals, attended, middle, second, inner, active = saved
    grads = {}
    out_low = grad_out.astype(NARROW)
    fc_two_weight = weight_grad(active, out_low)
    fc_two_bias = rows_sum(grad_out)
    gelu_pull = jax.vjp(lambda value: jax.nn.gelu(value, approximate=False), inner)[1]
    inner_grad = gelu_pull(back_input(out_low, p.fc_two_weight))[0]
    inner_low = inner_grad.astype(NARROW)
    fc_one_weight = weight_grad(second, inner_low)
    fc_one_bias = rows_sum(inner_grad)
    pull = norm_pull(middle, p.norm_two_gain, p.norm_two_shift)
    middle_grad, norm_two_gain, norm_two_shift = pull(back_input(inner_low, p.fc_one_weight))
    middle_grad = middle_grad + grad_out
    middle_low = middle_grad.astype(NARROW)
    proj_weight = weight_grad(attended, middle_low)
    proj_bias = rows_sum(middle_grad)
    attended_grad = back_input(middle_low, p.proj_weight).astype(NARROW).reshape(-1, HEADS, HEAD_DIM)
    queries, keys, values = split_heads(mixed)
    probs = jnp.exp(masked_scores(queries, keys, keep) - totals[..., None])
    values_grad = jnp.einsum("hqk,qhe->khe", probs.astype(NARROW), attended_grad, preferred_element_type=WIDE)
    prob_grad = jnp.einsum("qhe,khe->hqk", attended_grad, values, preferred_element_type=WIDE)
    score_grad = (probs * (prob_grad - jnp.sum(probs * prob_grad, -1, keepdims=True))).astype(NARROW)
    scale = HEAD_DIM ** (-0.5)
    query_grad = jnp.einsum("hqk,khe->qhe", score_grad, keys, preferred_element_type=WIDE) * scale
    key_grad = jnp.einsum("hqk,qhe->khe", score_grad, queries, preferred_element_type=WIDE) * scale
    parts = [item.reshape(-1, D) for item in (query_grad, key_grad, values_grad)]
    attn_bias = jnp.concatenate([rows_sum(parts[0]), rows_sum(parts[2])])
    mixed_low = jnp.concatenate(parts, -1).astype(NARROW)
    attn_weight = weight_grad(normed, mixed_low)
    pull = norm_pull(stream, p.norm_one_gain, p.norm_one_shift)
    stream_grad, norm_one_gain, norm_one_shift = pull(back_input(mixed_low, p.attn_weight))
    grads = dict(
        norm_one_gain=norm_one_gain, norm_one_shift=norm_one_shift, attn_weight=attn_weight, attn_bias=attn_bias,
        proj_weight=proj_weight, proj_bias=proj_bias, norm_two_gain=norm_two_gain, norm_two_shift=norm_two_shift,
        fc_one_weight=fc_one_weight, fc_one_bias=fc_one_bias, fc_two_weight=fc_two_weight, fc_two_bias=fc_two_bias,
    )
    return stream_grad + middle_grad, grads


def time_features(times):
    half = FREQ // 2
    freqs = jnp.exp(-math.log(10000.0) * jnp.arange(half, dtype=WIDE) / half)
    angles = times[..., None] * freqs
    return jnp.concatenate([jnp.cos(angles), jnp.sin(angles)], -1)


def alpha_level(times):
    start = math.cos(0.008 / 1.008 * math.pi / 2) ** 2
    return jnp.cos(((times + 1.0) / STEPS_T + 0.008) / 1.008 * math.pi / 2) ** 2 / start


def head_pass(p, conditions, clean, filled, steps, noise, divisor):
    cond = dense(conditions, p.cond_weight) + p.cond_bias.astype(WIDE)
    times = steps.astype(WIDE)
    features = time_features(times).astype(NARROW)
    temporal = dense(features, p.time_weight) + p.time_bias.astype(WIDE)
    level = alpha_level(times)[..., None]
    noisy = (jnp.sqrt(level) * clean.astype(WIDE) + jnp.sqrt(1.0 - level) * noise).astype(NARROW)
    hidden_in = dense(noisy, p.input_weight) + p.input_bias.astype(WIDE)
    joined = temporal + cond[None]
    signal = jax.nn.silu(joined).astype(NARROW)
    modulation = dense(signal, p.ada_weight) + p.ada_bias.astype(WIDE)
    normed = layer_norm(hidden_in, p.head_gain.astype(WIDE), p.head_shift.astype(WIDE))
    modulated = (normed * (1.0 + modulation[..., HW : 2 * HW]) + modulation[..., :HW]).astype(NARROW)
    inner = dense(modulated, p.inner_weight) + p.inner_bias.astype(WIDE)
    active = jax.nn.silu(inner).astype(NARROW)
    outer = dense(active, p.outer_weight) + p.outer_bias.astype(WIDE)
    hidden = hidden_in + modulation[..., 2 * HW :] * outer
    final = layer_norm(hidden, 1.0, 0.0).astype(NARROW)
    predicted = dense(final, p.final_weight) + p.final_bias.astype(WIDE)
    error = predicted - noise
    marks = filled.astype(WIDE)
    loss_part = jnp.sum(jnp.sum(error * error, -1) * marks)
    pred_grad = 2.0 * error * marks[:, None] / divisor
    pred_low = pred_grad.astype(NARROW)
    hidden_grad = jax.vjp(lambda value: layer_norm(value, 1.0, 0.0), hidden)[1](back_input(pred_low, p.final_weight))[0]
    gate_grad = hidden_grad * outer
    outer_grad = hidden_grad * modulation[..., 2 * HW :]
    outer_low = outer_grad.astype(NARROW)
    inner_grad = jax.vjp(jax.nn.silu, inner)[1](back_input(outer_low, p.outer_weight))[0]
    inner_low = inner_grad.astype(NARROW)
    mod_grad = back_input(inner_low, p.inner_weight)
    pull = norm_pull(hidden_in, p.head_gain, p.head_shift)
    norm_grad, head_gain, head_shift = pull(mod_grad * (1.0 + modulation[..., HW : 2 * HW]))
    hidden_grad = hidden_grad + norm_grad
    modulation_grad = jnp.concatenate([mod_grad, mod_grad * normed, gate_grad], -1)
    modulation_low = modulation_grad.astype(NARROW)
    signal_grad = back_input(modulation_low, p.ada_weight)
    joined_grad = jax.vjp(jax.nn.silu, joined)[1](signal_grad)[0]
    joined_low = joined_grad.astype(NARROW)
    cond_grad = jnp.sum(joined_grad, 0)
    cond_low = cond_grad.astype(NARROW)
    hidden_low = hidden_grad.astype(NARROW)
    grads = dict(
        final_weight=weight_grad(final, pred_low), final_bias=rows_sum(pred_grad),
        outer_weight=weight_grad(active, outer_low), outer_bias=rows_sum(outer_grad),
        inner_weight=weight_grad(modulated, inner_low), inner_bias=rows_sum(inner_grad),
        head_gain=head_gain, head_shift=head_shift,
        ada_weight=weight_grad(signal, modulation_low), ada_bias=rows_sum(modulation_grad),
        time_weight=weight_grad(features, joined_low), time_bias=rows_sum(joined_grad),
        cond_weight=weight_grad(conditions, cond_low), cond_bias=rows_sum(cond_grad),
        input_weight=weight_grad(noisy, hidden_low), input_bias=rows_sum(hidden_grad),
    )
    return loss_part, grads, back_input(cond_low, p.cond_weight)


def exchange(payload, parts):
    shape = payload.shape
    moved = lax.all_to_all(payload.reshape(parts, -1, shape[-1]), "dp", split_axis=0, concat_axis=0, tiled=True)
    return moved.reshape(shape)


def body(latents, route, labels, timesteps, noise, image_weight, weights, momentum, average):
    ranks_dp, ranks_rep = lax.axis_size("dp"), lax.axis_size("rep")
    ranks = ranks_dp * ranks_rep
    meshed = (ranks_dp, ranks_rep) == (8, 4)
    rows = route.shape[0]
    images = labels.shape[0]
    assert images == 1 and rows == SEQ
    size = weights.shape[0] // LANES
    padded = -(-(size + 1) // 48) * 48
    masked = route < rows
    own = jnp.sum(masked.astype(WIDE))
    low = weights.reshape(size, LANES).astype(NARROW)
    extra = jnp.full((padded - size, LANES), own).astype(NARROW)
    block = jnp.concatenate([low, extra], 0)
    gathered = spread(block) if meshed else lax.all_gather(block, BOTH, axis=0)
    base, enc, mid, dec, head = unpack(gathered, size)
    count = jnp.sum(gathered[:, size, 0].astype(WIDE))
    keep = jnp.concatenate([jnp.ones((BUF,), bool), ~masked])
    tokens = dense(latents, base.embed_weight) + base.embed_bias.astype(WIDE)
    at = next(e.start for e in ENTRIES if e.sparse) + labels[0] * (D // LANES) + jnp.arange(D // LANES, dtype=jnp.int32)
    classes = gathered[at // size, at % size].reshape(1, D).astype(WIDE)
    stream = jnp.concatenate([jnp.broadcast_to(classes, (BUF, D)), tokens], 0) + base.encoder_pos.astype(WIDE)
    stream, enc_stored = block_forward(stream, keep, enc)
    encoded = layer_norm(stream, mid.enc_gain.astype(WIDE), mid.enc_shift.astype(WIDE)).astype(NARROW)
    decoded = dense(encoded, mid.dec_weight) + mid.dec_bias.astype(WIDE)
    decoded = jnp.where(keep[:, None], decoded, mid.mask_token.astype(WIDE))
    before = decoded + mid.decoder_pos.astype(WIDE)
    flow_out, dec_stored = block_forward(before, None, dec)
    after = layer_norm(flow_out, head.dec_gain.astype(WIDE), head.dec_shift.astype(WIDE))
    conditions = (after[BUF:] + head.diffusion_pos.astype(WIDE)).astype(NARROW)
    token_weight = jnp.broadcast_to(image_weight.astype(NARROW)[:, None], (rows, 1))
    payload = jnp.concatenate([conditions, latents, token_weight, jnp.zeros((rows, LANES - TOK_CH - 1), NARROW)], 1)
    picks = (jnp.arange(rows, dtype=jnp.int32)[:, None] == route[None, :]).astype(NARROW)
    arrived = exchange(dense(picks, payload).astype(NARROW), ranks_dp)
    divisor = TOK_CH * COPIES * count
    loss_part, head_grads, cond_back = head_pass(
        head, arrived[:, :D], arrived[:, D : D + TOK_CH], arrived[:, D + TOK_CH], timesteps, noise, divisor
    )
    returned = exchange(cond_back.astype(NARROW), ranks_dp)
    token_grad = lax.dot_general(picks, returned, (((0,), (0,)), ((), ())), preferred_element_type=WIDE)
    loss = lax.psum(loss_part, BOTH) / divisor
    after_grad = jnp.concatenate([jnp.zeros((BUF, D), WIDE), token_grad], 0)
    flow_grad, dec_gain, dec_shift = norm_pull(flow_out, head.dec_gain, head.dec_shift)(after_grad)
    head_grads.update(diffusion_pos=token_grad, dec_gain=dec_gain, dec_shift=dec_shift)
    before_grad, dec_grads = block_backward(flow_grad, None, dec, dec_stored)
    decoded_grad = jnp.where(keep[:, None], before_grad, 0.0)
    decoded_low = decoded_grad.astype(NARROW)
    pull = norm_pull(stream, mid.enc_gain, mid.enc_shift)
    stream_grad, enc_gain, enc_shift = pull(back_input(decoded_low, mid.dec_weight))
    mid_grads = dict(
        enc_gain=enc_gain, enc_shift=enc_shift, dec_weight=weight_grad(encoded, decoded_low), dec_bias=rows_sum(decoded_grad),
        mask_token=rows_sum(jnp.where(keep[:, None], 0.0, before_grad)), decoder_pos=before_grad,
    )
    stream_grad, enc_grads = block_backward(stream_grad, keep, enc, enc_stored)
    token_in = stream_grad[BUF:]
    base_grads = dict(
        encoder_pos=stream_grad,
        class_table=jnp.zeros((CLASSES, D), WIDE).at[labels].add(jnp.sum(stream_grad[:BUF], 0)[None]),
        embed_weight=weight_grad(latents, token_in.astype(NARROW)), embed_bias=rows_sum(token_in),
    )
    grads = {}
    for group, found in enumerate((base_grads, enc_grads, mid_grads, dec_grads, head_grads)):
        grads.update({(group, name): value for name, value in found.items()})
    height = -(-((ranks - 1) * size + padded) // 8) * 8
    full = fold(grads, height)
    if meshed:
        owned = collect(full, size, padded)[:size]
    else:
        owned = lax.psum_scatter(full[: ranks * size].reshape(ranks, size, LANES), BOTH, scatter_dimension=0, tiled=False)
    owned = owned.reshape(-1)
    rate = 0.05 * math.sqrt(images * ranks * SEQ)
    new_momentum = 0.9 * momentum + owned
    new_weights = weights - rate * (owned + 0.9 * new_momentum)
    new_average = 0.75 * average + 0.25 * new_weights
    return new_weights, new_momentum, new_average, loss


def solution(mesh):
    flat = P(BOTH)
    placed = (P(BOTH, None), flat, flat, P(None, BOTH), P(None, BOTH, None), flat, flat, flat, flat)
    return jax.shard_map(body, mesh=mesh, in_specs=placed, out_specs=(flat, flat, flat, P()), check_vma=False)
```

profile of v0, /device:TPU:21, one launch (start us, length us, event | category | flops | bytes accessed | tf_op | source)
XLA Modules:
  0.0 1023.9 jit_solution(14803174194272856474)
XLA Ops:
  3.1 1.9 convert_bitcast_fusion
  5.1 1.8 concatenate.59.own
  6.9 161.8 %shard_map.120.g_ref = bf16[32,5520,128]{2,1,0:T(8,128)(2,1)} custom-call(bf16[5520,128]{1,0:T(8,128)(2,1)} %concatenate.59.own), custom_call_target="tpu_custom_call" | custom-call | tf_op jit(solution)/shard_map/pallas_call | solution.py:451
  172.3 62.5 %shard_map.121 = (bf16[16,768]{1,0:T(8,128)(2,1)S(1)}, bf16[320,768]{1,0:T(8,128)(2,1)S(1)}, bf16[768,2304]{1,0:T(8,128)(2,1)}, bf16[768,768]{1,0:T(8,128)(2,1)S...) custom-call(bf16[32,5520,128]{2,1,0:T(8,128)(2,1)} %shard_map.120.g_ref), custom_call_target="tpu_custom_call" | custom-call | flops 21753856 | bytes 87015424 | tf_op jit(solution)/shard_map/pallas_call | solution.py:179
  249.8 2.3 copy.123
  252.1 2.1 copy.122
  254.3 2.7 fusion.8
  258.5 1.5 convolution_convert_fusion.1
  260.1 1.7 copy-done.18
  262.9 13.3 %multiply_convert_fusion.6 = (bf16[320,3072]{1,0:T(8,128)(2,1)S(1)}, f32[320,3072]{1,0:T(8,128)}, f32[320,3072]{1,0:T(8,128)}) fusion(f32[3072]{0:T(1024)S(1)} %copy-done.130, bf16[768,3072]{1,0:T(8,128)(2,1)S(1)} %bitcast.388, f32[320,768]{1,0:T(8,128)S(1)} %get-tuple-element.178, f32[768]{0:T(1024)S(1)} %get-tuple-element.143, ...), kind=kOutput, calls=%fused_computation.73 | convolution fusion | flops 1576058880 | bytes 15553024 | tf_op jit(solution)/shard_map/dot_general | solution.py:637
  276.3 1.8 fusion.186
  283.9 1.5 copy.126
  291.7 13.0 %multiply_convert_fusion.5 = (bf16[320,3072]{1,0:T(8,128)(2,1)S(1)}, f32[320,3072]{1,0:T(8,128)}, f32[320,3072]{1,0:T(8,128)}) fusion(f32[3072]{0:T(1024)S(1)} %copy-done.129, bf16[768,3072]{1,0:T(8,128)(2,1)S(1)} %bitcast.396, f32[320,768]{1,0:T(8,128)S(1)} %get-tuple-element.187, f32[768]{0:T(1024)S(1)} %get-tuple-element.131, ...), kind=kOutput, calls=%fused_computation.60 | convolution fusion | flops 1576058880 | bytes 15553024 | tf_op jit(solution)/shard_map/dot_general | solution.py:637
  304.8 1.8 fusion.189
  308.6 9.9 all-to-all-start
  324.0 2.2 fusion.89
  327.1 2.8 fusion.91
  333.3 9.0 broadcast_add_fusion
  342.4 1.6 fusion.13
  344.0 4.3 fusion.40
  348.3 7.5 fusion.175
  357.5 2.1 convolution_bitcast_fusion.5
  360.7 1.7 fusion.174
  364.0 7.1 fusion.192
  371.1 4.4 convolution_bitcast_fusion.1.refs_19_
  375.6 10.2 multiply_reduce_fusion.3
  385.8 3.1 fusion.166
  391.1 2.8 fusion.59
  393.9 15.7 %fusion.162 = (f32[1024]{0:T(1024)S(1)}, bf16[256,1024]{1,0:T(8,128)(2,1)}, bf16[4,256,1024]{2,1,0:T(8,128)(2,1)}) fusion(f32[256,1024]{1,0:T(8,128)} %copy-done.71, f32[4,256,1024]{2,1,0:T(8,128)} %fusion.91, f32[1024]{0:T(1024)S(1)} %get-tuple-element.123, bf16[1024,3072]{1,0:T(8,128)(2,1)} %get-tuple-element.52, ...), kind=kOutput, calls=%fused_computation.384 | convolution fusion | flops 6475742208 | bytes 26746880 | tf_op jit(solution)/shard_map/dot_general | solution.py:641
  409.6 5.1 fusion
  414.7 17.6 %convolution_bitcast_fusion.refs_17_ = f32[1024,3072]{1,0:T(8,128)} fusion(f32[4,256,1024]{2,1,0:T(8,128)} %get-tuple-element.152, f32[4,256,1024]{2,1,0:T(8,128)} %get-tuple-element.151, f32[4,256,1024]{2,1,0:T(8,128)} %get-tuple-element.196, f32[4,256,1024]{2,1,0:T(8,128)} %fusion.91, f32[256,1024]{1,0:T(8,128)} %copy-done.71, f32[1024]{0:T(1024)S(1)} %get-tuple-element.123), kind=kOutput, calls=%fused_computation.4 | convolution fusion | flops 6468665344 | bytes 30412800 | tf_op jit(solution)/shard_map/dot_general | solution.py:647
  432.3 2.5 convolution_convert_fusion.5
  434.8 3.4 fusion.100.refs_16_
  438.7 5.6 all-to-all-start.1
  444.3 3.4 fusion.52.refs_15_
  447.7 41.1 %psum.7 = f32[]{:T(128)} all-reduce(f32[]{:T(128)} %multiply_reduce_fusion.26), channel_id=1, replica_groups=mesh['dp'=8,'rep'=4] {'dp','rep'}, use_global_device_ids=true, to_apply=%region_78.79 | all-reduce | flops 1 | bytes 8 | tf_op jit(solution)/shard_map/psum | solution.py:838
  489.7 6.6 convolution_bitcast_fusion.2.refs_18_
  496.7 1.8 pad_reduce_fusion
  498.5 2.1 fusion.173
  500.7 7.4 fusion.191
  508.1 2.0 multiply_reduce_fusion.8
  512.0 2.2 fusion.112.refs_10_
  514.5 4.1 fusion.182
  518.6 4.5 multiply_reduce_fusion.1
  527.1 1.9 multiply_reduce_fusion.9
  531.6 2.4 fusion.152.refs_7_
  534.6 5.6 fusion.190
  540.3 2.0 multiply_reduce_fusion.11
  544.2 2.2 fusion.109.refs_4_
  546.4 5.2 fusion.87.refs_9_
  551.9 4.4 fusion.184
  556.4 5.0 multiply_reduce_fusion
  561.4 2.0 multiply_convert_fusion
  566.0 1.9 multiply_reduce_fusion.12
  568.8 5.1 fusion.85.refs_3_
  574.0 5.3 fusion.74.refs_5_
  579.3 5.3 fusion.78.refs_11_
  584.7 5.2 fusion.156.refs_6_
  589.9 5.4 fusion.154.refs_12_
  596.3 1.8 broadcast_in_dim.105
  599.5 1.7 copy-done
  602.4 86.4 %shard_map.122.refs_0_ = f32[176368,128]{1,0:T(8,128)} custom-call(f32[16,768]{1,0:T(8,128)S(1)} %convolution_bitcast_fusion.6.refs_0_, f32[1000,768]{1,0:T(8,128)} %scatter-add.4.refs_1_, f32[320,768]{1,0:T(8,128)S(1)} %add_add_fusion.11.refs_2_, f32[768,2304]{1,0:T(8,128)} %fusion.85.refs_3_, f32[768,768]{1,0:T(8,128)S(1)} %copy-done, ...), custom_call_target="tpu_custom_call" | custom-call | flops 22575104 | bytes 180600832 | tf_op jit(solution)/shard_map/pallas_call | solution.py:293
  688.8 325.9 %shard_map.123 = (f32[5520,128]{1,0:T(8,128)}, f32[96,920,128]{2,1,0:T(8,128)}) custom-call(f32[176368,128]{1,0:T(8,128)} %shard_map.122.refs_0_), custom_call_target="tpu_custom_call" | custom-call | tf_op jit(solution)/shard_map/pallas_call | solution.py:617
  1014.7 7.6 multiply_add_fusion.4
  (479 shorter events, 70.4 us)
Async XLA Ops:
  169.5 75.4 %copy-start.79 = (f32[768]{0:T(1024)}, f32[768]{0:T(1024)S(1)}, u32[]{:S(2)}) copy-start(f32[768]{0:T(1024)S(1)} %get-tuple-element.147) | copy-start | bytes 9220
  169.5 75.4 %copy-start.89 = (f32[768]{0:T(1024)}, f32[768]{0:T(1024)S(1)}, u32[]{:S(2)}) copy-start(f32[768]{0:T(1024)S(1)} %get-tuple-element.149) | copy-start | bytes 9220
  172.2 90.6 %copy-start.75 = (f32[768]{0:T(1024)}, f32[768]{0:T(1024)S(1)}, u32[]{:S(2)}) copy-start(f32[768]{0:T(1024)S(1)} %get-tuple-element.144) | copy-start | bytes 9220
  172.3 90.6 %copy-start.85 = (f32[768]{0:T(1024)}, f32[768]{0:T(1024)S(1)}, u32[]{:S(2)}) copy-start(f32[768]{0:T(1024)S(1)} %get-tuple-element.143) | copy-start | bytes 9220
  172.3 106.2 %copy-start.106 = (f32[768]{0:T(1024)}, f32[768]{0:T(1024)S(1)}, u32[]{:S(2)}) copy-start(f32[768]{0:T(1024)S(1)} %get-tuple-element.141) | copy-start | bytes 9220
  172.3 106.2 %copy-start.125 = (f32[768]{0:T(1024)}, f32[768]{0:T(1024)S(1)}, u32[]{:S(2)}) copy-start(f32[768]{0:T(1024)S(1)} %get-tuple-element.140) | copy-start | bytes 9220
  172.3 107.4 %copy-start.77 = (f32[768]{0:T(1024)}, f32[768]{0:T(1024)S(1)}, u32[]{:S(2)}) copy-start(f32[768]{0:T(1024)S(1)} %get-tuple-element.137) | copy-start | bytes 9220
  172.3 107.4 %copy-start.87 = (f32[768]{0:T(1024)}, f32[768]{0:T(1024)S(1)}, u32[]{:S(2)}) copy-start(f32[768]{0:T(1024)S(1)} %get-tuple-element.136) | copy-start | bytes 9220
  172.3 118.2 %copy-start.83 = (f32[768]{0:T(1024)}, f32[768]{0:T(1024)S(1)}, u32[]{:S(2)}) copy-start(f32[768]{0:T(1024)S(1)} %get-tuple-element.131) | copy-start | bytes 9220
  172.3 69.0 %copy-start.91 = (bf16[256,16]{0,1:T(8,128)(2,1)S(1)}, bf16[256,16]{0,1:T(8,128)(2,1)}, u32[]{:S(2)}) copy-start(bf16[256,16]{0,1:T(8,128)(2,1)} %param.11) | copy-start | bytes 24580
  238.6 21.5 %copy-start.1 = (bf16[768,768]{1,0:T(8,128)(2,1)}, bf16[768,768]{1,0:T(8,128)(2,1)S(1)}, u32[]{:S(2)}) copy-start(bf16[768,768]{1,0:T(8,128)(2,1)S(1)} %get-tuple-element.39) | copy-start | bytes 3538948
  238.6 50.4 %copy-start.3 = (bf16[768,768]{1,0:T(8,128)(2,1)}, bf16[768,768]{1,0:T(8,128)(2,1)S(1)}, u32[]{:S(2)}) copy-start(bf16[768,768]{1,0:T(8,128)(2,1)S(1)} %get-tuple-element.45) | copy-start | bytes 3538948
  247.2 7.0 copy-start.146
  249.8 7.2 copy-start.40
  254.3 24.2 %copy-start.110 = (pred[320]{0:T(512)(128)(4,1)}, pred[320]{0:T(512)(128)(4,1)S(1)}, u32[]{:S(2)}) copy-start(pred[320]{0:T(512)(128)(4,1)S(1)} %concatenate.63) | copy-start | bytes 964
  257.0 5.8 slice-start.4
  260.1 16.1 %copy-start.57 = (bf16[12,64,320]{2,1,0:T(8,128)(2,1)}, bf16[12,64,320]{2,1,0:T(8,128)(2,1)S(1)}, u32[]{:S(2)}) copy-start(bf16[12,64,320]{2,1,0:T(8,128)(2,1)S(1)} %convolution_convert_fusion.1) | copy-start | bytes 1474564
  261.8 14.5 %slice-start.8 = ((s8[4718592]{0:T(1024)(128)(4,1)}), s8[4194304]{0:T(1024)(128)(4,1)S(1)}, s32[]{:S(2)}) async-start(s8[4718592]{0:T(1024)(128)(4,1)} %bitcast.391), calls=%async_computation.10 | async-start | bytes 8388608
  262.5 13.7 %copy-start.20 = (f32[320,768]{1,0:T(8,128)}, f32[320,768]{1,0:T(8,128)S(1)}, u32[]{:S(2)}) copy-start(f32[320,768]{1,0:T(8,128)S(1)} %get-tuple-element.178) | copy-start | bytes 2949124
  262.5 13.7 %copy-start.93 = (f32[320]{0:T(512)}, f32[320]{0:T(512)S(1)}, u32[]{:S(2)}) copy-start(f32[320]{0:T(512)S(1)} %broadcast_multiply_fusion.6) | copy-start | bytes 3844
  262.8 13.4 %copy-start.114 = (f32[320]{0:T(512)}, f32[320]{0:T(512)S(1)}, u32[]{:S(2)}) copy-start(f32[320]{0:T(512)S(1)} %multiply_reduce_fusion.23) | copy-start | bytes 3844
  262.8 13.4 %copy-start.100 = (f32[320]{0:T(512)}, f32[320]{0:T(512)S(1)}, u32[]{:S(2)}) copy-start(f32[320]{0:T(512)S(1)} %fusion.128) | copy-start | bytes 3844
  262.9 13.4 %copy-start.135 = (f32[768]{0:T(1024)S(1)}, f32[768]{0:T(1024)}, u32[]{:S(2)}) copy-start(f32[768]{0:T(1024)} %get-tuple-element.142) | copy-start | bytes 9220
  262.9 13.4 %slice-start.9 = ((s8[4718592]{0:T(1024)(128)(4,1)}), s8[524288]{0:T(1024)(128)(4,1)S(1)}, s32[]{:S(2)}) async-start(s8[4718592]{0:T(1024)(128)(4,1)} %bitcast.391), calls=%async_computation.11 | async-start | bytes 1048576
  289.0 15.7 %copy-start.47 = (bf16[12,64,320]{2,1,0:T(8,128)(2,1)}, bf16[12,64,320]{2,1,0:T(8,128)(2,1)S(1)}, u32[]{:S(2)}) copy-start(bf16[12,64,320]{2,1,0:T(8,128)(2,1)S(1)} %convolution_convert_fusion) | copy-start | bytes 1474564
  289.5 15.2 %slice-start.16 = ((s8[4718592]{0:T(1024)(128)(4,1)}), s8[4194304]{0:T(1024)(128)(4,1)S(1)}, s32[]{:S(2)}) async-start(s8[4718592]{0:T(1024)(128)(4,1)} %bitcast.399), calls=%async_computation.18 | async-start | bytes 8388608
  290.3 219.9 %copy-start.23 = (f32[320,768]{1,0:T(8,128)}, f32[320,768]{1,0:T(8,128)S(1)}, u32[]{:S(2)}) copy-start(f32[320,768]{1,0:T(8,128)S(1)} %get-tuple-element.187) | copy-start | bytes 2949124
  290.5 14.2 %copy-start.120 = (f32[320]{0:T(512)}, f32[320]{0:T(512)S(1)}, u32[]{:S(2)}) copy-start(f32[320]{0:T(512)S(1)} %multiply_reduce_fusion.20) | copy-start | bytes 3844
  291.7 13.0 %copy-start.132 = (f32[768]{0:T(1024)S(1)}, f32[768]{0:T(1024)}, u32[]{:S(2)}) copy-start(f32[768]{0:T(1024)} %get-tuple-element.130) | copy-start | bytes 9220
  291.7 13.0 %slice-start.17 = ((s8[4718592]{0:T(1024)(128)(4,1)}), s8[524288]{0:T(1024)(128)(4,1)S(1)}, s32[]{:S(2)}) async-start(s8[4718592]{0:T(1024)(128)(4,1)} %bitcast.399), calls=%async_computation.19 | async-start | bytes 1048576
  306.6 19.7 %copy-start.25 = (f32[320,768]{1,0:T(8,128)}, f32[320,768]{1,0:T(8,128)S(1)}, u32[]{:S(2)}) copy-start(f32[320,768]{1,0:T(8,128)S(1)} %get-tuple-element.190) | copy-start | bytes 2949124
  306.7 11.9 %copy-start.124 = (s32[4,256]{1,0:T(4,128)S(1)}, s32[4,256]{1,0:T(4,128)}, u32[]{:S(2)}) copy-start(s32[4,256]{1,0:T(4,128)} %param.14) | copy-start | bytes 12292
  306.7 15.3 %copy-start.140 = (s32[2]{0:T(128)S(1)}, s32[2]{0:T(128)}, u32[]{:S(2)}) copy-start(s32[2]{0:T(128)} %constant.217.clone.1) | copy-start | bytes 28
  308.6 21.5 %copy-start.74 = (f32[4,256,16]{1,2,0:T(8,128)S(1)}, f32[4,256,16]{1,2,0:T(8,128)}, u32[]{:S(2)}) copy-start(f32[4,256,16]{1,2,0:T(8,128)} %param.15) | copy-start | bytes 196612
  308.6 21.2 %all-to-all-start = ((bf16[8,32,896]{2,1,0:T(8,128)(2,1)}), bf16[8,32,896]{2,1,0:T(8,128)(2,1)S(1)}, u32[]{:S(2)}, u32[]{:S(2)}) async-start(bf16[8,32,896]{2,1,0:T(8,128)(2,1)} %bitcast.385), calls=%async_computation | async-start | bytes 917504 | tf_op jit(solution)/shard_map/all_to_all | solution.py:794
  332.3 10.0 copy-start.71
  364.0 7.1 copy-start.147
  432.3 12.0 %copy-start.69 = (bf16[4,256,128]{2,1,0:T(8,128)(2,1)S(1)}, bf16[4,256,128]{2,1,0:T(8,128)(2,1)}, u32[]{:S(2)}) copy-start(bf16[4,256,128]{2,1,0:T(8,128)(2,1)} %copy-done.68) | copy-start | bytes 786436
  434.7 54.7 %copy-start.63 = (f32[1024,16]{1,0:T(8,128)S(1)}, f32[1024,16]{1,0:T(8,128)}, u32[]{:S(2)}) copy-start(f32[1024,16]{1,0:T(8,128)} %convolution_bitcast_fusion.5) | copy-start | bytes 196612
  438.7 57.6 %all-to-all-start.1 = ((bf16[8,32,768]{2,1,0:T(8,128)(2,1)}), bf16[8,32,768]{2,1,0:T(8,128)(2,1)S(1)}, u32[]{:S(2)}, u32[]{:S(2)}) async-start(bf16[8,32,768]{2,1,0:T(8,128)(2,1)} %bitcast.386), calls=%async_computation.1 | async-start | bytes 786432 | tf_op jit(solution)/shard_map/all_to_all | solution.py:794
  489.7 6.6 copy-start.139
  496.3 11.8 %slice-start.14 = ((s8[4718592]{0:T(1024)(128)(4,1)}), s8[4194304]{0:T(1024)(128)(4,1)S(1)}, s32[]{:S(2)}) async-start(s8[4718592]{0:T(1024)(128)(4,1)} %bitcast.397), calls=%async_computation.16 | async-start | bytes 8388608
  500.6 10.0 copy-start.36
  500.6 7.5 slice-start.15
  514.5 8.6 slice-start
  518.6 7.9 copy-start.59
  527.1 7.4 slice-start.10
  529.1 5.4 slice-start.11
  531.6 8.6 slice-start.6
  534.5 8.3 copy-start.34
  534.6 5.7 copy-start.21
  534.6 5.7 copy-start.76
  534.6 5.7 copy-start.94
  534.6 5.7 copy-start.101
  534.6 5.7 slice-start.7
  546.4 5.5 copy-start.82
  551.9 9.5 slice-start.2
  573.9 5.4 copy-start.24
  573.9 5.3 copy-start.65
  574.0 5.3 copy-start.84
  579.3 5.4 copy-start.35
  579.3 5.4 copy-start.52
  584.7 5.2 copy-start.54
  688.8 325.9 %copy-start.31 = (f32[705408]{0:T(1024)S(1)}, f32[705408]{0:T(1024)}, u32[]{:S(2)}) copy-start(f32[705408]{0:T(1024)} %param.17) | copy-start | bytes 8464900
  (106 other events, 246.8 us)
where the time goes:
time: 1040 us; the launch traced here: 1020 us
  Pallas kernels  637 us (61%)
  matrix products  227 us (22%)
  other arithmetic  55 us (5%)
  local copies, waits for them, and re-layouts  41.1 us (4%)
  blocking collectives  41.1 us (4%)
  starting transfers between devices  15.5 us (1%)
    pallas_call x1, Pallas kernels, collect(): pl.pallas_call(functools.partial(collect_kernel, size), out_shape=(jax.Sh...  326 us
    pallas_call x1, Pallas kernels, spread(): pl.pallas_call(spread_kernel, out_shape=jax.ShapeDtypeStruct((32,) + own....  162 us
    pallas_call x1, Pallas kernels, fold(): pl.pallas_call(functools.partial(fold_kernel, items, plain), out_shape=ja...  86.4 us
    dot_general x17, matrix products, weight_grad(): lax.dot_general(flat_in, flat_grad, (((0,), (0,)), ((), ())), preferred_e...  76.9 us
    dot_general x18, matrix products, dense(): lax.dot_general(inputs, weight, (((inputs.ndim - 1,), (0,)), ((), ())), p...  62.5 us
    pallas_call x1, Pallas kernels, unfold(): pl.pallas_call(functools.partial(unfold_kernel, rows, padded, items), out...  62.5 us
    dot_general x14, matrix products, back_input(): lax.dot_general(grads_low, weight, (((grads_low.ndim - 1,), (1,)), ((), (...  59.4 us
    psum x1, blocking collectives, body(): loss = lax.psum(loss_part, BOTH) / divisor  41.1 us
  transfers between devices with their start and end apart: 2, of which 0 were waited for; matrix products, arithmetic and copies ran while one was open for 2% of the time, Pallas kernels for 0%

commit v1 on v0

--- a/solution.py
+++ b/solution.py
@@ -88,6 +88,37 @@
     return best
 
 
+class Slots:
+    def __init__(self, number):
+        self.number, self.base, self.last = number, 0, {}
+
+    def at(self, b):
+        return (self.base + b) % self.number
+
+    def claim(self, b, put):
+        for k in range(self.number):
+            before = self.last.get((self.base + k) % self.number)
+            if before is not None:
+
+                @pl.when(b == k)
+                def _(before=before):
+                    before().wait()
+
+        @pl.when(b >= self.number)
+        def _():
+            put(b - self.number).wait()
+
+    def close(self, blocks, put):
+        base = self.base
+        for b in range(max(0, blocks - self.number), blocks):
+            self.last[(base + b) % self.number] = functools.partial(put, b)
+        self.base = base + blocks
+
+    def drain(self):
+        for before in self.last.values():
+            before().wait()
+
+
 SLOTS = 4
 
 
@@ -95,58 +126,78 @@
     count = len(items)
     outs = refs[:count]
     first, second, wide, first_sem, second_sem, out_sem = refs[count : count + 6]
-    stages = dict(zip(sorted({(h, e.across) for e, h in items}), refs[count + 6 :]))
-    place = 0
+    kinds = sorted({(h, e.across) for e, h in items})
+    stages = dict(zip(kinds, refs[count + 6 :]))
+    turns = {kind: Slots(2) for kind in kinds}
+    bases = [0]
+    for entry, height in items:
+        bases.append(bases[-1] + entry.shape[0] // height)
+
+    def spot(t, b):
+        entry, height = items[t]
+        span = height * entry.across
+        start = entry.start + b * span
+        dev = start // rows
+        row = start - dev * rows
+        low = jnp.minimum(row // 8 * 8, padded - span - 8)
+        return dev, row, low, row + span > rows
+
+    def copies(t, b):
+        entry, height = items[t]
+        window = height * entry.across + 8
+        dev, row, low, more = spot(t, b)
+        slot = (bases[t] + b) % SLOTS
+        one = pltpu.make_async_copy(
+            g_ref.at[dev, pl.ds(pl.multiple_of(low, 8), window)], first.at[slot, pl.ds(0, window)], first_sem.at[slot]
+        )
+        two = pltpu.make_async_copy(
+            g_ref.at[jnp.minimum(dev + 1, g_ref.shape[0] - 1), pl.ds(0, window)],
+            second.at[slot, pl.ds(0, window)], second_sem.at[slot],
+        )
+        return one, two, more
+
+    def fetch(t, b):
+        one, two, more = copies(t, b)
+        one.start()
+
+        @pl.when(more)
+        def _():
+            two.start()
+
+    def fetch_number(g):
+        if g < bases[-1]:
+            t = next(t for t in range(count) if g < bases[t + 1])
+            fetch(t, g - bases[t])
+
+    ahead = SLOTS - 1
+    for g in range(ahead):
+        fetch_number(g)
     for t, (entry, height) in enumerate(items):
-        span = height * entry.across
-        window = span + 8
+        kind = (height, entry.across)
+        stage, turn = stages[kind], turns[kind]
+        window = height * entry.across + 8
         blocks = entry.shape[0] // height
-        stage = stages[(height, entry.across)]
-
-        def spot(b, entry=entry, span=span, window=window):
-            start = entry.start + b * span
-            dev = start // rows
-            row = start - dev * rows
-            low = jnp.minimum(row // 8 * 8, padded - window)
-            return dev, row, low, row + span > rows
-
-        def copies(b, spot=spot, window=window):
-            dev, row, low, more = spot(b)
-            slot = b % SLOTS
-            one = pltpu.make_async_copy(
-                g_ref.at[dev, pl.ds(pl.multiple_of(low, 8), window)], first.at[slot, pl.ds(0, window)], first_sem.at[slot]
+
+        def put(b, t=t, stage=stage, height=height, place=turn.base, kind=kind):
+            slot = (place + b) % 2
+            return pltpu.make_async_copy(
+                stage.at[slot], outs[t].at[pl.ds(pl.multiple_of(b * height, 8), height)], out_sem.at[kinds.index(kind), slot]
             )
-            two = pltpu.make_async_copy(
-                g_ref.at[jnp.minimum(dev + 1, g_ref.shape[0] - 1), pl.ds(0, window)],
-                second.at[slot, pl.ds(0, window)], second_sem.at[slot],
-            )
-            return one, two, more
-
-        def fetch(b, copies=copies):
-            one, two, more = copies(b)
-            one.start()
-
-            @pl.when(more)
+
+        def body(b, carry, t=t, entry=entry, height=height, window=window, blocks=blocks, stage=stage, turn=turn, put=put):
+            @pl.when(b + ahead < blocks)
             def _():
-                two.start()
-
-        def put(b, t=t, stage=stage, height=height):
-            return pltpu.make_async_copy(
-                stage.at[b % 2], outs[t].at[pl.ds(pl.multiple_of(b * height, 8), height)], out_sem.at[b % 2]
-            )
-
-        for b in range(min(SLOTS - 1, blocks)):
-            fetch(b)
-
-        def body(b, carry, entry=entry, height=height, span=span, window=window, blocks=blocks, stage=stage,
-                 spot=spot, copies=copies, fetch=fetch, put=put):
-            @pl.when(b + SLOTS - 1 < blocks)
-            def _():
-                fetch(b + SLOTS - 1)
-
-            dev, row, low, _ = spot(b)
-            slot = b % SLOTS
-            one, two, more = copies(b)
+                fetch(t, b + ahead)
+
+            for k in range(max(0, ahead - blocks), ahead):
+
+                @pl.when(b == blocks - ahead + k)
+                def _(k=k):
+                    fetch_number(bases[t + 1] + k)
+
+            dev, row, low, _ = spot(t, b)
+            slot = (bases[t] + b) % SLOTS
+            one, two, more = copies(t, b)
             one.wait()
             wide[pl.ds(0, window), :] = first[slot, pl.ds(0, window), :].astype(WIDE)
 
@@ -155,19 +206,18 @@
                 two.wait()
                 wide[pl.ds(rows - low, window), :] = second[slot, pl.ds(0, window), :].astype(WIDE)
 
-            @pl.when(b >= 2)
-            def _():
-                put(b - 2).wait()
-
+            turn.claim(b, put)
             off = row - low
+            place = turn.at(b)
             for j in range(entry.across):
-                stage[b % 2, :, j * LANES : (j + 1) * LANES] = wide[pl.ds(off + j, height, stride=entry.across), :].astype(NARROW)
+                stage[place, :, j * LANES : (j + 1) * LANES] = wide[pl.ds(off + j, height, stride=entry.across), :].astype(NARROW)
             put(b).start()
             return carry
 
         lax.fori_loop(0, blocks, body, 0)
-        for b in range(max(0, blocks - 2), blocks):
-            put(b).wait()
+        turn.close(blocks, put)
+    for turn in turns.values():
+        turn.drain()
 
 
 def unfold(gathered, rows):
@@ -183,7 +233,7 @@
         out_specs=[ANY] * len(items),
         scratch_shapes=[
             pltpu.VMEM((SLOTS, tall, LANES), NARROW), pltpu.VMEM((SLOTS, tall, LANES), NARROW),
-            pltpu.VMEM((2 * tall, LANES), WIDE), DMA((SLOTS,)), DMA((SLOTS,)), DMA((2,)),
+            pltpu.VMEM((2 * tall, LANES), WIDE), DMA((SLOTS,)), DMA((SLOTS,)), DMA((len(kinds), 2)),
         ]
         + [pltpu.VMEM((2, h, n * LANES), NARROW) for h, n in kinds],
         compiler_params=pltpu.CompilerParams(vmem_limit_bytes=48 * 1000 * 1000),
@@ -217,90 +267,131 @@
 
 
 DEPTH = 3
-
-
-def fold_kernel(items, plain, *refs):
-    count = len(items) + len(plain)
-    ins, full = refs[:count], refs[count]
-    plain_sem, in_sem, out_sem = refs[count + 1 : count + 4]
-    kinds = sorted({(h, e.across) for e, h in items})
-    loads = dict(zip(kinds, refs[count + 4 : count + 4 + len(kinds)]))
-    stage = refs[count + 4 + len(kinds)]
+TALL = 256
+CHUNK = 512
+
+
+def product_height(entry):
+    return min(TALL, entry.shape[0])
+
+
+def fold_kernel(products, items, plain, label, row, *refs):
+    refs = list(refs)
+
+    def take(number):
+        found, refs[:number] = refs[:number], []
+        return found
+
+    pairs = take(2 * len(products))
+    given = take(len(items))
+    rest = take(len(plain))
+    (full,) = take(1)
+    pair_sem, given_sem, plain_sem, out_sem = take(4)
+    held = take(2 * len(products))
+    loads = take(len(items))
+    (stage,) = take(1)
+    gets = [pltpu.make_async_copy(given[i], loads[i], given_sem.at[i]) for i in range(len(items))]
+    fills = [pltpu.make_async_copy(pairs[i], held[i], pair_sem.at[i]) for i in range(len(pairs))]
+    for move in gets + fills:
+        move.start()
     moves = []
     for i, (start, number) in enumerate(plain):
-        move = pltpu.make_async_copy(ins[len(items) + i].at[pl.ds(0, number)], full.at[pl.ds(start, number)], plain_sem.at[i])
+        move = pltpu.make_async_copy(rest[i].at[pl.ds(0, number)], full.at[pl.ds(start, number)], plain_sem.at[i])
         move.start()
         moves.append(move)
-    for t, (entry, height) in enumerate(items):
+    turn = Slots(DEPTH)
+
+    def each(entry, height, make):
         span = height * entry.across
         blocks = entry.shape[0] // height
-        load = loads[(height, entry.across)]
-
-        def get(b, t=t, load=load, height=height):
+
+        def put(b, base=turn.base):
+            slot = (base + b) % DEPTH
             return pltpu.make_async_copy(
-                ins[t].at[pl.ds(pl.multiple_of(b * height, 8), height)], load.at[b % DEPTH], in_sem.at[b % DEPTH]
+                stage.at[slot, pl.ds(0, span)], full.at[pl.ds(entry.start + b * span, span)], out_sem.at[slot]
             )
 
-        def put(b, entry=entry, span=span):
-            return pltpu.make_async_copy(
-                stage.at[b % DEPTH, pl.ds(0, span)], full.at[pl.ds(entry.start + b * span, span)], out_sem.at[b % DEPTH]
-            )
-
-        for b in range(min(DEPTH - 1, blocks)):
-            get(b).start()
-
-        def body(b, carry, entry=entry, height=height, blocks=blocks, load=load, get=get, put=put):
-            @pl.when(b + DEPTH - 1 < blocks)
-            def _():
-                get(b + DEPTH - 1).start()
-
-            get(b).wait()
-
-            @pl.when(b >= DEPTH)
-            def _():
-                put(b - DEPTH).wait()
-
-            slot = b % DEPTH
-            for j in range(entry.across):
-                stage[slot, pl.ds(j, height, stride=entry.across), :] = load[slot, :, j * LANES : (j + 1) * LANES]
+        def step(b, carry):
+            turn.claim(b, put)
+            make(b, turn.at(b))
             put(b).start()
             return carry
 
-        lax.fori_loop(0, blocks, body, 0)
-        for b in range(max(0, blocks - DEPTH), blocks):
-            put(b).wait()
+        lax.fori_loop(0, blocks, step, 0)
+        turn.close(blocks, put)
+
+    sparse = next(e for e in ENTRIES if e.sparse)
+    height = block_height(sparse, 1200)
+
+    def lone(b, slot):
+        here = lax.broadcasted_iota(jnp.int32, (height, LANES), 0) + b * height == label[0]
+        for j in range(sparse.across):
+            value = jnp.broadcast_to(row[0:1, j * LANES : (j + 1) * LANES], (height, LANES))
+            stage[slot, pl.ds(j, height, stride=sparse.across), :] = jnp.where(here, value, 0.0)
+
+    each(sparse, height, lone)
+    for t, entry in enumerate(items):
+        gets[t].wait()
+
+        def make(b, slot, t=t, entry=entry):
+            for j in range(entry.across):
+                stage[slot, pl.ds(j, entry.shape[0], stride=entry.across), :] = loads[t][:, j * LANES : (j + 1) * LANES]
+
+        each(entry, entry.shape[0], make)
+    for t, entry in enumerate(products):
+        left, right = held[2 * t], held[2 * t + 1]
+        fills[2 * t].wait()
+        fills[2 * t + 1].wait()
+        height = product_height(entry)
+        chunk = math.gcd(CHUNK, entry.shape[1])
+
+        def make(b, slot, left=left, right=right, entry=entry, height=height, chunk=chunk):
+            turned = left[:, pl.ds(pl.multiple_of(b * height, LANES), height)].T
+            for k in range(entry.shape[1] // chunk):
+                found = jnp.dot(turned, right[:, k * chunk : (k + 1) * chunk], preferred_element_type=WIDE)
+                for j in range(chunk // LANES):
+                    at = pl.ds(k * (chunk // LANES) + j, height, stride=entry.across)
+                    stage[slot, at, :] = found[:, j * LANES : (j + 1) * LANES]
+
+        each(entry, height, make)
+    turn.drain()
     for move in moves:
         move.wait()
 
 
-def fold(grads, height_total):
-    items = [(e, block_height(e, 2304)) for e in ENTRIES if e.matrix]
-    matrices = [grads[(e.group, e.name)] for e, _ in items]
+def fold(grads, label, height_total):
+    found = {e: grads[(e.group, e.name)] for e in ENTRIES}
+    products = [e for e in ENTRIES if isinstance(found[e], tuple)]
+    items = [e for e in ENTRIES if e.matrix and not e.sparse and e not in products]
     plain, values = [], []
     for e in ENTRIES:
         if e.matrix:
             continue
-        value = grads[(e.group, e.name)].reshape(-1)
+        value = found[e].reshape(-1)
         value = jnp.pad(value, (0, e.rows * LANES - value.shape[0]))
         plain.append((e.start, e.rows))
         values.append(value.reshape(e.rows, LANES))
     if height_total > USED:
         plain.append((USED, height_total - USED))
         values.append(jnp.zeros((height_total - USED, LANES), WIDE))
-    kinds = sorted({(h, e.across) for e, h in items})
-    tall = max(e.across * h for e, h in items)
+    row = next(found[e] for e in ENTRIES if e.sparse)
+    operands = [x.reshape(-1, x.shape[-1]) for e in products for x in found[e]]
+    tall = max([e.rows for e in items] + [e.across * product_height(e) for e in products])
     total = height_total * LANES
+    flops = sum(2 * math.prod(e.shape) * operands[2 * i].shape[0] for i, e in enumerate(products))
     return pl.pallas_call(
-        functools.partial(fold_kernel, items, plain),
+        functools.partial(fold_kernel, products, items, plain),
         out_shape=jax.ShapeDtypeStruct((height_total, LANES), WIDE),
-        in_specs=[ANY] * (len(items) + len(plain)),
+        in_specs=[pl.BlockSpec(memory_space=pltpu.SMEM), pl.BlockSpec(memory_space=pltpu.VMEM)]
+        + [ANY] * (len(operands) + len(items) + len(plain)),
         out_specs=ANY,
-        scratch_shapes=[DMA((len(plain),)), DMA((DEPTH,)), DMA((DEPTH,))]
-        + [pltpu.VMEM((DEPTH, h, n * LANES), WIDE) for h, n in kinds]
+        scratch_shapes=[DMA((len(operands),)), DMA((len(items),)), DMA((len(plain),)), DMA((DEPTH,))]
+        + [pltpu.VMEM(x.shape, x.dtype) for x in operands]
+        + [pltpu.VMEM(e.shape, WIDE) for e in items]
         + [pltpu.VMEM((DEPTH, tall, LANES), WIDE)],
-        compiler_params=pltpu.CompilerParams(vmem_limit_bytes=48 * 1000 * 1000),
-        cost_estimate=pl.CostEstimate(flops=total, bytes_accessed=8 * total, transcendentals=0),
-    )(*matrices, *values)
+        compiler_params=pltpu.CompilerParams(vmem_limit_bytes=62 * 1000 * 1000),
+        cost_estimate=pl.CostEstimate(flops=flops, bytes_accessed=4 * total, transcendentals=0),
+    )(label, jnp.broadcast_to(row, (8, row.shape[-1])), *operands, *[found[e] for e in items], *values)
 
 
 X, Y, Z = 0, 1, 2
@@ -532,7 +623,7 @@
     lax.fori_loop(0, into.shape[0] // STEP, body, 0)
 
 
-def collect_at(low, size, full, out, aside, store, ring, side, ring_sem, side_sem, send_sem, link_sem, core_send, core_sem, out_sem):
+def collect_at(low, size, full, mark, out, aside, store, ring, side, ring_sem, side_sem, send_sem, link_sem, core_send, core_sem, out_sem, marks, mark_sem):
     chip = Chip(low)
     me = (low, 0, 0)
     tasks, spots = sum_programs()[low], landing()
@@ -558,6 +649,13 @@
             ring.at[i % RING], store.at[spot], send_sem.at[i], link_sem.at[spot], device_id=chip.device(to), device_id_type=MESH
         )
 
+    tail = pl.ds(unit - 8, 8)
+    ours_too = pltpu.make_async_copy(mark, marks.at[0], mark_sem.at[0])
+    theirs_too = pltpu.make_async_remote_copy(
+        mark, marks.at[1], mark_sem.at[1], mark_sem.at[2], device_id=chip.device(me, 1), device_id_type=MESH
+    )
+    ours_too.start()
+    theirs_too.start()
     leaving = {}
 
     def fetch(i):
@@ -571,6 +669,8 @@
         across(i).start()
     for i in range(SIDE - 1):
         fetch(i)
+    ours_too.wait()
+    theirs_too.wait()
     for i, (u, q, kids, to) in enumerate(tasks):
         if i + EARLY < count:
             across(i + EARLY).start()
@@ -578,6 +678,9 @@
             fetch(i + SIDE - 1)
         ours(i).wait()
         theirs(i).wait()
+        if u == SHARES - 1:
+            ring[i % RING, tail, :] = marks[0] + marks[1]
+            side[i % SIDE, tail, :] = jnp.zeros((8, LANES), WIDE)
         terms = [side.at[i % SIDE]]
         for kid in kids:
             spot = spots[low][(u, q, kid)]
@@ -611,20 +714,21 @@
         collect_at(1, size, *refs)
 
 
-def collect(full, size, rows):
+def collect(full, mark, size, rows):
     slots = max(len(spots) for spots in landing())
     count, unit = len(sum_programs()[0]), rows // SHARES
     return pl.pallas_call(
         functools.partial(collect_kernel, size),
         out_shape=(jax.ShapeDtypeStruct((rows, LANES), WIDE), jax.ShapeDtypeStruct((count, unit, LANES), WIDE)),
-        in_specs=[ANY],
+        in_specs=[ANY, ANY],
         out_specs=(ANY, ANY),
         scratch_shapes=[
             pltpu.VMEM((slots, unit, LANES), WIDE), pltpu.VMEM((RING, unit, LANES), WIDE), pltpu.VMEM((SIDE, unit, LANES), WIDE),
             DMA((RING,)), DMA((SIDE,)), DMA((count,)), DMA((slots,)), DMA((count,)), DMA((count,)), DMA((SHARES,)),
+            pltpu.VMEM((2, 8, LANES), WIDE), DMA((3,)),
         ],
         compiler_params=pltpu.CompilerParams(collective_id=1, has_side_effects=True, vmem_limit_bytes=62 * 1000 * 1000),
-    )(full)[0]
+    )(full, mark)[0]
 
 
 def layer_norm(value, gain, shift):
@@ -644,6 +748,8 @@
 def weight_grad(inputs, grads_low):
     flat_in = inputs.reshape(-1, inputs.shape[-1])
     flat_grad = grads_low.reshape(-1, grads_low.shape[-1])
+    if min(flat_in.shape[1], flat_grad.shape[1]) >= LANES:
+        return flat_in, flat_grad
     return lax.dot_general(flat_in, flat_grad, (((0,), (0,)), ((), ())), preferred_element_type=WIDE)
 
 
@@ -835,7 +941,6 @@
     )
     returned = exchange(cond_back.astype(NARROW), ranks_dp)
     token_grad = lax.dot_general(picks, returned, (((0,), (0,)), ((), ())), preferred_element_type=WIDE)
-    loss = lax.psum(loss_part, BOTH) / divisor
     after_grad = jnp.concatenate([jnp.zeros((BUF, D), WIDE), token_grad], 0)
     flow_grad, dec_gain, dec_shift = norm_pull(flow_out, head.dec_gain, head.dec_shift)(after_grad)
     head_grads.update(diffusion_pos=token_grad, dec_gain=dec_gain, dec_shift=dec_shift)
@@ -852,17 +957,22 @@
     token_in = stream_grad[BUF:]
     base_grads = dict(
         encoder_pos=stream_grad,
-        class_table=jnp.zeros((CLASSES, D), WIDE).at[labels].add(jnp.sum(stream_grad[:BUF], 0)[None]),
+        class_table=jnp.sum(stream_grad[:BUF], 0, keepdims=True),
         embed_weight=weight_grad(latents, token_in.astype(NARROW)), embed_bias=rows_sum(token_in),
     )
     grads = {}
     for group, found in enumerate((base_grads, enc_grads, mid_grads, dec_grads, head_grads)):
         grads.update({(group, name): value for name, value in found.items()})
     height = -(-((ranks - 1) * size + padded) // 8) * 8
-    full = fold(grads, height)
+    full = fold(grads, labels, height)
     if meshed:
-        owned = collect(full, size, padded)[:size]
+        lane = lax.broadcasted_iota(jnp.int32, (8, LANES), 1)
+        mark = jnp.where(lane == lax.axis_index("dp") * ranks_rep + lax.axis_index("rep"), loss_part, 0.0)
+        owned = collect(full, mark, size, padded)
+        loss = jnp.sum(owned[padded - 8, :ranks]) / divisor
+        owned = owned[:size]
     else:
+        loss = lax.psum(loss_part, BOTH) / divisor
         owned = lax.psum_scatter(full[: ranks * size].reshape(ranks, size, LANES), BOTH, scatter_dimension=0, tiled=False)
     owned = owned.reshape(-1)
     rate = 0.05 * math.sqrt(images * ranks * SEQ)

time: 1040 us -> 919 us (0.88)
  matrix products: 227 us -> 156 us
  Pallas kernels: 637 us -> 594 us
  blocking collectives: 41.1 us -> 0 us
  other arithmetic: 55 us -> 80.8 us
  local copies, waits for them, and re-layouts: 41.1 us -> 52 us
    dot_general x17 -> x3, matrix products: 76.9 us -> 3.45 us  [weight_grad(): lax.dot_general(flat_in, flat_grad, (((0,), (0,)), ((), ())), preferred_e...]
    psum x1 -> x0, blocking collectives: 41.1 us -> none  [body(): loss = lax.psum(loss_part, BOTH) / divisor]
    pallas_call x1, Pallas kernels: 86.4 us -> 62.1 us  [fold(): pl.pallas_call(functools.partial(fold_kernel, products, items, plain), ou...]
    pallas_call x1, Pallas kernels: 62.5 us -> 41.6 us  [unfold(): pl.pallas_call(functools.partial(unfold_kernel, rows, padded, items), out...]
    unnamed x338 -> x370, local copies, waits for them, and re-layouts: 21.2 us -> 16.7 us
  transfers between devices with their start and end apart: 2 -> 2, of which waited for: 0 -> 1; matrix products, arithmetic and copies ran while one was open for 2% -> 2% of each run, Pallas kernels for 0% -> 0%
where the time goes in v1:
time: 919 us; the launch traced here: 909 us
  Pallas kernels  594 us (65%)
  matrix products  156 us (17%)
  other arithmetic  80.8 us (9%)
  local copies, waits for them, and re-layouts  52 us (6%)
  starting transfers between devices  16.3 us (2%)
    pallas_call x1, Pallas kernels, collect(): pl.pallas_call(functools.partial(collect_kernel, size), out_shape=(jax.Sh...  328 us
    pallas_call x1, Pallas kernels, spread(): pl.pallas_call(spread_kernel, out_shape=jax.ShapeDtypeStruct((32,) + own....  162 us
    dot_general x14, matrix products, back_input(): lax.dot_general(grads_low, weight, (((grads_low.ndim - 1,), (1,)), ((), (...  66.3 us
    pallas_call x1, Pallas kernels, fold(): pl.pallas_call(functools.partial(fold_kernel, products, items, plain), ou...  62.1 us
    dot_general x18, matrix products, dense(): lax.dot_general(inputs, weight, (((inputs.ndim - 1,), (0,)), ((), ())), p...  58.3 us
    pallas_call x1, Pallas kernels, unfold(): pl.pallas_call(functools.partial(unfold_kernel, rows, padded, items), out...  41.6 us
  transfers between devices with their start and end apart: 2, of which 1 were waited for; matrix products, arithmetic and copies ran while one was open for 2% of the time, Pallas kernels for 0%

profile of v1, /device:TPU:21, one launch (start us, length us, event | category | flops | bytes accessed | tf_op | source)
XLA Modules:
  0.0 908.6 jit_solution(524474434599713806)
XLA Ops:
  3.2 1.9 convert_bitcast_fusion
  5.1 1.8 concatenate.69.own
  6.9 161.8 %shard_map.120.g_ref = bf16[32,5520,128]{2,1,0:T(8,128)(2,1)} custom-call(bf16[5520,128]{1,0:T(8,128)(2,1)} %concatenate.69.own), custom_call_target="tpu_custom_call" | custom-call | tf_op jit(solution)/shard_map/pallas_call | solution.py:542
  171.5 1.5 bitcast_convert_fusion.11
  173.0 41.6 %shard_map.121 = (bf16[16,768]{1,0:T(8,128)(2,1)S(1)}, bf16[320,768]{1,0:T(8,128)(2,1)S(1)}, bf16[768,2304]{1,0:T(8,128)(2,1)}, bf16[768,768]{1,0:T(8,128)(2,1)S...) custom-call(bf16[32,5520,128]{2,1,0:T(8,128)(2,1)} %shard_map.120.g_ref), custom_call_target="tpu_custom_call" | custom-call | flops 21753856 | bytes 87015424 | tf_op jit(solution)/shard_map/pallas_call | solution.py:229
  225.5 1.4 fusion.102
  229.4 2.1 copy.108
  231.5 2.1 copy.110
  233.6 2.1 copy.109
  236.4 2.8 fusion.9
  240.8 1.5 convolution_convert_fusion.1
  242.4 1.7 copy-done.7
  246.0 12.0 %multiply_convert_fusion.6 = (bf16[320,3072]{1,0:T(8,128)(2,1)S(1)}, f32[320,3072]{1,0:T(8,128)}, f32[320,3072]{1,0:T(8,128)}) fusion(f32[3072]{0:T(1024)S(1)} %copy-done.149, bf16[320,768]{1,0:T(8,128)(2,1)S(1)} %add_convert_fusion.3.refs_4_, bf16[768,3072]{1,0:T(8,128)(2,1)S(1)} %bitcast.397), kind=kOutput, calls=%fused_computation.73 | convolution fusion | flops 1574830080 | bytes 15052800 | tf_op jit(solution)/shard_map/dot_general | solution.py:741
  258.1 1.8 fusion.161
  267.7 2.3 copy.113
  270.0 2.2 multiply_reduce_fusion.2
  277.5 11.7 %multiply_convert_fusion.5 = (bf16[320,3072]{1,0:T(8,128)(2,1)S(1)}, f32[320,3072]{1,0:T(8,128)}, f32[320,3072]{1,0:T(8,128)}) fusion(f32[3072]{0:T(1024)S(1)} %copy-done.148, bf16[320,768]{1,0:T(8,128)(2,1)S(1)} %add_convert_fusion.refs_14_, bf16[768,3072]{1,0:T(8,128)(2,1)S(1)} %bitcast.403), kind=kOutput, calls=%fused_computation.60 | convolution fusion | flops 1574830080 | bytes 15052800 | tf_op jit(solution)/shard_map/dot_general | solution.py:741
  289.3 1.8 fusion.164
  293.0 10.8 %all-to-all-start = ((bf16[8,32,896]{2,1,0:T(8,128)(2,1)}), bf16[8,32,896]{2,1,0:T(8,128)(2,1)}, u32[]{:S(2)}, u32[]{:S(2)}) async-start(bf16[8,32,896]{2,1,0:T(8,128)(2,1)} %bitcast.363), calls=%async_computation | async-start | bytes 917504 | tf_op jit(solution)/shard_map/all_to_all | solution.py:900
  303.8 1.6 convert_reduce_fusion.1
  306.8 2.1 copy.135.refs_2_
  310.1 2.2 fusion.75
  314.8 2.9 fusion.73
  319.6 1.8 slice.243.refs_20_
  323.0 3.4 convolution_add_fusion.4
  326.4 3.2 multiply_convert_fusion.4
  329.7 6.7 broadcast_add_fusion
  336.4 1.6 fusion.14
  338.1 1.5 copy-done.61
  339.6 4.7 multiply_convert_fusion.3
  344.3 4.8 fusion.150
  352.0 3.0 multiply_reduce_fusion.5
  356.5 4.1 fusion.149
  360.7 3.1 fusion.58
  364.7 4.1 fusion.153
  368.8 10.0 %multiply_reduce_fusion.3 = (f32[1024]{0:T(1024)}, f32[4,256]{1,0:T(4,128)S(1)}, f32[1024]{0:T(1024)}, f32[4,256,1024]{2,1,0:T(8,128)}, bf16[4,256,1024]{2,1,0:T...) fusion(f32[4,256]{1,0:T(4,128)S(1)} %fusion.103, ...), kind=kOutput, calls=%fused_computation.36 | convolution fusion | flops 2164257792 | bytes 29392896 | tf_op jit(solution)/shard_map/dot_general | solution.py:745
  378.9 4.7 fusion.138
  383.6 1.4 fusion.65.refs_32_
  385.8 4.9 fusion.57
  390.8 2.0 fusion
  392.8 15.2 %fusion.132 = (f32[1024]{0:T(1024)}, bf16[256,1024]{1,0:T(8,128)(2,1)S(1)}, bf16[4,256,1024]{2,1,0:T(8,128)(2,1)}) fusion(f32[256,1024]{1,0:T(8,128)} %copy-done.88, f32[4,256,1024]{2,1,0:T(8,128)} %get-tuple-element.198, f32[1024]{0:T(1024)S(1)} %get-tuple-element.117, bf16[1024,3072]{1,0:T(8,128)(2,1)} %get-tuple-element.40, ...), kind=kOutput, calls=%fused_computation.357 | convolution fusion | flops 6475742208 | bytes 26746880 | tf_op jit(solution)/shard_map/dot_general | solution.py:745
  408.0 1.4 convolution_convert_fusion.5
  409.4 5.5 all-to-all-start.1
  416.0 6.5 pad_maximum_fusion.1.refs_23_
  422.5 2.2 all-to-all-done.1
  427.2 8.2 fusion.134
  435.5 2.5 multiply_reduce_fusion.8
  442.0 4.0 fusion.157
  446.1 4.3 multiply_reduce_fusion.1
  450.5 1.4 multiply_convert_fusion.1
  454.6 4.3 multiply_reduce_fusion.9
  463.4 7.1 fusion.136
  470.6 2.5 multiply_reduce_fusion.11
  478.0 5.2 fusion.159
  483.2 2.2 multiply_reduce_fusion
  485.4 2.0 multiply_convert_fusion
  488.5 1.5 fusion.158
  490.0 2.1 copy.133
  492.1 2.1 copy.131
  495.3 4.7 multiply_reduce_fusion.12
  500.1 1.8 pad_maximum_fusion.2
  506.3 62.1 %shard_map.122.refs_0_ = f32[176368,128]{1,0:T(8,128)} custom-call(s32[1]{0:T(128)S(6)} %copy.152.label, f32[8,768]{1,0:T(8,128)} %broadcast_in_dim.111.row, bf16[320,768]{1,0:T(8,128)(2,1)} %copy-done.73, bf16[320,2304]{1,0:T(8,128)(2,1)} %get-tuple-element.224.refs_1_, bf16[320,768]{1,0:T(8,128)(2,1)} %copy.135.refs_2_, bf16[320,768]{1,0:T(8,128)(2,1)} %copy-done.72, ...), custom_call_target="tpu_custom_call" | custom-call | flops 21114126336 | bytes 90300416 | tf_op jit(solution)/shard_map/pallas_call | solution.py:382
  569.0 328.5 %shard_map.123 = (f32[5520,128]{1,0:T(8,128)}, f32[96,920,128]{2,1,0:T(8,128)}) custom-call(f32[176368,128]{1,0:T(8,128)} %shard_map.122.refs_0_, f32[8,128]{1,0:T(8,128)} %iota.25.refs_1_), custom_call_target="tpu_custom_call" | custom-call | tf_op jit(solution)/shard_map/pallas_call | solution.py:720
  899.4 7.6 multiply_add_fusion.4
  (518 shorter events, 77.6 us)
Async XLA Ops:
  173.0 72.4 %copy-start.99 = (f32[768]{0:T(1024)}, f32[768]{0:T(1024)S(1)}, u32[]{:S(2)}) copy-start(f32[768]{0:T(1024)S(1)} %get-tuple-element.135) | copy-start | bytes 9220
  173.0 87.3 %copy-start.101 = (f32[768]{0:T(1024)}, f32[768]{0:T(1024)S(1)}, u32[]{:S(2)}) copy-start(f32[768]{0:T(1024)S(1)} %get-tuple-element.132) | copy-start | bytes 9220
  173.0 88.6 %copy-start.103 = (f32[768]{0:T(1024)}, f32[768]{0:T(1024)S(1)}, u32[]{:S(2)}) copy-start(f32[768]{0:T(1024)S(1)} %get-tuple-element.128) | copy-start | bytes 9220
  173.0 48.6 %copy-start.97 = (bf16[256,16]{0,1:T(8,128)(2,1)S(1)}, bf16[256,16]{0,1:T(8,128)(2,1)}, u32[]{:S(2)}) copy-start(bf16[256,16]{0,1:T(8,128)(2,1)} %param.9) | copy-start | bytes 24580
  219.0 23.3 %copy-start = (bf16[320,768]{1,0:T(8,128)(2,1)}, bf16[320,768]{1,0:T(8,128)(2,1)S(1)}, u32[]{:S(2)}) copy-start(bf16[320,768]{1,0:T(8,128)(2,1)S(1)} %get-tuple-element.25) | copy-start | bytes 1474564
  219.0 55.7 %copy-start.2 = (bf16[768,768]{1,0:T(8,128)(2,1)}, bf16[768,768]{1,0:T(8,128)(2,1)S(1)}, u32[]{:S(2)}) copy-start(bf16[768,768]{1,0:T(8,128)(2,1)S(1)} %get-tuple-element.33) | copy-start | bytes 3538948
  223.5 18.9 %copy-start.56 = (f32[64,768]{1,0:T(8,128)}, f32[64,768]{1,0:T(8,128)S(1)}, u32[]{:S(2)}) copy-start(f32[64,768]{1,0:T(8,128)S(1)} %broadcast_in_dim.88) | copy-start | bytes 589828
  236.4 24.2 %copy-start.118 = (pred[320]{0:T(512)(128)(4,1)}, pred[320]{0:T(512)(128)(4,1)S(1)}, u32[]{:S(2)}) copy-start(pred[320]{0:T(512)(128)(4,1)S(1)} %concatenate.73) | copy-start | bytes 964
  239.3 6.7 slice-start.6
  240.8 5.2 slice-start.7
  245.0 13.0 %copy-start.38 = (f32[320,768]{1,0:T(8,128)}, f32[320,768]{1,0:T(8,128)S(1)}, u32[]{:S(2)}) copy-start(f32[320,768]{1,0:T(8,128)S(1)} %get-tuple-element.184) | copy-start | bytes 2949124
  245.4 12.7 %slice-start.10 = ((s8[4718592]{0:T(1024)(128)(4,1)}), s8[4194304]{0:T(1024)(128)(4,1)S(1)}, s32[]{:S(2)}) async-start(s8[4718592]{0:T(1024)(128)(4,1)} %bitcast.400), calls=%async_computation.12 | async-start | bytes 8388608
  245.6 12.4 %copy-start.65 = (bf16[320,768]{1,0:T(8,128)(2,1)}, bf16[320,768]{1,0:T(8,128)(2,1)S(1)}, u32[]{:S(2)}) copy-start(bf16[320,768]{1,0:T(8,128)(2,1)S(1)} %add_convert_fusion.3.refs_4_) | copy-start | bytes 1474564
  246.0 12.0 %copy-start.154 = (f32[768]{0:T(1024)S(1)}, f32[768]{0:T(1024)}, u32[]{:S(2)}) copy-start(f32[768]{0:T(1024)} %get-tuple-element.133) | copy-start | bytes 9220
  246.0 12.0 %slice-start.11 = ((s8[4718592]{0:T(1024)(128)(4,1)}), s8[524288]{0:T(1024)(128)(4,1)S(1)}, s32[]{:S(2)}) async-start(s8[4718592]{0:T(1024)(128)(4,1)} %bitcast.400), calls=%async_computation.13 | async-start | bytes 1048576
  267.7 5.7 copy-start.48
  275.3 14.0 %slice-start.16 = ((s8[4718592]{0:T(1024)(128)(4,1)}), s8[4194304]{0:T(1024)(128)(4,1)S(1)}, s32[]{:S(2)}) async-start(s8[4718592]{0:T(1024)(128)(4,1)} %bitcast.406), calls=%async_computation.18 | async-start | bytes 8388608
  276.0 13.2 %copy-start.32 = (f32[320,768]{1,0:T(8,128)}, f32[320,768]{1,0:T(8,128)S(1)}, u32[]{:S(2)}) copy-start(f32[320,768]{1,0:T(8,128)S(1)} %get-tuple-element.193) | copy-start | bytes 2949124
  276.0 13.2 %copy-start.114 = (f32[320]{0:T(512)}, f32[320]{0:T(512)S(1)}, u32[]{:S(2)}) copy-start(f32[320]{0:T(512)S(1)} %broadcast_multiply_fusion.3) | copy-start | bytes 3844
  276.3 12.9 %copy-start.128 = (f32[320]{0:T(512)}, f32[320]{0:T(512)S(1)}, u32[]{:S(2)}) copy-start(f32[320]{0:T(512)S(1)} %multiply_reduce_fusion.20) | copy-start | bytes 3844
  276.3 12.9 %copy-start.136 = (f32[320]{0:T(512)}, f32[320]{0:T(512)S(1)}, u32[]{:S(2)}) copy-start(f32[320]{0:T(512)S(1)} %fusion.109) | copy-start | bytes 3844
  276.7 12.5 %copy-start.68 = (bf16[320,768]{1,0:T(8,128)(2,1)}, bf16[320,768]{1,0:T(8,128)(2,1)S(1)}, u32[]{:S(2)}) copy-start(bf16[320,768]{1,0:T(8,128)(2,1)S(1)} %add_convert_fusion.refs_14_) | copy-start | bytes 1474564
  277.5 11.8 %copy-start.151 = (f32[768]{0:T(1024)S(1)}, f32[768]{0:T(1024)}, u32[]{:S(2)}) copy-start(f32[768]{0:T(1024)} %get-tuple-element.121) | copy-start | bytes 9220
  277.5 11.8 %slice-start.17 = ((s8[4718592]{0:T(1024)(128)(4,1)}), s8[524288]{0:T(1024)(128)(4,1)S(1)}, s32[]{:S(2)}) async-start(s8[4718592]{0:T(1024)(128)(4,1)} %bitcast.406), calls=%async_computation.19 | async-start | bytes 1048576
  291.2 17.7 %copy-start.55 = (bf16[12,64,320]{2,1,0:T(8,128)(2,1)S(1)}, bf16[12,64,320]{2,1,0:T(8,128)(2,1)}, u32[]{:S(2)}) copy-start(bf16[12,64,320]{2,1,0:T(8,128)(2,1)} %copy-done.54) | copy-start | bytes 1474564
  291.4 18.5 %copy-start.145 = (s32[4,256]{1,0:T(4,128)S(1)}, s32[4,256]{1,0:T(4,128)}, u32[]{:S(2)}) copy-start(s32[4,256]{1,0:T(4,128)} %param.12) | copy-start | bytes 12292
  291.8 29.6 %copy-start.91 = (f32[4,256,16]{1,2,0:T(8,128)S(1)}, f32[4,256,16]{1,2,0:T(8,128)}, u32[]{:S(2)}) copy-start(f32[4,256,16]{1,2,0:T(8,128)} %param.13) | copy-start | bytes 196612
  293.0 24.7 %all-to-all-start = ((bf16[8,32,896]{2,1,0:T(8,128)(2,1)}), bf16[8,32,896]{2,1,0:T(8,128)(2,1)}, u32[]{:S(2)}, u32[]{:S(2)}) async-start(bf16[8,32,896]{2,1,0:T(8,128)(2,1)} %bitcast.363), calls=%async_computation | async-start | bytes 917504 | tf_op jit(solution)/shard_map/all_to_all | solution.py:900
  322.3 22.0 %copy-start.17 = (f32[4,256,1024]{2,1,0:T(8,128)}, f32[4,256,1024]{2,1,0:T(8,128)S(1)}, u32[]{:S(2)}) copy-start(f32[4,256,1024]{2,1,0:T(8,128)S(1)} %get-tuple-element.200) | copy-start | bytes 12582916
  322.3 7.4 slice-start.4
  329.7 6.7 copy-start.60
  336.4 7.8 copy-start.21
  338.1 6.1 copy-start.44
  368.8 10.0 %copy-start.46 = (bf16[4,256,1024]{2,1,0:T(8,128)(2,1)}, bf16[4,256,1024]{2,1,0:T(8,128)(2,1)S(1)}, u32[]{:S(2)}) copy-start(bf16[4,256,1024]{2,1,0:T(8,128)(2,1)S(1)} %get-tuple-element.150) | copy-start | bytes 6291460
  378.9 11.9 %copy-start.25 = (f32[4,256,1024]{2,1,0:T(8,128)}, f32[4,256,1024]{2,1,0:T(8,128)S(1)}, u32[]{:S(2)}) copy-start(f32[4,256,1024]{2,1,0:T(8,128)S(1)} %get-tuple-element.146) | copy-start | bytes 12582916
  408.0 14.5 %copy-start.93 = (bf16[256,1024]{1,0:T(8,128)(2,1)}, bf16[256,1024]{1,0:T(8,128)(2,1)S(1)}, u32[]{:S(2)}) copy-start(bf16[256,1024]{1,0:T(8,128)(2,1)S(1)} %get-tuple-element.50.refs_21_) | copy-start | bytes 1572868
  409.4 15.3 %all-to-all-start.1 = ((bf16[8,32,768]{2,1,0:T(8,128)(2,1)}), bf16[8,32,768]{2,1,0:T(8,128)(2,1)S(1)}, u32[]{:S(2)}, u32[]{:S(2)}) async-start(bf16[8,32,768]{2,1,0:T(8,128)(2,1)} %bitcast.59), calls=%async_computation.1 | async-start | bytes 786432 | tf_op jit(solution)/shard_map/all_to_all | solution.py:900
  416.0 8.7 copy-start.159
  425.0 10.3 %copy-start.35 = (f32[256,768]{1,0:T(8,128)}, f32[256,768]{1,0:T(8,128)S(1)}, u32[]{:S(2)}) copy-start(f32[256,768]{1,0:T(8,128)S(1)} %fusion.92.refs_31_) | copy-start | bytes 2359300
  425.1 10.3 %slice-start.14 = ((s8[4718592]{0:T(1024)(128)(4,1)}), s8[4194304]{0:T(1024)(128)(4,1)S(1)}, s32[]{:S(2)}) async-start(s8[4718592]{0:T(1024)(128)(4,1)} %bitcast.404), calls=%async_computation.16 | async-start | bytes 8388608
  427.2 8.2 copy-start.69
  427.2 8.2 copy-start.33
  427.2 8.2 copy-start.106
  427.2 8.2 copy-start.115
  427.2 8.2 copy-start.137
  427.2 8.2 slice-start.15
  442.0 8.4 slice-start
  460.5 10.0 %slice-start.8 = ((s8[4718592]{0:T(1024)(128)(4,1)}), s8[4194304]{0:T(1024)(128)(4,1)S(1)}, s32[]{:S(2)}) async-start(s8[4718592]{0:T(1024)(128)(4,1)} %bitcast.398), calls=%async_computation.10 | async-start | bytes 8388608
  463.2 7.3 copy-start.71
  463.4 7.1 copy-start.39
  463.4 7.1 copy-start.100
  463.4 7.2 copy-start.109
  463.4 7.2 copy-start.131
  463.4 7.2 slice-start.9
  473.6 9.6 %slice-start.2 = ((s8[5898240]{0:T(1024)(128)(4,1)}), s8[1703936]{0:T(1024)(128)(4,1)S(1)}, s32[]{:S(2)}) async-start(s8[5898240]{0:T(1024)(128)(4,1)} %bitcast.325), calls=%async_computation.4 | async-start | bytes 3407872
  478.0 5.2 slice-start.3
  478.0 5.2 copy-start.59
  488.4 6.8 copy-start.1
  488.4 6.8 copy-start.24
  488.5 6.8 copy-start.57
  488.5 6.8 copy-start.107
  488.5 6.8 copy-start.117
  488.5 6.8 copy-start.139
  569.0 330.4 %copy-start.36 = (f32[705408]{0:T(1024)S(1)}, f32[705408]{0:T(1024)}, u32[]{:S(2)}) copy-start(f32[705408]{0:T(1024)} %param.15) | copy-start | bytes 8464900
  (122 other events, 317.4 us)

commit v2 on v1

--- a/solution.py
+++ b/solution.py
@@ -269,6 +269,7 @@
 DEPTH = 3
 TALL = 256
 CHUNK = 512
+NEXT = 3
 
 
 def product_height(entry):
@@ -292,7 +293,7 @@
     (stage,) = take(1)
     gets = [pltpu.make_async_copy(given[i], loads[i], given_sem.at[i]) for i in range(len(items))]
     fills = [pltpu.make_async_copy(pairs[i], held[i], pair_sem.at[i]) for i in range(len(pairs))]
-    for move in gets + fills:
+    for move in gets + fills[: 2 * NEXT]:
         move.start()
     moves = []
     for i, (start, number) in enumerate(plain):
@@ -340,6 +341,8 @@
         each(entry, entry.shape[0], make)
     for t, entry in enumerate(products):
         left, right = held[2 * t], held[2 * t + 1]
+        for move in fills[2 * (t + NEXT) : 2 * (t + NEXT) + 2]:
+            move.start()
         fills[2 * t].wait()
         fills[2 * t + 1].wait()
         height = product_height(entry)
@@ -761,71 +764,197 @@
     return jax.vjp(layer_norm, value, gain.astype(WIDE), shift.astype(WIDE))[1]
 
 
-def split_heads(mixed):
-    return [mixed[:, part * D : (part + 1) * D].reshape(-1, HEADS, HEAD_DIM) for part in range(3)]
-
-
-def masked_scores(queries, keys, keep):
-    scores = jnp.einsum("qhe,khe->hqk", queries, keys, preferred_element_type=WIDE) * HEAD_DIM ** (-0.5)
-    return scores if keep is None else jnp.where(keep[None, None, :], scores, -1e30)
+HALF_ROOT = math.sqrt(0.5)
+PDF = 1.0 / math.sqrt(2.0 * math.pi)
+SCALE = HEAD_DIM ** (-0.5)
+PART = 512
+
+
+def column_sum(value):
+    return jnp.sum(value, 0, keepdims=True)
+
+
+def whiten(value):
+    centered = value - jnp.mean(value, -1, keepdims=True)
+    r = lax.rsqrt(jnp.mean(centered * centered, -1, keepdims=True) + NORM_EPS)
+    return centered * r, r
+
+
+def whiten_back(grad, hat, r):
+    return r * (grad - jnp.mean(grad, -1, keepdims=True) - hat * jnp.mean(grad * hat, -1, keepdims=True))
+
+
+def side_masks(length):
+    lane = lax.broadcasted_iota(jnp.int32, (length, LANES), 1)
+    return lane < HEAD_DIM, lane >= HEAD_DIM
+
+
+def one_side(value, side):
+    return jnp.where(side, value, jnp.zeros_like(value))
+
+
+def start_all(sources, targets, sem):
+    moves = [pltpu.make_async_copy(s, t, sem.at[i]) for i, (s, t) in enumerate(zip(sources, targets))]
+    for move in moves:
+        move.start()
+    return moves
+
+
+def forward_kernel(masked, stream, keep, wide_b, attn_b, fc_b, *refs):
+    outs = refs[4:13]
+    normed, mixed, totals, attended, middle, second, slope, active, output = outs
+    attn_w, proj_w, one_w, two_w, sem = refs[13:]
+    moves = start_all(refs[:4], (attn_w, proj_w, one_w, two_w), sem)
+    hat, _ = whiten(stream[...])
+    normed[...] = (hat * wide_b[0:1, :] + wide_b[1:2, :]).astype(NARROW)
+    moves[0].wait()
+    for k in range(3 * D // D):
+        at = slice(k * D, (k + 1) * D)
+        mixed[:, at] = (matmul(normed[...], attn_w[:, at]) + attn_b[0:1, at]).astype(NARROW)
+    sides = side_masks(stream.shape[0])
+    for pair in range(HEADS // 2):
+        q, k, v = (mixed[:, part * D + pair * LANES : part * D + (pair + 1) * LANES] for part in range(3))
+        found = None
+        for i, side in enumerate(sides):
+            scores = matmul_turned(one_side(q, side), k) * SCALE
+            if masked:
+                scores = jnp.where(keep[0:1, :] > 0.0, scores, -1e30)
+            top = jnp.max(scores, -1, keepdims=True)
+            powers = jnp.exp(scores - top)
+            total = jnp.sum(powers, -1, keepdims=True)
+            totals[:, 2 * pair + i : 2 * pair + i + 1] = top + jnp.log(total)
+            probs = (powers * (1.0 / total)).astype(NARROW)
+            part = matmul(probs, one_side(v, side))
+            found = part if found is None else found + part
+        attended[:, pair * LANES : (pair + 1) * LANES] = found.astype(NARROW)
+    moves[1].wait()
+    value = stream[...] + matmul(attended[...], proj_w[...]) + wide_b[4:5, :]
+    middle[...] = value
+    hat, _ = whiten(value)
+    second[...] = (hat * wide_b[2:3, :] + wide_b[3:4, :]).astype(NARROW)
+    moves[2].wait()
+    for k in range(MLP // PART):
+        at = slice(k * PART, (k + 1) * PART)
+        value = matmul(second[...], one_w[:, at]) + fc_b[0:1, at]
+        share = 0.5 + 0.5 * lax.erf(value * HALF_ROOT)
+        active[:, at] = (value * share).astype(NARROW)
+        slope[:, at] = share + value * (PDF * jnp.exp(-0.5 * value * value))
+    moves[3].wait()
+    output[...] = middle[...] + matmul(active[...], two_w[...]) + wide_b[5:6, :]
+
+
+def block_vectors(p):
+    rows = (p.norm_one_gain, p.norm_one_shift, p.norm_two_gain, p.norm_two_shift, p.proj_bias, p.fc_two_bias)
+    wide_b = jnp.stack(rows + rows[:2]).astype(WIDE)
+    attn_b = jnp.concatenate([p.attn_bias[:D], jnp.zeros((D,), NARROW), p.attn_bias[D:]]).astype(WIDE)[None]
+    return wide_b, attn_b, p.fc_one_bias.astype(WIDE)[None]
+
+
+VMEM = pl.BlockSpec(memory_space=pltpu.VMEM)
+BLOCK_WEIGHTS = ((D, 3 * D), (D, D), (D, MLP), (MLP, D))
+
+
+def block_cost(length, passes):
+    weights = sum(math.prod(s) for s in BLOCK_WEIGHTS)
+    return pl.CostEstimate(flops=2 * passes * length * weights, bytes_accessed=2 * weights + 36 * length * D, transcendentals=4 * length * MLP)
 
 
 def block_forward(stream, keep, p):
-    normed = layer_norm(stream, p.norm_one_gain.astype(WIDE), p.norm_one_shift.astype(WIDE)).astype(NARROW)
-    bias = jnp.concatenate([p.attn_bias[:D].astype(WIDE), jnp.zeros((D,), WIDE), p.attn_bias[D:].astype(WIDE)])
-    mixed = (dense(normed, p.attn_weight) + bias).astype(NARROW)
-    queries, keys, values = split_heads(mixed)
-    scores = masked_scores(queries, keys, keep)
-    totals = jax.nn.logsumexp(scores, axis=-1)
-    probs = jnp.exp(scores - totals[..., None]).astype(NARROW)
-    attended = jnp.einsum("hqk,khe->qhe", probs, values, preferred_element_type=WIDE)
-    attended = attended.reshape(-1, D).astype(NARROW)
-    middle = stream + dense(attended, p.proj_weight) + p.proj_bias.astype(WIDE)
-    second = layer_norm(middle, p.norm_two_gain.astype(WIDE), p.norm_two_shift.astype(WIDE)).astype(NARROW)
-    inner = dense(second, p.fc_one_weight) + p.fc_one_bias.astype(WIDE)
-    active = jax.nn.gelu(inner, approximate=False).astype(NARROW)
-    output = middle + dense(active, p.fc_two_weight) + p.fc_two_bias.astype(WIDE)
-    return output, (stream, normed, mixed, totals, attended, middle, second, inner, active)
+    length = stream.shape[0]
+    shapes = [(D, NARROW), (3 * D, NARROW), (LANES, WIDE), (D, NARROW), (D, WIDE), (D, NARROW), (MLP, WIDE), (MLP, NARROW), (D, WIDE)]
+    row = jnp.ones((1, length), WIDE) if keep is None else keep.astype(WIDE)[None]
+    vectors = block_vectors(p)
+    found = pl.pallas_call(
+        functools.partial(forward_kernel, keep is not None),
+        out_shape=[jax.ShapeDtypeStruct((length, w), t) for w, t in shapes],
+        in_specs=[VMEM] * 5 + [ANY] * 4,
+        out_specs=[VMEM] * len(shapes),
+        scratch_shapes=[pltpu.VMEM(s, NARROW) for s in BLOCK_WEIGHTS] + [DMA((4,))],
+        compiler_params=pltpu.CompilerParams(vmem_limit_bytes=60 * 1000 * 1000),
+        cost_estimate=block_cost(length, 1),
+    )(stream, row, *vectors, p.attn_weight, p.proj_weight, p.fc_one_weight, p.fc_two_weight)
+    return found[-1], (stream, row, vectors[0]) + tuple(found[:-1])
+
+
+def backward_kernel(masked, grad_out, stream, keep, wide_b, mixed, totals, middle, *refs):
+    slope_in = refs[4]
+    out_low, inner_low, middle_low, mixed_low, stream_grad, sums, one_sum, mixed_sum = refs[5:13]
+    attn_w, proj_w, one_w, two_w, slope, attended_grad, sem = refs[13:]
+    attn_src, proj_src, one_src, two_src = refs[:4]
+    moves = start_all((two_src, slope_in, one_src, proj_src, attn_src), (two_w, slope, one_w, proj_w, attn_w), sem)
+    value = grad_out[...]
+    low = value.astype(NARROW)
+    out_low[...] = low
+    sums[0:1, :] = column_sum(value)
+    moves[0].wait()
+    moves[1].wait()
+    for k in range(MLP // PART):
+        at = slice(k * PART, (k + 1) * PART)
+        part = matmul_turned(low, two_w[at, :]) * slope[:, at]
+        inner_low[:, at] = part.astype(NARROW)
+        one_sum[0:1, at] = column_sum(part)
+    moves[2].wait()
+    part = matmul_turned(inner_low[...], one_w[...])
+    hat, r = whiten(middle[...])
+    sums[1:2, :] = column_sum(part * hat)
+    sums[2:3, :] = column_sum(part)
+    value = value + whiten_back(part * wide_b[2:3, :], hat, r)
+    stream_grad[...] = value
+    sums[3:4, :] = column_sum(value)
+    middle_low[...] = value.astype(NARROW)
+    moves[3].wait()
+    attended_grad[...] = matmul_turned(middle_low[...], proj_w[...]).astype(NARROW)
+    sides = side_masks(stream.shape[0])
+    for pair in range(HEADS // 2):
+        here = [slice(part * D + pair * LANES, part * D + (pair + 1) * LANES) for part in range(3)]
+        q, k, v = (mixed[:, at] for at in here)
+        g = attended_grad[:, here[0]]
+        grads = [None, None, None]
+        for i, side in enumerate(sides):
+            q_side, k_side, g_side = one_side(q, side), one_side(k, side), one_side(g, side)
+            scores = matmul_turned(q_side, k) * SCALE
+            if masked:
+                scores = jnp.where(keep[0:1, :] > 0.0, scores, -1e30)
+            probs = jnp.exp(scores - totals[:, 2 * pair + i : 2 * pair + i + 1])
+            prob_grad = matmul_turned(g_side, v)
+            score_grad = (probs * (prob_grad - jnp.sum(probs * prob_grad, -1, keepdims=True))).astype(NARROW)
+            parts = (
+                matmul(score_grad, k_side) * SCALE, matmul(score_grad.T, q_side) * SCALE, matmul(probs.astype(NARROW).T, g_side)
+            )
+            grads = [part if old is None else old + part for old, part in zip(grads, parts)]
+        for at, part in zip(here, grads):
+            mixed_low[:, at] = part.astype(NARROW)
+            mixed_sum[0:1, at] = column_sum(part)
+    moves[4].wait()
+    part = matmul_turned(mixed_low[...], attn_w[...])
+    hat, r = whiten(stream[...])
+    sums[4:5, :] = column_sum(part * hat)
+    sums[5:6, :] = column_sum(part)
+    stream_grad[...] = stream_grad[...] + whiten_back(part * wide_b[0:1, :], hat, r)
 
 
 def block_backward(grad_out, keep, p, saved):
-    stream, normed, mixed, totals, attended, middle, second, inner, active = saved
-    grads = {}
-    out_low = grad_out.astype(NARROW)
-    fc_two_weight = weight_grad(active, out_low)
-    fc_two_bias = rows_sum(grad_out)
-    gelu_pull = jax.vjp(lambda value: jax.nn.gelu(value, approximate=False), inner)[1]
-    inner_grad = gelu_pull(back_input(out_low, p.fc_two_weight))[0]
-    inner_low = inner_grad.astype(NARROW)
-    fc_one_weight = weight_grad(second, inner_low)
-    fc_one_bias = rows_sum(inner_grad)
-    pull = norm_pull(middle, p.norm_two_gain, p.norm_two_shift)
-    middle_grad, norm_two_gain, norm_two_shift = pull(back_input(inner_low, p.fc_one_weight))
-    middle_grad = middle_grad + grad_out
-    middle_low = middle_grad.astype(NARROW)
-    proj_weight = weight_grad(attended, middle_low)
-    proj_bias = rows_sum(middle_grad)
-    attended_grad = back_input(middle_low, p.proj_weight).astype(NARROW).reshape(-1, HEADS, HEAD_DIM)
-    queries, keys, values = split_heads(mixed)
-    probs = jnp.exp(masked_scores(queries, keys, keep) - totals[..., None])
-    values_grad = jnp.einsum("hqk,qhe->khe", probs.astype(NARROW), attended_grad, preferred_element_type=WIDE)
-    prob_grad = jnp.einsum("qhe,khe->hqk", attended_grad, values, preferred_element_type=WIDE)
-    score_grad = (probs * (prob_grad - jnp.sum(probs * prob_grad, -1, keepdims=True))).astype(NARROW)
-    scale = HEAD_DIM ** (-0.5)
-    query_grad = jnp.einsum("hqk,khe->qhe", score_grad, keys, preferred_element_type=WIDE) * scale
-    key_grad = jnp.einsum("hqk,qhe->khe", score_grad, queries, preferred_element_type=WIDE) * scale
-    parts = [item.reshape(-1, D) for item in (query_grad, key_grad, values_grad)]
-    attn_bias = jnp.concatenate([rows_sum(parts[0]), rows_sum(parts[2])])
-    mixed_low = jnp.concatenate(parts, -1).astype(NARROW)
-    attn_weight = weight_grad(normed, mixed_low)
-    pull = norm_pull(stream, p.norm_one_gain, p.norm_one_shift)
-    stream_grad, norm_one_gain, norm_one_shift = pull(back_input(mixed_low, p.attn_weight))
+    stream, row, wide_b, normed, mixed, totals, attended, middle, second, slope, active = saved
+    length = stream.shape[0]
+    shapes = [((length, D), NARROW), ((length, MLP), NARROW), ((length, D), NARROW), ((length, 3 * D), NARROW), ((length, D), WIDE)]
+    shapes += [((8, D), WIDE), ((1, MLP), WIDE), ((1, 3 * D), WIDE)]
+    out_low, inner_low, middle_low, mixed_low, stream_grad, sums, one_sum, mixed_sum = pl.pallas_call(
+        functools.partial(backward_kernel, keep is not None),
+        out_shape=[jax.ShapeDtypeStruct(s, t) for s, t in shapes],
+        in_specs=[VMEM] * 7 + [ANY] * 5,
+        out_specs=[VMEM] * len(shapes),
+        scratch_shapes=[pltpu.VMEM(s, NARROW) for s in BLOCK_WEIGHTS]
+        + [pltpu.VMEM((length, MLP), WIDE), pltpu.VMEM((length, D), NARROW), DMA((5,))],
+        compiler_params=pltpu.CompilerParams(vmem_limit_bytes=60 * 1000 * 1000),
+        cost_estimate=block_cost(length, 1),
+    )(grad_out, stream, row, wide_b, mixed, totals, middle, p.attn_weight, p.proj_weight, p.fc_one_weight, p.fc_two_weight, slope)
     grads = dict(
-        norm_one_gain=norm_one_gain, norm_one_shift=norm_one_shift, attn_weight=attn_weight, attn_bias=attn_bias,
-        proj_weight=proj_weight, proj_bias=proj_bias, norm_two_gain=norm_two_gain, norm_two_shift=norm_two_shift,
-        fc_one_weight=fc_one_weight, fc_one_bias=fc_one_bias, fc_two_weight=fc_two_weight, fc_two_bias=fc_two_bias,
+        norm_one_gain=sums[4], norm_one_shift=sums[5], attn_weight=weight_grad(normed, mixed_low),
+        attn_bias=jnp.concatenate([mixed_sum[0, :D], mixed_sum[0, 2 * D :]]), proj_weight=weight_grad(attended, middle_low),
+        proj_bias=sums[3], norm_two_gain=sums[1], norm_two_shift=sums[2], fc_one_weight=weight_grad(second, inner_low),
+        fc_one_bias=one_sum[0], fc_two_weight=weight_grad(active, out_low), fc_two_bias=sums[0],
     )
-    return stream_grad + middle_grad, grads
+    return stream_grad, grads
 
 
 def time_features(times):
@@ -840,59 +969,238 @@
     return jnp.cos(((times + 1.0) / STEPS_T + 0.008) / 1.008 * math.pi / 2) ** 2 / start
 
 
+ROWS = 256
+TOGETHER = 1
+SUMS = 9
+
+
+def matmul(left, right):
+    return jnp.dot(left, right, preferred_element_type=WIDE)
+
+
+def matmul_turned(left, right):
+    return lax.dot_general(left, right, (((1,), (1,)), ((), ())), preferred_element_type=WIDE)
+
+
+def eighths(value):
+    found = value[:8]
+    for k in range(8, value.shape[0], 8):
+        found = found + value[k : k + 8]
+    return found
+
+
+def sigmoid(value):
+    return 0.5 + 0.5 * jnp.tanh(0.5 * value)
+
+
+def silu_and_slope(value):
+    s = sigmoid(value)
+    silu = value * s
+    return silu, s + silu * (1.0 - s)
+
+
+def head_kernel(
+    divisor, conditions, features, noisy, noise, marks,
+    cond_w, time_w, input_w, ada_w, inner_w, outer_w, final_w, wide_b, ada_b, final_b,
+    signal, mod_low, modulated, inner_low, active, outer_low, final, hidden_low, joined_low, error, sums, cond_low, cond_sum, cond_back,
+    cond, joined, hidden, mod, hat, inner, outer, top, total, spread,
+):
+    step = pl.program_id(0)
+    tile = joined.shape[0]
+    count = tile // ROWS
+    slots = total.shape[0]
+    grad = hidden
+
+    def rows(i):
+        return pl.ds(pl.multiple_of(i * ROWS, ROWS), ROWS)
+
+    def loop(action, *more):
+        def one(i, carry):
+            action(rows(i), *(rows(i % (slots // ROWS)) for _ in more))
+            return carry
+
+        lax.fori_loop(0, count, one, 0)
+
+    def bias(k):
+        return wide_b[k : k + 1, :]
+
+    def add_sum(k, value):
+        sums[k * 8 : (k + 1) * 8, :] = sums[k * 8 : (k + 1) * 8, :] + eighths(value)
+
+    @pl.when(step == 0)
+    def _():
+        sums[...] = jnp.zeros_like(sums)
+        total[...] = jnp.zeros_like(total)
+        cond[...] = matmul(conditions[...], cond_w[...]) + bias(0)
+
+    joined[...] = matmul(features[...], time_w[...])
+    hidden[...] = matmul(noisy[...], input_w[...])
+
+    def enter(at, slot):
+        value, slope = silu_and_slope(joined[at, :] + bias(1) + cond[slot, :])
+        joined[at, :] = slope
+        signal[at, :] = value.astype(NARROW)
+        h = hidden[at, :] + bias(2)
+        hidden[at, :] = h
+        centered = h - jnp.mean(h, -1, keepdims=True)
+        r = lax.rsqrt(jnp.mean(centered * centered, -1, keepdims=True) + NORM_EPS)
+        spread[at, 0:1] = r
+        hat[at, :] = centered * r
+
+    loop(enter, cond)
+    mod[...] = matmul(signal[...], ada_w[...])
+
+    def modulate(at):
+        normed = hat[at, :] * bias(3) + bias(4)
+        shift = mod[at, :HW] + ada_b[0:1, :HW]
+        scale = 1.0 + (mod[at, HW : 2 * HW] + ada_b[0:1, HW : 2 * HW])
+        mod[at, HW : 2 * HW] = scale
+        modulated[at, :] = (normed * scale + shift).astype(NARROW)
+
+    loop(modulate)
+    inner[...] = matmul(modulated[...], inner_w[...])
+
+    def activate(at):
+        value, slope = silu_and_slope(inner[at, :] + bias(5))
+        inner[at, :] = slope
+        active[at, :] = value.astype(NARROW)
+
+    loop(activate)
+    outer[...] = matmul(active[...], outer_w[...])
+
+    def leave(at):
+        out = outer[at, :] + bias(6)
+        outer[at, :] = out
+        gate = mod[at, 2 * HW :] + ada_b[0:1, 2 * HW :]
+        mod[at, 2 * HW :] = gate
+        value = hidden[at, :] + gate * out
+        centered = value - jnp.mean(value, -1, keepdims=True)
+        r = lax.rsqrt(jnp.mean(centered * centered, -1, keepdims=True) + NORM_EPS)
+        spread[at, 1:2] = r
+        value = centered * r
+        top[at, :] = value
+        final[at, :] = value.astype(NARROW)
+
+    loop(leave)
+    off = matmul(final[...], final_w[...]) + final_b[0:1, :] - noise[...]
+    error[...] = off
+    pred_low = (2.0 * off * marks[...] / divisor[0]).astype(NARROW)
+    grad[...] = matmul_turned(pred_low, final_w[...])
+
+    def enter_back(at):
+        g, value = grad[at, :], top[at, :]
+        g = spread[at, 1:2] * (g - jnp.mean(g, -1, keepdims=True) - value * jnp.mean(g * value, -1, keepdims=True))
+        grad[at, :] = g
+        gate_grad = g * outer[at, :]
+        mod_low[at, 2 * HW :] = gate_grad.astype(NARROW)
+        add_sum(0, gate_grad)
+        out_grad = g * mod[at, 2 * HW :]
+        outer_low[at, :] = out_grad.astype(NARROW)
+        add_sum(1, out_grad)
+
+    loop(enter_back)
+    outer[...] = matmul_turned(outer_low[...], outer_w[...])
+
+    def activate_back(at):
+        g = outer[at, :] * inner[at, :]
+        inner_low[at, :] = g.astype(NARROW)
+        add_sum(2, g)
+
+    loop(activate_back)
+    inner[...] = matmul_turned(inner_low[...], inner_w[...])
+
+    def modulate_back(at):
+        g, value = inner[at, :], hat[at, :]
+        mod_low[at, :HW] = g.astype(NARROW)
+        add_sum(3, g)
+        scale_grad = g * (value * bias(3) + bias(4))
+        mod_low[at, HW : 2 * HW] = scale_grad.astype(NARROW)
+        add_sum(4, scale_grad)
+        g = g * mod[at, HW : 2 * HW]
+        add_sum(5, g)
+        add_sum(6, g * value)
+        g = g * bias(3)
+        g = spread[at, 0:1] * (g - jnp.mean(g, -1, keepdims=True) - value * jnp.mean(g * value, -1, keepdims=True))
+        g = grad[at, :] + g
+        hidden_low[at, :] = g.astype(NARROW)
+        add_sum(7, g)
+
+    loop(modulate_back)
+    top[...] = matmul_turned(mod_low[...], ada_w[...])
+
+    def enter_last(at, slot):
+        g = top[at, :] * joined[at, :]
+        joined_low[at, :] = g.astype(NARROW)
+        add_sum(8, g)
+        total[slot, :] = total[slot, :] + g
+
+    loop(enter_last, total)
+
+    @pl.when(step == pl.num_programs(0) - 1)
+    def _():
+        found = total[...].astype(NARROW)
+        cond_low[...] = found
+        cond_back[...] = matmul_turned(found, cond_w[...]).astype(NARROW)
+        acc = jnp.zeros((8, HW), WIDE)
+        for i in range(slots // 8):
+            acc = acc + total[i * 8 : (i + 1) * 8, :]
+        cond_sum[...] = acc
+
+
 def head_pass(p, conditions, clean, filled, steps, noise, divisor):
-    cond = dense(conditions, p.cond_weight) + p.cond_bias.astype(WIDE)
+    slots = conditions.shape[0]
     times = steps.astype(WIDE)
-    features = time_features(times).astype(NARROW)
-    temporal = dense(features, p.time_weight) + p.time_bias.astype(WIDE)
+    features = time_features(times).astype(NARROW).reshape(-1, FREQ)
     level = alpha_level(times)[..., None]
-    noisy = (jnp.sqrt(level) * clean.astype(WIDE) + jnp.sqrt(1.0 - level) * noise).astype(NARROW)
-    hidden_in = dense(noisy, p.input_weight) + p.input_bias.astype(WIDE)
-    joined = temporal + cond[None]
-    signal = jax.nn.silu(joined).astype(NARROW)
-    modulation = dense(signal, p.ada_weight) + p.ada_bias.astype(WIDE)
-    normed = layer_norm(hidden_in, p.head_gain.astype(WIDE), p.head_shift.astype(WIDE))
-    modulated = (normed * (1.0 + modulation[..., HW : 2 * HW]) + modulation[..., :HW]).astype(NARROW)
-    inner = dense(modulated, p.inner_weight) + p.inner_bias.astype(WIDE)
-    active = jax.nn.silu(inner).astype(NARROW)
-    outer = dense(active, p.outer_weight) + p.outer_bias.astype(WIDE)
-    hidden = hidden_in + modulation[..., 2 * HW :] * outer
-    final = layer_norm(hidden, 1.0, 0.0).astype(NARROW)
-    predicted = dense(final, p.final_weight) + p.final_bias.astype(WIDE)
-    error = predicted - noise
-    marks = filled.astype(WIDE)
-    loss_part = jnp.sum(jnp.sum(error * error, -1) * marks)
-    pred_grad = 2.0 * error * marks[:, None] / divisor
-    pred_low = pred_grad.astype(NARROW)
-    hidden_grad = jax.vjp(lambda value: layer_norm(value, 1.0, 0.0), hidden)[1](back_input(pred_low, p.final_weight))[0]
-    gate_grad = hidden_grad * outer
-    outer_grad = hidden_grad * modulation[..., 2 * HW :]
-    outer_low = outer_grad.astype(NARROW)
-    inner_grad = jax.vjp(jax.nn.silu, inner)[1](back_input(outer_low, p.outer_weight))[0]
-    inner_low = inner_grad.astype(NARROW)
-    mod_grad = back_input(inner_low, p.inner_weight)
-    pull = norm_pull(hidden_in, p.head_gain, p.head_shift)
-    norm_grad, head_gain, head_shift = pull(mod_grad * (1.0 + modulation[..., HW : 2 * HW]))
-    hidden_grad = hidden_grad + norm_grad
-    modulation_grad = jnp.concatenate([mod_grad, mod_grad * normed, gate_grad], -1)
-    modulation_low = modulation_grad.astype(NARROW)
-    signal_grad = back_input(modulation_low, p.ada_weight)
-    joined_grad = jax.vjp(jax.nn.silu, joined)[1](signal_grad)[0]
-    joined_low = joined_grad.astype(NARROW)
-    cond_grad = jnp.sum(joined_grad, 0)
-    cond_low = cond_grad.astype(NARROW)
-    hidden_low = hidden_grad.astype(NARROW)
+    noisy = (jnp.sqrt(level) * clean.astype(WIDE) + jnp.sqrt(1.0 - level) * noise).astype(NARROW).reshape(-1, TOK_CH)
+    flat_noise = noise.reshape(-1, TOK_CH)
+    marks = jnp.tile(filled.astype(WIDE)[:, None], (COPIES, 1))
+    wide_b = jnp.stack(
+        [p.cond_bias, p.time_bias, p.input_bias, p.head_gain, p.head_shift, p.inner_bias, p.outer_bias, p.outer_bias]
+    ).astype(WIDE)
+    total = COPIES * slots
+
+    def tiled(width):
+        return pl.BlockSpec((TOGETHER * slots, width), lambda i: (i, 0))
+
+    def whole(x):
+        return pl.BlockSpec(x, lambda i: (0, 0), pipeline_mode=pl.Buffered(1))
+
+    weights = (p.cond_weight, p.time_weight, p.input_weight, p.ada_weight, p.inner_weight, p.outer_weight, p.final_weight)
+    biases = (wide_b, p.ada_bias.astype(WIDE)[None], p.final_bias.astype(WIDE)[None])
+    widths = (HW, 3 * HW, HW, HW, HW, HW, HW, HW, HW)
+    kept = [((total, w), NARROW, tiled(w)) for w in widths] + [((total, TOK_CH), WIDE, tiled(TOK_CH))]
+    kept += [(s, t, whole(s)) for s, t in (((SUMS * 8, HW), WIDE), ((slots, HW), NARROW), ((8, HW), WIDE), ((slots, D), NARROW))]
+    flops = 4 * total * (FREQ * HW // 2 + 5 * HW * HW) + 4 * slots * D * HW
+    found = pl.pallas_call(
+        head_kernel,
+        grid=(COPIES // TOGETHER,),
+        out_shape=[jax.ShapeDtypeStruct(s, t) for s, t, _ in kept],
+        in_specs=[pl.BlockSpec(memory_space=pltpu.SMEM), whole(conditions.shape), tiled(FREQ), tiled(TOK_CH), tiled(TOK_CH), tiled(1)]
+        + [whole(x.shape) for x in weights + biases],
+        out_specs=[spec for _, _, spec in kept],
+        scratch_shapes=[
+            pltpu.VMEM((n * slots, w), WIDE)
+            for n, w in [(1, HW)] + [(TOGETHER, w) for w in (HW, HW, 3 * HW, HW, HW, HW, HW)] + [(1, HW), (TOGETHER, LANES)]
+        ],
+        compiler_params=pltpu.CompilerParams(vmem_limit_bytes=60 * 1000 * 1000),
+        cost_estimate=pl.CostEstimate(flops=flops, bytes_accessed=26 * total * HW, transcendentals=3 * total * HW),
+    )(divisor[None], conditions, features, noisy, flat_noise, marks, *weights, *biases)
+    signal, mod_low, modulated, inner_low, active, outer_low, final, hidden_low, joined_low, error, sums, cond_low, cond_sum, cond_back = found
+    sums = jnp.sum(sums.reshape(SUMS, 8, HW), 1)
+    loss_part = jnp.sum(jnp.sum(error * error, -1) * marks[:, 0])
+    pred_grad = 2.0 * error * marks / divisor
     grads = dict(
-        final_weight=weight_grad(final, pred_low), final_bias=rows_sum(pred_grad),
-        outer_weight=weight_grad(active, outer_low), outer_bias=rows_sum(outer_grad),
-        inner_weight=weight_grad(modulated, inner_low), inner_bias=rows_sum(inner_grad),
-        head_gain=head_gain, head_shift=head_shift,
-        ada_weight=weight_grad(signal, modulation_low), ada_bias=rows_sum(modulation_grad),
-        time_weight=weight_grad(features, joined_low), time_bias=rows_sum(joined_grad),
-        cond_weight=weight_grad(conditions, cond_low), cond_bias=rows_sum(cond_grad),
-        input_weight=weight_grad(noisy, hidden_low), input_bias=rows_sum(hidden_grad),
+        final_weight=weight_grad(final, pred_grad.astype(NARROW)), final_bias=rows_sum(pred_grad),
+        outer_weight=weight_grad(active, outer_low), outer_bias=sums[1],
+        inner_weight=weight_grad(modulated, inner_low), inner_bias=sums[2],
+        head_gain=sums[6], head_shift=sums[5],
+        ada_weight=weight_grad(signal, mod_low), ada_bias=jnp.concatenate([sums[3], sums[4], sums[0]]),
+        time_weight=weight_grad(features, joined_low), time_bias=sums[8],
+        cond_weight=weight_grad(conditions, cond_low), cond_bias=rows_sum(cond_sum),
+        input_weight=weight_grad(noisy, hidden_low), input_bias=sums[7],
     )
-    return loss_part, grads, back_input(cond_low, p.cond_weight)
+    return loss_part, grads, cond_back
 
 
 def exchange(payload, parts):

time: 919 us -> 827 us (0.90)
  matrix products: 156 us -> 11.8 us
  Pallas kernels: 594 us -> 705 us
  local copies, waits for them, and re-layouts: 52 us -> 22.4 us
  other arithmetic: 80.8 us -> 51.8 us
    pallas_call x0 -> x5, Pallas kernels: none -> 119 us  [the longest x1 43.6 us: head_pass(): pl.pallas_call(head_kernel, grid=(COPIES // TOGETHER,), out_shape=[jax.Sh...]
    dot_general x14 -> x1, matrix products: 66.3 us -> 1.33 us  [back_input(): lax.dot_general(grads_low, weight, (((grads_low.ndim - 1,), (1,)), ((), (...]
    dot_general x18 -> x3, matrix products: 58.3 us -> 2.94 us  [dense(): lax.dot_general(inputs, weight, (((inputs.ndim - 1,), (0,)), ((), ())), p...]
    dot_general x12 -> x0, matrix products: 27.8 us -> none  [the longest x2 9.2 us: block_backward(): jnp.einsum('hqk,qhe->khe', probs.astype(NARROW), attended_grad, preferred...]
    slice x8 -> x5, local copies, waits for them, and re-layouts: 13.2 us -> 3.62 us  [the longest x2 2.28 us: block_backward(): sums[0]]
  transfers between devices with their start and end apart: 2 -> 2, of which waited for: 1 -> 2; matrix products, arithmetic and copies ran while one was open for 2% -> 2% of each run, Pallas kernels for 0% -> 0%
where the time goes in v2:
time: 827 us; the launch traced here: 816 us
  Pallas kernels  705 us (85%)
  other arithmetic  51.8 us (6%)
  local copies, waits for them, and re-layouts  22.4 us (3%)
  starting transfers between devices  16.2 us (2%)
  matrix products  11.8 us (1%)
    pallas_call x1, Pallas kernels, collect(): pl.pallas_call(functools.partial(collect_kernel, size), out_shape=(jax.Sh...  328 us
    pallas_call x1, Pallas kernels, spread(): pl.pallas_call(spread_kernel, out_shape=jax.ShapeDtypeStruct((32,) + own....  162 us
    pallas_call x1, Pallas kernels, fold(): pl.pallas_call(functools.partial(fold_kernel, products, items, plain), ou...  53.4 us
    pallas_call x1, Pallas kernels, head_pass(): pl.pallas_call(head_kernel, grid=(COPIES // TOGETHER,), out_shape=[jax.Sh...  43.6 us
    pallas_call x2, Pallas kernels, block_backward(): pl.pallas_call(functools.partial(backward_kernel, keep is not None), out_...  42.7 us
    pallas_call x1, Pallas kernels, unfold(): pl.pallas_call(functools.partial(unfold_kernel, rows, padded, items), out...  41.4 us
    pallas_call x2, Pallas kernels, block_forward(): pl.pallas_call(functools.partial(forward_kernel, keep is not None), out_s...  33.1 us
  transfers between devices with their start and end apart: 2, of which 2 were waited for; matrix products, arithmetic and copies ran while one was open for 2% of the time, Pallas kernels for 0%

profile of v2, /device:TPU:21, one launch (start us, length us, event | category | flops | bytes accessed | tf_op | source)
XLA Modules:
  0.0 815.8 jit_solution(13531691000057969337)
XLA Ops:
  0.6 1.3 convert_reduce_fusion.2
  1.9 0.7 fusion.37
  2.6 1.9 convert_bitcast_fusion
  4.5 1.8 concatenate.80.own
  6.4 161.8 %shard_map.120.g_ref = bf16[32,5520,128]{2,1,0:T(8,128)(2,1)} custom-call(bf16[5520,128]{1,0:T(8,128)(2,1)} %concatenate.80.own), custom_call_target="tpu_custom_call" | custom-call | tf_op jit(solution)/shard_map/pallas_call | solution.py:545
  168.2 0.8 slice_bitcast_fusion.20
  169.0 1.3 slice_convert_fusion.3
  170.3 0.8 bitcast_convert_fusion.1
  171.1 41.4 %shard_map.121 = (bf16[16,768]{1,0:T(8,128)(2,1)S(1)}, bf16[320,768]{1,0:T(8,128)(2,1)S(1)}, bf16[768,2304]{1,0:T(8,128)(2,1)}, bf16[768,768]{1,0:T(8,128)(2,1)S...) custom-call(bf16[32,5520,128]{2,1,0:T(8,128)(2,1)} %shard_map.120.g_ref), custom_call_target="tpu_custom_call" | custom-call | flops 21753856 | bytes 87015424 | tf_op jit(solution)/shard_map/pallas_call | solution.py:229
  212.5 1.0 copy-done
  213.5 1.0 copy-done.1
  214.6 1.1 copy-done.2
  215.7 0.8 copy-done.3
  219.4 1.3 gather_fusion
  222.4 1.1 maximum_add_fusion.stream
  224.1 16.3 %shard_map.122 = (bf16[320,768]{1,0:T(8,128)(2,1)}, bf16[320,2304]{1,0:T(8,128)(2,1)}, f32[320,128]{1,0:T(8,128)}, bf16[320,768]{1,0:T(8,128)(2,1)}, f32[320,768...) custom-call(f32[320,768]{1,0:T(8,128)} %maximum_add_fusion.stream, ...), custom_call_target="tpu_custom_call" | custom-call | flops 4529848320 | bytes 23003136 | tf_op jit(solution)/shard_map/pallas_call | solution.py:867
  240.4 1.3 reduce_sum.212
  241.8 1.5 multiply_reduce_fusion.4
  243.3 1.4 add_convert_fusion.refs_8_
  244.7 1.5 fusion.3.stream
  246.8 16.8 %shard_map.123 = (bf16[320,768]{1,0:T(8,128)(2,1)}, bf16[320,2304]{1,0:T(8,128)(2,1)}, f32[320,128]{1,0:T(8,128)}, bf16[320,768]{1,0:T(8,128)(2,1)}, f32[320,768...) custom-call(f32[320,768]{1,0:T(8,128)} %fusion.3.stream, ...), custom_call_target="tpu_custom_call" | custom-call | flops 4529848320 | bytes 23003136 | tf_op jit(solution)/shard_map/pallas_call | solution.py:867
  263.7 1.4 reduce_sum.217
  265.0 1.5 multiply_reduce_fusion.3
  266.5 1.4 subtract_multiply_fusion
  268.1 1.1 convolution_convert_fusion
  269.2 10.3 %all-to-all-start = ((bf16[8,32,896]{2,1,0:T(8,128)(2,1)}), bf16[8,32,896]{2,1,0:T(8,128)(2,1)S(1)}, u32[]{:S(2)}, u32[]{:S(2)}) async-start(bf16[8,32,896]{2,1,0:T(8,128)(2,1)} %bitcast.16), calls=%async_computation | async-start | bytes 917504 | tf_op jit(solution)/shard_map/all_to_all | solution.py:1208
  279.5 1.5 convert_reduce_fusion.1
  281.0 0.8 slice_bitcast_fusion
  281.8 0.8 slice.250
  282.6 1.0 copy.27
  284.3 0.9 reshape_reshape_squeeze.3.final_w
  285.9 2.2 fusion.9
  288.1 0.9 pad_maximum_fusion.features.refs_18_
  289.0 1.2 bitcast_convert_fusion.8.final_b
  290.8 0.8 slice.292.conditions.refs_20_
  291.7 0.8 copy.26
  292.6 1.0 copy.49
  293.6 43.6 %shard_map.124 = (bf16[1024,1024]{1,0:T(8,128)(2,1)}, bf16[1024,3072]{1,0:T(8,128)(2,1)}, bf16[1024,1024]{1,0:T(8,128)(2,1)}, bf16[1024,1024]{1,0:T(8,128)(2,1)}...) custom-call(f32[1]{0:T(128)} %bitcast.1.divisor, ...), custom_call_target="tpu_custom_call" | custom-call | flops 22817013760 | bytes 27262976 | tf_op jit(solution)/shard_map/pallas_call | solution.py:1175
  337.2 1.4 reduce_sum.244
  338.6 1.4 multiply_reduce_fusion.5
  340.0 2.7 fusion.16
  342.7 0.8 reshape.564.refs_64_
  344.0 5.9 all-to-all-start.1
  349.9 1.0 bitcast_reduce_fusion
  353.5 2.6 fusion.44.refs_32_
  356.1 3.5 all-to-all-done.1
  360.0 1.0 pad_reduce_fusion
  361.4 1.1 broadcast_add_fusion.1.grad_out
  362.5 21.5 %shard_map.125 = (bf16[320,768]{1,0:T(8,128)(2,1)}, bf16[320,3072]{1,0:T(8,128)(2,1)}, bf16[320,768]{1,0:T(8,128)(2,1)}, bf16[320,2304]{1,0:T(8,128)(2,1)}, f32[...) custom-call(f32[320,768]{1,0:T(8,128)} %broadcast_add_fusion.1.grad_out, ...), custom_call_target="tpu_custom_call" | custom-call | flops 4529848320 | bytes 23003136 | tf_op jit(solution)/shard_map/pallas_call | solution.py:941
  384.0 2.0 select_reduce_fusion
  386.0 1.3 select_convert_fusion.refs_9_
  387.3 1.3 multiply_reduce_fusion
  389.1 1.1 broadcast_add_fusion.grad_out
  390.2 21.2 %shard_map.126 = (bf16[320,768]{1,0:T(8,128)(2,1)}, bf16[320,3072]{1,0:T(8,128)(2,1)}, bf16[320,768]{1,0:T(8,128)(2,1)}, bf16[320,2304]{1,0:T(8,128)(2,1)}, f32[...) custom-call(f32[320,768]{1,0:T(8,128)} %broadcast_add_fusion.grad_out, ...), custom_call_target="tpu_custom_call" | custom-call | flops 4529848320 | bytes 23003136 | tf_op jit(solution)/shard_map/pallas_call | solution.py:941
  411.4 1.8 slice_reduce_fusion
  413.2 0.9 slice_reduce_fusion.1
  414.2 1.9 convolution_bitcast_fusion.refs_28_
  416.1 0.6 slice_reduce_fusion.2
  416.8 0.7 slice_reduce_fusion.15
  417.5 1.6 slice_reduce_fusion.10
  421.5 53.4 %shard_map.127.refs_0_ = f32[176368,128]{1,0:T(8,128)} custom-call(s32[1]{0:T(128)S(6)} %copy.83.label, f32[8,768]{1,0:T(8,128)} %broadcast_in_dim.79.row, bf16[320,768]{1,0:T(8,128)(2,1)} %get-tuple-element.104.refs_0_, bf16[320,2304]{1,0:T(8,128)(2,1)} %get-tuple-element.105.refs_1_, bf16[320,768]{1,0:T(8,128)(2,1)} %get-tuple-element.106.refs_2_, ...), custom_call_target="tpu_custom_call" | custom-call | flops 21114126336 | bytes 90300416 | tf_op jit(solution)/shard_map/pallas_call | solution.py:385
  475.6 328.5 %shard_map.128 = (f32[5520,128]{1,0:T(8,128)}, f32[96,920,128]{2,1,0:T(8,128)}) custom-call(f32[176368,128]{1,0:T(8,128)} %shard_map.127.refs_0_, f32[8,128]{1,0:T(8,128)} %iota.23.refs_1_), custom_call_target="tpu_custom_call" | custom-call | tf_op jit(solution)/shard_map/pallas_call | solution.py:723
  804.0 1.3 slice_reduce_fusion.18
  806.0 8.4 %multiply_add_fusion = (f32[705408]{0:T(1024)}, f32[705408]{0:T(1024)}, f32[705408]{0:T(1024)}) fusion(f32[705408]{0:T(1024)} %param.17, f32[705408]{0:T(1024)} %param.15, f32[5520,128]{1,0:T(8,128)} %get-tuple-element.139, f32[705408]{0:T(1024)} %param.16), kind=kLoop, calls=%fused_computation.5 | loop fusion | flops 6348672 | bytes 19751424 | tf_op jit(solution)/shard_map/add | solution.py:1289
  (101 shorter events, 13.2 us)
Async XLA Ops:
  171.1 48.2 %copy-start.12 = (bf16[256,16]{0,1:T(8,128)(2,1)S(1)}, bf16[256,16]{0,1:T(8,128)(2,1)}, u32[]{:S(2)}) copy-start(bf16[256,16]{0,1:T(8,128)(2,1)} %param.9) | copy-start | bytes 24580
  212.5 1.0 copy-start
  213.5 1.1 copy-start.1
  214.6 1.1 copy-start.2
  215.7 0.8 copy-start.3
  216.5 0.6 copy-start.4
  244.7 18.9 %copy-start.8 = (bf16[320,768]{1,0:T(8,128)(2,1)}, bf16[320,768]{1,0:T(8,128)(2,1)S(1)}, u32[]{:S(2)}) copy-start(bf16[320,768]{1,0:T(8,128)(2,1)S(1)} %add_convert_fusion.refs_8_) | copy-start | bytes 1474564
  263.7 4.4 copy-start.16
  266.5 16.0 %copy-start.13 = (s32[4,256]{1,0:T(4,128)S(1)}, s32[4,256]{1,0:T(4,128)}, u32[]{:S(2)}) copy-start(s32[4,256]{1,0:T(4,128)} %param.12) | copy-start | bytes 12292
  266.5 16.1 %copy-start.11 = (f32[4,256,16]{1,2,0:T(8,128)S(1)}, f32[4,256,16]{1,2,0:T(8,128)}, u32[]{:S(2)}) copy-start(f32[4,256,16]{1,2,0:T(8,128)} %param.13) | copy-start | bytes 196612
  269.2 21.4 %all-to-all-start = ((bf16[8,32,896]{2,1,0:T(8,128)(2,1)}), bf16[8,32,896]{2,1,0:T(8,128)(2,1)S(1)}, u32[]{:S(2)}, u32[]{:S(2)}) async-start(bf16[8,32,896]{2,1,0:T(8,128)(2,1)} %bitcast.16), calls=%async_computation | async-start | bytes 917504 | tf_op jit(solution)/shard_map/all_to_all | solution.py:1208
  340.0 13.5 %copy-start.10 = (bf16[4,256,16]{2,1,0:T(8,128)(2,1)S(1)}, bf16[4,256,16]{2,1,0:T(8,128)(2,1)}, u32[]{:S(2)}) copy-start(bf16[4,256,16]{2,1,0:T(8,128)(2,1)} %copy.26) | copy-start | bytes 98308
  342.7 17.2 %copy-start.5 = (f32[320,768]{1,0:T(8,128)S(1)}, f32[320,768]{1,0:T(8,128)}, u32[]{:S(2)}) copy-start(f32[320,768]{1,0:T(8,128)} %get-tuple-element.85) | copy-start | bytes 2949124
  344.0 15.6 %all-to-all-start.1 = ((bf16[8,32,768]{2,1,0:T(8,128)(2,1)}), bf16[8,32,768]{2,1,0:T(8,128)(2,1)S(1)}, u32[]{:S(2)}, u32[]{:S(2)}) async-start(bf16[8,32,768]{2,1,0:T(8,128)(2,1)} %bitcast.222), calls=%async_computation.1 | async-start | bytes 786432 | tf_op jit(solution)/shard_map/all_to_all | solution.py:1208
  359.9 2.5 copy-start.7
  362.5 24.9 %copy-start.6 = (f32[320,768]{1,0:T(8,128)S(1)}, f32[320,768]{1,0:T(8,128)}, u32[]{:S(2)}) copy-start(f32[320,768]{1,0:T(8,128)} %get-tuple-element.78) | copy-start | bytes 2949124
  387.3 1.8 copy-start.9
  390.2 25.9 %copy-start.15 = (f32[1,2304]{1,0:T(1,128)S(1)}, f32[1,2304]{1,0:T(1,128)}, u32[]{:S(2)}) copy-start(f32[1,2304]{1,0:T(1,128)} %get-tuple-element.133) | copy-start | bytes 27652
  390.2 25.9 %copy-start.14 = (f32[8,768]{1,0:T(8,128)S(1)}, f32[8,768]{1,0:T(8,128)}, u32[]{:S(2)}) copy-start(f32[8,768]{1,0:T(8,128)} %get-tuple-element.132) | copy-start | bytes 73732

commit v3 on v2

--- a/solution.py
+++ b/solution.py
@@ -28,6 +28,8 @@
 NORM_EPS = 1e-06
 MESH = pl.DeviceIdType.MESH
 ANY = pl.BlockSpec(memory_space=pl.ANY)
+HBM = pl.BlockSpec(memory_space=pltpu.HBM)
+VMEM = pl.BlockSpec(memory_space=pltpu.VMEM)
 DMA = pltpu.SemaphoreType.DMA
 BOTH = ("dp", "rep")
 
@@ -119,7 +121,8 @@
             before().wait()
 
 
-SLOTS = 4
+SLOTS = 8
+OUT = 3
 
 
 def unfold_kernel(rows, padded, items, g_ref, *refs):
@@ -128,7 +131,7 @@
     first, second, wide, first_sem, second_sem, out_sem = refs[count : count + 6]
     kinds = sorted({(h, e.across) for e, h in items})
     stages = dict(zip(kinds, refs[count + 6 :]))
-    turns = {kind: Slots(2) for kind in kinds}
+    turns = {kind: Slots(OUT) for kind in kinds}
     bases = [0]
     for entry, height in items:
         bases.append(bases[-1] + entry.shape[0] // height)
@@ -179,7 +182,7 @@
         blocks = entry.shape[0] // height
 
         def put(b, t=t, stage=stage, height=height, place=turn.base, kind=kind):
-            slot = (place + b) % 2
+            slot = (place + b) % OUT
             return pltpu.make_async_copy(
                 stage.at[slot], outs[t].at[pl.ds(pl.multiple_of(b * height, 8), height)], out_sem.at[kinds.index(kind), slot]
             )
@@ -233,9 +236,9 @@
         out_specs=[ANY] * len(items),
         scratch_shapes=[
             pltpu.VMEM((SLOTS, tall, LANES), NARROW), pltpu.VMEM((SLOTS, tall, LANES), NARROW),
-            pltpu.VMEM((2 * tall, LANES), WIDE), DMA((SLOTS,)), DMA((SLOTS,)), DMA((len(kinds), 2)),
+            pltpu.VMEM((2 * tall, LANES), WIDE), DMA((SLOTS,)), DMA((SLOTS,)), DMA((len(kinds), OUT)),
         ]
-        + [pltpu.VMEM((2, h, n * LANES), NARROW) for h, n in kinds],
+        + [pltpu.VMEM((OUT, h, n * LANES), NARROW) for h, n in kinds],
         compiler_params=pltpu.CompilerParams(vmem_limit_bytes=48 * 1000 * 1000),
         cost_estimate=pl.CostEstimate(flops=total, bytes_accessed=4 * total, transcendentals=0),
     )(gathered)
@@ -252,9 +255,8 @@
     return pieces[0] if len(pieces) == 1 else jnp.concatenate(pieces, 0)
 
 
-def unpack(gathered, rows):
+def unpack(gathered, rows, groups):
     matrices = unfold(gathered, rows)
-    groups = [types.SimpleNamespace() for _ in GROUPS]
     for e in ENTRIES:
         if e.sparse:
             continue
@@ -263,7 +265,6 @@
         else:
             value = rows_at(gathered, rows, e.start, e.rows).reshape(-1)[: math.prod(e.shape)].reshape(e.shape)
         setattr(groups[e.group], e.name, value)
-    return groups
 
 
 DEPTH = 3
@@ -276,23 +277,31 @@
     return min(TALL, entry.shape[0])
 
 
-def fold_kernel(products, items, plain, label, row, *refs):
+def fold_kernel(products, items, plain, vectors, lone_place, zero, count, going_on, label, *refs):
     refs = list(refs)
 
     def take(number):
         found, refs[:number] = refs[:number], []
         return found
 
+    small = take(count)
     pairs = take(2 * len(products))
     given = take(len(items))
     rest = take(len(plain))
+    take(int(going_on))
     (full,) = take(1)
-    pair_sem, given_sem, plain_sem, out_sem = take(4)
+    pair_sem, given_sem, plain_sem, out_sem, vector_sem = take(5)
     held = take(2 * len(products))
     loads = take(len(items))
-    (stage,) = take(1)
+    stage, lines = take(2)
     gets = [pltpu.make_async_copy(given[i], loads[i], given_sem.at[i]) for i in range(len(items))]
-    fills = [pltpu.make_async_copy(pairs[i], held[i], pair_sem.at[i]) for i in range(len(pairs))]
+    fills = []
+    for i, entry in enumerate(products):
+        for k in (2 * i, 2 * i + 1):
+            source = pairs[k]
+            if source.shape != held[k].shape:
+                source = source.at[:, pl.ds(0, held[k].shape[1])]
+            fills.append(pltpu.make_async_copy(source, held[k], pair_sem.at[k]))
     for move in gets + fills[: 2 * NEXT]:
         move.start()
     moves = []
@@ -300,6 +309,22 @@
         move = pltpu.make_async_copy(rest[i].at[pl.ds(0, number)], full.at[pl.ds(start, number)], plain_sem.at[i])
         move.start()
         moves.append(move)
+    at = 0
+    for i, (entry, which, parts) in enumerate(vectors):
+        begin = at
+        for k, column, width in parts:
+            for j in range(0, width, LANES):
+                lines[at : at + 1, :] = small[which][k : k + 1, column + j : column + j + LANES]
+                at += 1
+        move = pltpu.make_async_copy(lines.at[pl.ds(begin, at - begin)], full.at[pl.ds(entry.start, at - begin)], vector_sem.at[i])
+        move.start()
+        moves.append(move)
+        at = -(-at // 8) * 8
+    if zero:
+        lines[at : at + zero, :] = jnp.zeros((zero, LANES), WIDE)
+        move = pltpu.make_async_copy(lines.at[pl.ds(at, zero)], full.at[pl.ds(USED, zero)], vector_sem.at[len(vectors)])
+        move.start()
+        moves.append(move)
     turn = Slots(DEPTH)
 
     def each(entry, height, make):
@@ -321,16 +346,18 @@
         lax.fori_loop(0, blocks, step, 0)
         turn.close(blocks, put)
 
-    sparse = next(e for e in ENTRIES if e.sparse)
-    height = block_height(sparse, 1200)
-
-    def lone(b, slot):
-        here = lax.broadcasted_iota(jnp.int32, (height, LANES), 0) + b * height == label[0]
-        for j in range(sparse.across):
-            value = jnp.broadcast_to(row[0:1, j * LANES : (j + 1) * LANES], (height, LANES))
-            stage[slot, pl.ds(j, height, stride=sparse.across), :] = jnp.where(here, value, 0.0)
-
-    each(sparse, height, lone)
+    if lone_place:
+        sparse = next(e for e in ENTRIES if e.sparse)
+        height = block_height(sparse, 1200)
+        row, row_at = small[lone_place[0]], lone_place[1]
+
+        def lone(b, slot):
+            here = lax.broadcasted_iota(jnp.int32, (height, LANES), 0) + b * height == label[0]
+            for j in range(sparse.across):
+                value = jnp.broadcast_to(row[row_at : row_at + 1, j * LANES : (j + 1) * LANES], (height, LANES))
+                stage[slot, pl.ds(j, height, stride=sparse.across), :] = jnp.where(here, value, 0.0)
+
+        each(sparse, height, lone)
     for t, entry in enumerate(items):
         gets[t].wait()
 
@@ -362,39 +389,45 @@
         move.wait()
 
 
-def fold(grads, label, height_total):
-    found = {e: grads[(e.group, e.name)] for e in ENTRIES}
-    products = [e for e in ENTRIES if isinstance(found[e], tuple)]
-    items = [e for e in ENTRIES if e.matrix and not e.sparse and e not in products]
-    plain, values = [], []
-    for e in ENTRIES:
-        if e.matrix:
-            continue
-        value = found[e].reshape(-1)
-        value = jnp.pad(value, (0, e.rows * LANES - value.shape[0]))
-        plain.append((e.start, e.rows))
-        values.append(value.reshape(e.rows, LANES))
-    if height_total > USED:
-        plain.append((USED, height_total - USED))
-        values.append(jnp.zeros((height_total - USED, LANES), WIDE))
-    row = next(found[e] for e in ENTRIES if e.sparse)
-    operands = [x.reshape(-1, x.shape[-1]) for e in products for x in found[e]]
+def fold(grads, label, height_total, full=None):
+    wanted = [e for e in ENTRIES if (e.group, e.name) in grads]
+    found = {e: grads[(e.group, e.name)] for e in wanted}
+    products = [e for e in wanted if isinstance(found[e], tuple)]
+    items = [e for e in wanted if e.matrix and not isinstance(found[e], (tuple, Vector))]
+    small, vectors, plain, values, lone_place = [], [], [], [], None
+    for e in wanted:
+        if isinstance(found[e], Vector):
+            place = next((i for i, x in enumerate(small) if x is found[e].array), len(small))
+            small[place : place + 1] = [found[e].array]
+            if e.sparse:
+                lone_place = (place, found[e].parts[0][0])
+            else:
+                vectors.append((e, place, found[e].parts))
+        elif not e.matrix and e not in products:
+            plain.append((e.start, e.rows))
+            values.append(found[e].reshape(e.rows, LANES))
+    zero = height_total - USED if full is None else 0
+    before = [] if full is None else [full]
+    lines = sum(-(-e.rows // 8) * 8 for e, _, _ in vectors) + -(-zero // 8) * 8
+    operands = [x for e in products for x in found[e]]
+    holds = [(x.shape[0], n) for e in products for x, n in zip(found[e], e.shape)]
     tall = max([e.rows for e in items] + [e.across * product_height(e) for e in products])
-    total = height_total * LANES
+    total = sum(e.rows for e in wanted) * LANES
+    taken = 1 + len(small) + len(operands) + len(items) + len(plain)
     flops = sum(2 * math.prod(e.shape) * operands[2 * i].shape[0] for i, e in enumerate(products))
     return pl.pallas_call(
-        functools.partial(fold_kernel, products, items, plain),
+        functools.partial(fold_kernel, products, items, plain, vectors, lone_place, zero, len(small), bool(before)),
         out_shape=jax.ShapeDtypeStruct((height_total, LANES), WIDE),
-        in_specs=[pl.BlockSpec(memory_space=pltpu.SMEM), pl.BlockSpec(memory_space=pltpu.VMEM)]
-        + [ANY] * (len(operands) + len(items) + len(plain)),
+        in_specs=[pl.BlockSpec(memory_space=pltpu.SMEM)] + [VMEM] * len(small) + [ANY] * (len(operands) + len(items) + len(plain) + len(before)),
         out_specs=ANY,
-        scratch_shapes=[DMA((len(operands),)), DMA((len(items),)), DMA((len(plain),)), DMA((DEPTH,))]
-        + [pltpu.VMEM(x.shape, x.dtype) for x in operands]
+        input_output_aliases={taken: 0} if before else {},
+        scratch_shapes=[DMA((len(operands),)), DMA((len(items),)), DMA((max(len(plain), 1),)), DMA((DEPTH,)), DMA((len(vectors) + 1,))]
+        + [pltpu.VMEM(s, NARROW) for s in holds]
         + [pltpu.VMEM(e.shape, WIDE) for e in items]
-        + [pltpu.VMEM((DEPTH, tall, LANES), WIDE)],
+        + [pltpu.VMEM((DEPTH, tall, LANES), WIDE), pltpu.VMEM((lines, LANES), WIDE)],
         compiler_params=pltpu.CompilerParams(vmem_limit_bytes=62 * 1000 * 1000),
         cost_estimate=pl.CostEstimate(flops=flops, bytes_accessed=4 * total, transcendentals=0),
-    )(label, jnp.broadcast_to(row, (8, row.shape[-1])), *operands, *[found[e] for e in items], *values)
+    )(label, *small, *operands, *[found[e] for e in items], *values, *before)
 
 
 X, Y, Z = 0, 1, 2
@@ -734,40 +767,21 @@
     )(full, mark)[0]
 
 
-def layer_norm(value, gain, shift):
-    centered = value - jnp.mean(value, -1, keepdims=True)
-    scaled = centered * lax.rsqrt(jnp.mean(centered * centered, -1, keepdims=True) + NORM_EPS)
-    return scaled * gain + shift
-
-
-def dense(inputs, weight):
-    return lax.dot_general(inputs, weight, (((inputs.ndim - 1,), (0,)), ((), ())), preferred_element_type=WIDE)
-
-
-def back_input(grads_low, weight):
-    return lax.dot_general(grads_low, weight, (((grads_low.ndim - 1,), (1,)), ((), ())), preferred_element_type=WIDE)
-
-
-def weight_grad(inputs, grads_low):
-    flat_in = inputs.reshape(-1, inputs.shape[-1])
-    flat_grad = grads_low.reshape(-1, grads_low.shape[-1])
-    if min(flat_in.shape[1], flat_grad.shape[1]) >= LANES:
-        return flat_in, flat_grad
-    return lax.dot_general(flat_in, flat_grad, (((0,), (0,)), ((), ())), preferred_element_type=WIDE)
-
-
-def rows_sum(values):
-    return jnp.sum(values.reshape(-1, values.shape[-1]), 0)
-
-
-def norm_pull(value, gain, shift):
-    return jax.vjp(layer_norm, value, gain.astype(WIDE), shift.astype(WIDE))[1]
-
-
 HALF_ROOT = math.sqrt(0.5)
 PDF = 1.0 / math.sqrt(2.0 * math.pi)
 SCALE = HEAD_DIM ** (-0.5)
 PART = 512
+BIG = pltpu.CompilerParams(vmem_limit_bytes=66 * 1000 * 1000)
+BLOCK_WEIGHTS = ((D, 3 * D), (D, D), (D, MLP), (MLP, D))
+EMBED_B, ENC_G, ENC_S, DEC_B, MASK_T, DEC_G, DEC_S, CLASS, ENC_ROWS, DEC_ROWS, ALL_ROWS = 0, 1, 2, 3, 4, 5, 6, 7, 8, 14, 24
+
+
+def matmul(left, right):
+    return jnp.dot(left, right, preferred_element_type=WIDE)
+
+
+def matmul_turned(left, right):
+    return lax.dot_general(left, right, (((1,), (1,)), ((), ())), preferred_element_type=WIDE)
 
 
 def column_sum(value):
@@ -800,24 +814,32 @@
     return moves
 
 
-def forward_kernel(masked, stream, keep, wide_b, attn_b, fc_b, *refs):
-    outs = refs[4:13]
-    normed, mixed, totals, attended, middle, second, slope, active, output = outs
-    attn_w, proj_w, one_w, two_w, sem = refs[13:]
-    moves = start_all(refs[:4], (attn_w, proj_w, one_w, two_w), sem)
-    hat, _ = whiten(stream[...])
-    normed[...] = (hat * wide_b[0:1, :] + wide_b[1:2, :]).astype(NARROW)
+def block_vectors(base, enc, mid, dec, head, classes):
+    rows = [base.embed_bias, mid.enc_gain, mid.enc_shift, mid.dec_bias, mid.mask_token, head.dec_gain, head.dec_shift, classes]
+    for p in (enc, dec):
+        rows += [p.norm_one_gain, p.norm_one_shift, p.norm_two_gain, p.norm_two_shift, p.proj_bias, p.fc_two_bias]
+    rows += rows[: ALL_ROWS - len(rows)]
+    gap = jnp.zeros((D,), NARROW)
+    attn_b = [jnp.concatenate([p.attn_bias[:D], gap, p.attn_bias[D:]]).astype(WIDE)[None] for p in (enc, dec)]
+    return jnp.stack(rows).astype(WIDE), attn_b, [p.fc_one_bias.astype(WIDE)[None] for p in (enc, dec)]
+
+
+def forward_block(value, first, keep, table, attn_b, fc_b, outs, weights, moves):
+    normed, mixed, totals, attended, middle, second, slope, active = outs
+    attn_w, proj_w, one_w, two_w = weights
+    hat, _ = whiten(value)
+    normed[...] = (hat * table[first : first + 1, :] + table[first + 1 : first + 2, :]).astype(NARROW)
     moves[0].wait()
-    for k in range(3 * D // D):
+    for k in range(3):
         at = slice(k * D, (k + 1) * D)
         mixed[:, at] = (matmul(normed[...], attn_w[:, at]) + attn_b[0:1, at]).astype(NARROW)
-    sides = side_masks(stream.shape[0])
+    sides = side_masks(value.shape[0])
     for pair in range(HEADS // 2):
         q, k, v = (mixed[:, part * D + pair * LANES : part * D + (pair + 1) * LANES] for part in range(3))
         found = None
         for i, side in enumerate(sides):
             scores = matmul_turned(one_side(q, side), k) * SCALE
-            if masked:
+            if keep is not None:
                 scores = jnp.where(keep[0:1, :] > 0.0, scores, -1e30)
             top = jnp.max(scores, -1, keepdims=True)
             powers = jnp.exp(scores - top)
@@ -828,10 +850,10 @@
             found = part if found is None else found + part
         attended[:, pair * LANES : (pair + 1) * LANES] = found.astype(NARROW)
     moves[1].wait()
-    value = stream[...] + matmul(attended[...], proj_w[...]) + wide_b[4:5, :]
+    value = value + matmul(attended[...], proj_w[...]) + table[first + 4 : first + 5, :]
     middle[...] = value
     hat, _ = whiten(value)
-    second[...] = (hat * wide_b[2:3, :] + wide_b[3:4, :]).astype(NARROW)
+    second[...] = (hat * table[first + 2 : first + 3, :] + table[first + 3 : first + 4, :]).astype(NARROW)
     moves[2].wait()
     for k in range(MLP // PART):
         at = slice(k * PART, (k + 1) * PART)
@@ -840,52 +862,98 @@
         active[:, at] = (value * share).astype(NARROW)
         slope[:, at] = share + value * (PDF * jnp.exp(-0.5 * value * value))
     moves[3].wait()
-    output[...] = middle[...] + matmul(active[...], two_w[...]) + wide_b[5:6, :]
-
-
-def block_vectors(p):
-    rows = (p.norm_one_gain, p.norm_one_shift, p.norm_two_gain, p.norm_two_shift, p.proj_bias, p.fc_two_bias)
-    wide_b = jnp.stack(rows + rows[:2]).astype(WIDE)
-    attn_b = jnp.concatenate([p.attn_bias[:D], jnp.zeros((D,), NARROW), p.attn_bias[D:]]).astype(WIDE)[None]
-    return wide_b, attn_b, p.fc_one_bias.astype(WIDE)[None]
-
-
-VMEM = pl.BlockSpec(memory_space=pltpu.VMEM)
-BLOCK_WEIGHTS = ((D, 3 * D), (D, D), (D, MLP), (MLP, D))
-
-
-def block_cost(length, passes):
-    weights = sum(math.prod(s) for s in BLOCK_WEIGHTS)
-    return pl.CostEstimate(flops=2 * passes * length * weights, bytes_accessed=2 * weights + 36 * length * D, transcendentals=4 * length * MLP)
-
-
-def block_forward(stream, keep, p):
-    length = stream.shape[0]
-    shapes = [(D, NARROW), (3 * D, NARROW), (LANES, WIDE), (D, NARROW), (D, WIDE), (D, NARROW), (MLP, WIDE), (MLP, NARROW), (D, WIDE)]
-    row = jnp.ones((1, length), WIDE) if keep is None else keep.astype(WIDE)[None]
-    vectors = block_vectors(p)
+    return middle[...] + matmul(active[...], two_w[...]) + table[first + 5 : first + 6, :]
+
+
+def forward_shapes(length):
+    widths = [(D, NARROW), (3 * D, NARROW), (LANES, WIDE), (D, NARROW), (D, WIDE), (D, NARROW), (MLP, WIDE), (MLP, NARROW)]
+    return [jax.ShapeDtypeStruct((length, w), t) for w, t in widths]
+
+
+def encode_kernel(latents, keep_row, keep_column, table, attn_b, fc_b, embed_w, enc_pos, dec_pos, *refs):
+    sources, outs, (stream, encoded, leaving, before) = refs[:5], refs[5:13], refs[13:17]
+    held, sem = refs[17:22], refs[22]
+    moves = start_all(sources, held, sem)
+    pos = enc_pos[...].astype(WIDE)
+    stream[:BUF, :] = table[CLASS : CLASS + 1, :] + pos[:BUF]
+    stream[BUF:, :] = matmul(latents[...], embed_w[...]) + table[EMBED_B : EMBED_B + 1, :] + pos[BUF:]
+    value = forward_block(stream[...], ENC_ROWS, keep_row, table, attn_b, fc_b, outs, held[:4], moves)
+    leaving[...] = value
+    hat, _ = whiten(value)
+    encoded[...] = (hat * table[ENC_G : ENC_G + 1, :] + table[ENC_S : ENC_S + 1, :]).astype(NARROW)
+    moves[4].wait()
+    value = matmul(encoded[...], held[4][...]) + table[DEC_B : DEC_B + 1, :]
+    value = jnp.where(keep_column[...] > 0.0, value, table[MASK_T : MASK_T + 1, :])
+    before[...] = value + dec_pos[...].astype(WIDE)
+
+
+def block_cost(length, weights):
+    work = sum(math.prod(s) for s in weights)
+    return pl.CostEstimate(flops=2 * length * work, bytes_accessed=2 * work + 36 * length * D, transcendentals=4 * length * MLP)
+
+
+def encode(latents, keep_row, keep_column, table, attn_b, fc_b, base, enc, mid):
+    length = BUF + SEQ
+    weights = BLOCK_WEIGHTS + ((D, D),)
     found = pl.pallas_call(
-        functools.partial(forward_kernel, keep is not None),
-        out_shape=[jax.ShapeDtypeStruct((length, w), t) for w, t in shapes],
-        in_specs=[VMEM] * 5 + [ANY] * 4,
-        out_specs=[VMEM] * len(shapes),
+        encode_kernel,
+        out_shape=forward_shapes(length)
+        + [jax.ShapeDtypeStruct((length, D), t) for t in (WIDE, NARROW, WIDE, WIDE)],
+        in_specs=[VMEM] * 9 + [HBM] * 5,
+        out_specs=[VMEM] * 12,
+        scratch_shapes=[pltpu.VMEM(s, NARROW) for s in weights] + [DMA((5,))],
+        compiler_params=BIG,
+        cost_estimate=block_cost(length, weights),
+    )(
+        latents, keep_row, keep_column, table, attn_b, fc_b, base.embed_weight, base.encoder_pos, mid.decoder_pos,
+        enc.attn_weight, enc.proj_weight, enc.fc_one_weight, enc.fc_two_weight, mid.dec_weight,
+    )
+    return found[:8], found[8:]
+
+
+def decode_kernel(before, route, extra, table, attn_b, fc_b, diff_pos, *refs):
+    sources, outs, (flow_out, payload) = refs[:4], refs[4:12], refs[12:14]
+    held, sem = refs[14:18], refs[18]
+    moves = start_all(sources, held, sem)
+    value = forward_block(before[...], DEC_ROWS, None, table, attn_b, fc_b, outs, held, moves)
+    flow_out[...] = value
+    hat, _ = whiten(flow_out[BUF:, :])
+    value = hat * table[DEC_G : DEC_G + 1, :] + table[DEC_S : DEC_S + 1, :]
+    conditions = (value + diff_pos[...].astype(WIDE)).astype(NARROW)
+    slots = payload.shape[0]
+    picks = lax.broadcasted_iota(jnp.int32, (slots, slots), 0) == route[...]
+    picks = jnp.where(picks, 1.0, 0.0).astype(NARROW)
+    payload[:, :D] = matmul(picks, conditions).astype(NARROW)
+    payload[:, D:] = matmul(picks, extra[...]).astype(NARROW)
+
+
+def decode(before, route, extra, table, attn_b, fc_b, dec, head):
+    length = BUF + SEQ
+    found = pl.pallas_call(
+        decode_kernel,
+        out_shape=forward_shapes(length)
+        + [jax.ShapeDtypeStruct((length, D), WIDE), jax.ShapeDtypeStruct((SEQ, D + LANES), NARROW)],
+        in_specs=[VMEM] * 7 + [HBM] * 4,
+        out_specs=[VMEM] * 10,
         scratch_shapes=[pltpu.VMEM(s, NARROW) for s in BLOCK_WEIGHTS] + [DMA((4,))],
-        compiler_params=pltpu.CompilerParams(vmem_limit_bytes=60 * 1000 * 1000),
-        cost_estimate=block_cost(length, 1),
-    )(stream, row, *vectors, p.attn_weight, p.proj_weight, p.fc_one_weight, p.fc_two_weight)
-    return found[-1], (stream, row, vectors[0]) + tuple(found[:-1])
-
-
-def backward_kernel(masked, grad_out, stream, keep, wide_b, mixed, totals, middle, *refs):
-    slope_in = refs[4]
-    out_low, inner_low, middle_low, mixed_low, stream_grad, sums, one_sum, mixed_sum = refs[5:13]
-    attn_w, proj_w, one_w, two_w, slope, attended_grad, sem = refs[13:]
-    attn_src, proj_src, one_src, two_src = refs[:4]
-    moves = start_all((two_src, slope_in, one_src, proj_src, attn_src), (two_w, slope, one_w, proj_w, attn_w), sem)
-    value = grad_out[...]
+        compiler_params=BIG,
+        cost_estimate=block_cost(length, BLOCK_WEIGHTS),
+    )(
+        before, route[None], extra, table, attn_b, fc_b, head.diffusion_pos,
+        dec.attn_weight, dec.proj_weight, dec.fc_one_weight, dec.fc_two_weight,
+    )
+    return found[:8], found[8], found[9]
+
+
+TWO_B, G_TWO, S_TWO, PROJ_B, G_ONE, S_ONE = 0, 1, 2, 3, 4, 5
+
+
+def backward_block(value, first, stream, keep, table, mixed, totals, middle, outs, weights, slope, attended_grad, moves):
+    out_low, inner_low, middle_low, mixed_low, sums, one_sum, mixed_sum = outs
+    attn_w, proj_w, one_w, two_w = weights
     low = value.astype(NARROW)
     out_low[...] = low
-    sums[0:1, :] = column_sum(value)
+    sums[TWO_B : TWO_B + 1, :] = column_sum(value)
     moves[0].wait()
     moves[1].wait()
     for k in range(MLP // PART):
@@ -896,15 +964,14 @@
     moves[2].wait()
     part = matmul_turned(inner_low[...], one_w[...])
     hat, r = whiten(middle[...])
-    sums[1:2, :] = column_sum(part * hat)
-    sums[2:3, :] = column_sum(part)
-    value = value + whiten_back(part * wide_b[2:3, :], hat, r)
-    stream_grad[...] = value
-    sums[3:4, :] = column_sum(value)
+    sums[G_TWO : G_TWO + 1, :] = column_sum(part * hat)
+    sums[S_TWO : S_TWO + 1, :] = column_sum(part)
+    value = value + whiten_back(part * table[first + 2 : first + 3, :], hat, r)
+    sums[PROJ_B : PROJ_B + 1, :] = column_sum(value)
     middle_low[...] = value.astype(NARROW)
     moves[3].wait()
     attended_grad[...] = matmul_turned(middle_low[...], proj_w[...]).astype(NARROW)
-    sides = side_masks(stream.shape[0])
+    sides = side_masks(value.shape[0])
     for pair in range(HEADS // 2):
         here = [slice(part * D + pair * LANES, part * D + (pair + 1) * LANES) for part in range(3)]
         q, k, v = (mixed[:, at] for at in here)
@@ -913,7 +980,7 @@
         for i, side in enumerate(sides):
             q_side, k_side, g_side = one_side(q, side), one_side(k, side), one_side(g, side)
             scores = matmul_turned(q_side, k) * SCALE
-            if masked:
+            if keep is not None:
                 scores = jnp.where(keep[0:1, :] > 0.0, scores, -1e30)
             probs = jnp.exp(scores - totals[:, 2 * pair + i : 2 * pair + i + 1])
             prob_grad = matmul_turned(g_side, v)
@@ -928,33 +995,312 @@
     moves[4].wait()
     part = matmul_turned(mixed_low[...], attn_w[...])
     hat, r = whiten(stream[...])
-    sums[4:5, :] = column_sum(part * hat)
-    sums[5:6, :] = column_sum(part)
-    stream_grad[...] = stream_grad[...] + whiten_back(part * wide_b[0:1, :], hat, r)
-
-
-def block_backward(grad_out, keep, p, saved):
-    stream, row, wide_b, normed, mixed, totals, attended, middle, second, slope, active = saved
-    length = stream.shape[0]
-    shapes = [((length, D), NARROW), ((length, MLP), NARROW), ((length, D), NARROW), ((length, 3 * D), NARROW), ((length, D), WIDE)]
-    shapes += [((8, D), WIDE), ((1, MLP), WIDE), ((1, 3 * D), WIDE)]
-    out_low, inner_low, middle_low, mixed_low, stream_grad, sums, one_sum, mixed_sum = pl.pallas_call(
-        functools.partial(backward_kernel, keep is not None),
-        out_shape=[jax.ShapeDtypeStruct(s, t) for s, t in shapes],
-        in_specs=[VMEM] * 7 + [ANY] * 5,
-        out_specs=[VMEM] * len(shapes),
-        scratch_shapes=[pltpu.VMEM(s, NARROW) for s in BLOCK_WEIGHTS]
-        + [pltpu.VMEM((length, MLP), WIDE), pltpu.VMEM((length, D), NARROW), DMA((5,))],
-        compiler_params=pltpu.CompilerParams(vmem_limit_bytes=60 * 1000 * 1000),
-        cost_estimate=block_cost(length, 1),
-    )(grad_out, stream, row, wide_b, mixed, totals, middle, p.attn_weight, p.proj_weight, p.fc_one_weight, p.fc_two_weight, slope)
+    sums[G_ONE : G_ONE + 1, :] = column_sum(part * hat)
+    sums[S_ONE : S_ONE + 1, :] = column_sum(part)
+    return value + whiten_back(part * table[first : first + 1, :], hat, r)
+
+
+def backward_shapes(length, rows):
+    shapes = [((length, D), NARROW), ((length, MLP), NARROW), ((length, D), NARROW), ((length, 3 * D), NARROW)]
+    shapes += [((rows, D), WIDE), ((1, MLP), WIDE), ((1, 3 * D), WIDE)]
+    return [jax.ShapeDtypeStruct(s, t) for s, t in shapes]
+
+
+def backward_scratch(length, weights):
+    return [pltpu.VMEM(s, NARROW) for s in weights] + [
+        pltpu.VMEM((length, MLP), WIDE), pltpu.VMEM((length, D), NARROW), DMA((len(weights) + 1,))
+    ]
+
+
+MORE = 6
+
+
+def decode_back_kernel(returned, route, flow_out, before, leaving, keep_column, table, mixed, totals, middle, *refs):
+    slope_src, attn_src, proj_src, one_src, two_src, dec_src = refs[:6]
+    outs, (token_grad, before_grad, decoded_low, leaving_grad) = refs[6:13], refs[13:17]
+    attn_w, proj_w, one_w, two_w, dec_w, slope, attended_grad, sem = refs[17:]
+    moves = start_all(
+        (two_src, slope_src, one_src, proj_src, attn_src, dec_src), (two_w, slope, one_w, proj_w, attn_w, dec_w), sem
+    )
+    slots = returned.shape[0]
+    picks = lax.broadcasted_iota(jnp.int32, (slots, slots), 1) == route[...]
+    picks = jnp.where(picks, 1.0, 0.0).astype(NARROW)
+    grad = matmul(picks, returned[...])
+    token_grad[...] = grad
+    sums = outs[4]
+    hat, r = whiten(flow_out[BUF:, :])
+    sums[MORE : MORE + 1, :] = column_sum(grad * hat)
+    sums[MORE + 1 : MORE + 2, :] = column_sum(grad)
+    before_grad[:BUF, :] = jnp.zeros((BUF, D), WIDE)
+    before_grad[BUF:, :] = whiten_back(grad * table[DEC_G : DEC_G + 1, :], hat, r)
+    value = backward_block(
+        before_grad[...], DEC_ROWS, before, None, table, mixed, totals, middle, outs,
+        (attn_w, proj_w, one_w, two_w), slope, attended_grad, moves,
+    )
+    before_grad[...] = value
+    kept = jnp.where(keep_column[...] > 0.0, value, 0.0)
+    sums[MORE + 2 : MORE + 3, :] = column_sum(kept)
+    sums[MORE + 3 : MORE + 4, :] = column_sum(value - kept)
+    decoded_low[...] = kept.astype(NARROW)
+    moves[5].wait()
+    part = matmul_turned(decoded_low[...], dec_w[...])
+    hat, r = whiten(leaving[...])
+    sums[MORE + 4 : MORE + 5, :] = column_sum(part * hat)
+    sums[MORE + 5 : MORE + 6, :] = column_sum(part)
+    leaving_grad[...] = whiten_back(part * table[ENC_G : ENC_G + 1, :], hat, r)
+
+
+def decode_back(returned, route, flow_out, before, leaving, keep_column, table, stored, dec, mid):
+    length = BUF + SEQ
+    weights = BLOCK_WEIGHTS + ((D, D),)
+    normed, mixed, totals, attended, middle, second, slope, active = stored
+    found = pl.pallas_call(
+        decode_back_kernel,
+        out_shape=backward_shapes(length, 16)
+        + [jax.ShapeDtypeStruct((n, D), t) for n, t in ((SEQ, WIDE), (length, WIDE), (length, NARROW), (length, WIDE))],
+        in_specs=[VMEM] * 10 + [HBM] * 6,
+        out_specs=[VMEM] * 11,
+        scratch_shapes=backward_scratch(length, weights),
+        compiler_params=BIG,
+        cost_estimate=block_cost(length, weights),
+    )(
+        returned, route[:, None], flow_out, before, leaving, keep_column, table, mixed, totals, middle,
+        slope, dec.attn_weight, dec.proj_weight, dec.fc_one_weight, dec.fc_two_weight, mid.dec_weight,
+    )
+    return found[:7], found[7:]
+
+
+def encode_back_kernel(leaving_grad, latents, stream, keep_row, table, mixed, totals, middle, *refs):
+    slope_src, attn_src, proj_src, one_src, two_src = refs[:5]
+    outs, (stream_grad, embed_grad) = refs[5:12], refs[12:14]
+    attn_w, proj_w, one_w, two_w, slope, attended_grad, sem = refs[14:]
+    moves = start_all((two_src, slope_src, one_src, proj_src, attn_src), (two_w, slope, one_w, proj_w, attn_w), sem)
+    value = backward_block(
+        leaving_grad[...], ENC_ROWS, stream, keep_row, table, mixed, totals, middle, outs,
+        (attn_w, proj_w, one_w, two_w), slope, attended_grad, moves,
+    )
+    stream_grad[...] = value
+    sums = outs[4]
+    sums[MORE : MORE + 1, :] = column_sum(stream_grad[:BUF, :])
+    tokens = stream_grad[BUF:, :]
+    sums[MORE + 1 : MORE + 2, :] = column_sum(tokens)
+    embed_grad[...] = lax.dot_general(latents[...], tokens.astype(NARROW), (((0,), (0,)), ((), ())), preferred_element_type=WIDE)
+
+
+def encode_back(leaving_grad, latents, stream, keep_row, table, stored, enc):
+    length = BUF + SEQ
+    normed, mixed, totals, attended, middle, second, slope, active = stored
+    found = pl.pallas_call(
+        encode_back_kernel,
+        out_shape=backward_shapes(length, 8)
+        + [jax.ShapeDtypeStruct((n, D), WIDE) for n in (length, TOK_CH)],
+        in_specs=[VMEM] * 8 + [HBM] * 5,
+        out_specs=[VMEM] * 9,
+        scratch_shapes=backward_scratch(length, BLOCK_WEIGHTS),
+        compiler_params=BIG,
+        cost_estimate=block_cost(length, BLOCK_WEIGHTS),
+    )(
+        leaving_grad, latents, stream, keep_row, table, mixed, totals, middle,
+        slope, enc.attn_weight, enc.proj_weight, enc.fc_one_weight, enc.fc_two_weight,
+    )
+    return found[:7], found[7:]
+
+
+class Vector:
+    def __init__(self, array, *parts):
+        self.array, self.parts = array, parts
+
+
+def block_grads(stored, found):
+    normed, mixed, totals, attended, middle, second, slope, active = stored
+    out_low, inner_low, middle_low, mixed_low, sums, one_sum, mixed_sum = found
+
+    def row(k):
+        return Vector(sums, (k, 0, D))
+
+    return dict(
+        norm_one_gain=row(G_ONE), norm_one_shift=row(S_ONE), attn_weight=(normed, mixed_low),
+        attn_bias=Vector(mixed_sum, (0, 0, D), (0, 2 * D, D)), proj_weight=(attended, middle_low), proj_bias=row(PROJ_B),
+        norm_two_gain=row(G_TWO), norm_two_shift=row(S_TWO), fc_one_weight=(second, inner_low),
+        fc_one_bias=Vector(one_sum, (0, 0, MLP)), fc_two_weight=(active, out_low), fc_two_bias=row(TWO_B),
+    )
+
+
+SUMS = 9
+
+
+def eighths(value):
+    found = value[:8]
+    for k in range(8, value.shape[0], 8):
+        found = found + value[k : k + 8]
+    return found
+
+
+def sigmoid(value):
+    return 0.5 + 0.5 * jnp.tanh(0.5 * value)
+
+
+def silu_and_slope(value):
+    s = sigmoid(value)
+    silu = value * s
+    return silu, s + silu * (1.0 - s)
+
+
+def turned_matmul(left, right):
+    return lax.dot_general(left, right, (((0,), (0,)), ((), ())), preferred_element_type=WIDE)
+
+
+def head_kernel(
+    divisor, arrived, features, levels, noise, input_w, final_w, wide_b, ada_b, final_b,
+    cond_src, time_src, ada_src, inner_src, outer_src,
+    signal, mod_low, modulated, inner_low, active, outer_low, joined_low, cond_low, cond_back, wide_sums, final_grad, input_grad, last,
+    cond, joined, hidden, mod, hat, inner, outer, top, total, sums, cond_w, time_w, ada_w, inner_w, outer_w, weight_sem,
+):
+    step = pl.program_id(0)
+    sources, held = (cond_src, time_src, ada_src, inner_src, outer_src), (cond_w, time_w, ada_w, inner_w, outer_w)
+    moves = [pltpu.make_async_copy(s, t, weight_sem.at[i]) for i, (s, t) in enumerate(zip(sources, held))]
+
+    def need(*which):
+        @pl.when(step == 0)
+        def _():
+            for i in which:
+                moves[i].wait()
+
+    def bias(k):
+        return wide_b[k : k + 1, :]
+
+    def add_sum(k, value):
+        sums[k * 8 : (k + 1) * 8, :] = sums[k * 8 : (k + 1) * 8, :] + eighths(value)
+
+    @pl.when(step == 0)
+    def _():
+        for move in moves:
+            move.start()
+        for ref in (sums, total, final_grad, input_grad, last):
+            ref[...] = jnp.zeros_like(ref)
+        moves[0].wait()
+        moves[1].wait()
+        cond[...] = matmul(arrived[:, :D], cond_w[...]) + bias(0)
+
+    clean = arrived[:, D : D + TOK_CH].astype(WIDE)
+    marks = arrived[:, D + TOK_CH : D + TOK_CH + 1].astype(WIDE)
+    noisy = (levels[:, 0:1] * clean + levels[:, 1:2] * noise[...]).astype(NARROW)
+    value, slope = silu_and_slope(matmul(features[...], time_w[...]) + bias(1) + cond[...])
+    joined[...] = slope
+    signal[...] = value.astype(NARROW)
+    h = matmul(noisy, input_w[...]) + bias(2)
+    hidden[...] = h
+    value, first_r = whiten(h)
+    hat[...] = value
+    need(2, 3, 4)
+    mod[...] = matmul(signal[...], ada_w[...])
+    normed = hat[...] * bias(3) + bias(4)
+    scale = 1.0 + (mod[:, HW : 2 * HW] + ada_b[0:1, HW : 2 * HW])
+    modulated[...] = (normed * scale + (mod[:, :HW] + ada_b[0:1, :HW])).astype(NARROW)
+    mod[:, HW : 2 * HW] = scale
+    value, slope = silu_and_slope(matmul(modulated[...], inner_w[...]) + bias(5))
+    inner[...] = slope
+    active[...] = value.astype(NARROW)
+    out = matmul(active[...], outer_w[...]) + bias(6)
+    outer[...] = out
+    gate = mod[:, 2 * HW :] + ada_b[0:1, 2 * HW :]
+    mod[:, 2 * HW :] = gate
+    value, r = whiten(hidden[...] + gate * out)
+    top[...] = value
+    final = value.astype(NARROW)
+    error = matmul(final, final_w[...]) + final_b[0:1, :] - noise[...]
+    pred_grad = 2.0 * error * marks / divisor[0]
+    pred_low = pred_grad.astype(NARROW)
+    last[0:1, :TOK_CH] = last[0:1, :TOK_CH] + column_sum(pred_grad)
+    last[1:2, 0:1] = last[1:2, 0:1] + column_sum(jnp.sum(error * error, -1, keepdims=True) * marks)
+    final_grad[...] = final_grad[...] + turned_matmul(final, pred_low)
+    g = whiten_back(matmul_turned(pred_low, final_w[...]), top[...], r)
+    hidden[...] = g
+    gate_grad = g * outer[...]
+    mod_low[:, 2 * HW :] = gate_grad.astype(NARROW)
+    add_sum(0, gate_grad)
+    out_grad = g * mod[:, 2 * HW :]
+    outer_low[...] = out_grad.astype(NARROW)
+    add_sum(1, out_grad)
+    g = matmul_turned(outer_low[...], outer_w[...]) * inner[...]
+    inner_low[...] = g.astype(NARROW)
+    add_sum(2, g)
+    g = matmul_turned(inner_low[...], inner_w[...])
+    value = hat[...]
+    mod_low[:, :HW] = g.astype(NARROW)
+    add_sum(3, g)
+    scale_grad = g * (value * bias(3) + bias(4))
+    mod_low[:, HW : 2 * HW] = scale_grad.astype(NARROW)
+    add_sum(4, scale_grad)
+    g = g * mod[:, HW : 2 * HW]
+    add_sum(5, g)
+    add_sum(6, g * value)
+    g = hidden[...] + whiten_back(g * bias(3), value, first_r)
+    add_sum(7, g)
+    input_grad[...] = input_grad[...] + turned_matmul(noisy, g.astype(NARROW))
+    g = matmul_turned(mod_low[...], ada_w[...]) * joined[...]
+    joined_low[...] = g.astype(NARROW)
+    add_sum(8, g)
+    total[...] = total[...] + g
+
+    @pl.when(step == pl.num_programs(0) - 1)
+    def _():
+        found = total[...].astype(NARROW)
+        cond_low[...] = found
+        cond_back[...] = matmul_turned(found, cond_w[...]).astype(NARROW)
+        for k in range(SUMS):
+            wide_sums[k : k + 1, :] = column_sum(sums[k * 8 : (k + 1) * 8, :])
+
+
+def head_pass(p, arrived, steps, noise, divisor):
+    slots = arrived.shape[0]
+    times = steps.astype(WIDE)
+    features = time_features(times).astype(NARROW).reshape(-1, FREQ)
+    level = alpha_level(times).reshape(-1, 1)
+    levels = jnp.concatenate([jnp.sqrt(level), jnp.sqrt(1.0 - level)], 1)
+    flat_noise = noise.reshape(-1, TOK_CH)
+    wide_b = jnp.stack(
+        [p.cond_bias, p.time_bias, p.input_bias, p.head_gain, p.head_shift, p.inner_bias, p.outer_bias, p.outer_bias]
+    ).astype(WIDE)
+    total = COPIES * slots
+
+    def tiled(width):
+        return pl.BlockSpec((slots, width), lambda i: (i, 0))
+
+    def whole(x):
+        return pl.BlockSpec(x, lambda i: (0, 0), pipeline_mode=pl.Buffered(1))
+
+    weights = (p.cond_weight, p.time_weight, p.ada_weight, p.inner_weight, p.outer_weight)
+    small = (p.input_weight, p.final_weight, wide_b, p.ada_bias.astype(WIDE)[None], p.final_bias.astype(WIDE)[None])
+    kept = [((total, w), NARROW, tiled(w)) for w in (HW, 3 * HW, HW, HW, HW, HW, HW)]
+    once = (((slots, HW), NARROW), ((slots, D), NARROW), ((16, HW), WIDE), ((HW, TOK_CH), WIDE), ((TOK_CH, HW), WIDE), ((8, LANES), WIDE))
+    kept += [(s, t, whole(s)) for s, t in once]
+    flops = 4 * total * (FREQ * HW // 2 + 5 * HW * HW) + 4 * slots * D * HW
+    found = pl.pallas_call(
+        head_kernel,
+        grid=(COPIES,),
+        out_shape=[jax.ShapeDtypeStruct(s, t) for s, t, _ in kept],
+        in_specs=[pl.BlockSpec(memory_space=pltpu.SMEM), whole(arrived.shape), tiled(FREQ), tiled(2), tiled(TOK_CH)]
+        + [whole(x.shape) for x in small] + [HBM] * len(weights),
+        out_specs=[spec for _, _, spec in kept],
+        scratch_shapes=[pltpu.VMEM((slots, w), WIDE) for w in (HW, HW, HW, 3 * HW, HW, HW, HW, HW, HW)]
+        + [pltpu.VMEM((SUMS * 8, HW), WIDE)] + [pltpu.VMEM(x.shape, NARROW) for x in weights] + [DMA((len(weights),))],
+        compiler_params=BIG,
+        cost_estimate=pl.CostEstimate(flops=flops, bytes_accessed=26 * total * HW, transcendentals=3 * total * HW),
+    )(divisor[None], arrived, features, levels, flat_noise, *small, *weights)
+    signal, mod_low, modulated, inner_low, active, outer_low, joined_low, cond_low, cond_back, sums, final_grad, input_grad, last = found
+
+    def row(k):
+        return Vector(sums, (k, 0, HW))
+
     grads = dict(
-        norm_one_gain=sums[4], norm_one_shift=sums[5], attn_weight=weight_grad(normed, mixed_low),
-        attn_bias=jnp.concatenate([mixed_sum[0, :D], mixed_sum[0, 2 * D :]]), proj_weight=weight_grad(attended, middle_low),
-        proj_bias=sums[3], norm_two_gain=sums[1], norm_two_shift=sums[2], fc_one_weight=weight_grad(second, inner_low),
-        fc_one_bias=one_sum[0], fc_two_weight=weight_grad(active, out_low), fc_two_bias=sums[0],
+        final_weight=final_grad, final_bias=Vector(last, (0, 0, LANES)),
+        outer_weight=(active, outer_low), outer_bias=row(1), inner_weight=(modulated, inner_low), inner_bias=row(2),
+        head_gain=row(6), head_shift=row(5), ada_weight=(signal, mod_low),
+        ada_bias=Vector(sums, (3, 0, HW), (4, 0, HW), (0, 0, HW)), time_weight=(features, joined_low), time_bias=row(8),
+        cond_weight=(arrived, cond_low), cond_bias=row(8), input_weight=input_grad, input_bias=row(7),
     )
-    return stream_grad, grads
+    return last[1, 0], grads, cond_back
 
 
 def time_features(times):
@@ -967,240 +1313,6 @@
 def alpha_level(times):
     start = math.cos(0.008 / 1.008 * math.pi / 2) ** 2
     return jnp.cos(((times + 1.0) / STEPS_T + 0.008) / 1.008 * math.pi / 2) ** 2 / start
-
-
-ROWS = 256
-TOGETHER = 1
-SUMS = 9
-
-
-def matmul(left, right):
-    return jnp.dot(left, right, preferred_element_type=WIDE)
-
-
-def matmul_turned(left, right):
-    return lax.dot_general(left, right, (((1,), (1,)), ((), ())), preferred_element_type=WIDE)
-
-
-def eighths(value):
-    found = value[:8]
-    for k in range(8, value.shape[0], 8):
-        found = found + value[k : k + 8]
-    return found
-
-
-def sigmoid(value):
-    return 0.5 + 0.5 * jnp.tanh(0.5 * value)
-
-
-def silu_and_slope(value):
-    s = sigmoid(value)
-    silu = value * s
-    return silu, s + silu * (1.0 - s)
-
-
-def head_kernel(
-    divisor, conditions, features, noisy, noise, marks,
-    cond_w, time_w, input_w, ada_w, inner_w, outer_w, final_w, wide_b, ada_b, final_b,
-    signal, mod_low, modulated, inner_low, active, outer_low, final, hidden_low, joined_low, error, sums, cond_low, cond_sum, cond_back,
-    cond, joined, hidden, mod, hat, inner, outer, top, total, spread,
-):
-    step = pl.program_id(0)
-    tile = joined.shape[0]
-    count = tile // ROWS
-    slots = total.shape[0]
-    grad = hidden
-
-    def rows(i):
-        return pl.ds(pl.multiple_of(i * ROWS, ROWS), ROWS)
-
-    def loop(action, *more):
-        def one(i, carry):
-            action(rows(i), *(rows(i % (slots // ROWS)) for _ in more))
-            return carry
-
-        lax.fori_loop(0, count, one, 0)
-
-    def bias(k):
-        return wide_b[k : k + 1, :]
-
-    def add_sum(k, value):
-        sums[k * 8 : (k + 1) * 8, :] = sums[k * 8 : (k + 1) * 8, :] + eighths(value)
-
-    @pl.when(step == 0)
-    def _():
-        sums[...] = jnp.zeros_like(sums)
-        total[...] = jnp.zeros_like(total)
-        cond[...] = matmul(conditions[...], cond_w[...]) + bias(0)
-
-    joined[...] = matmul(features[...], time_w[...])
-    hidden[...] = matmul(noisy[...], input_w[...])
-
-    def enter(at, slot):
-        value, slope = silu_and_slope(joined[at, :] + bias(1) + cond[slot, :])
-        joined[at, :] = slope
-        signal[at, :] = value.astype(NARROW)
-        h = hidden[at, :] + bias(2)
-        hidden[at, :] = h
-        centered = h - jnp.mean(h, -1, keepdims=True)
-        r = lax.rsqrt(jnp.mean(centered * centered, -1, keepdims=True) + NORM_EPS)
-        spread[at, 0:1] = r
-        hat[at, :] = centered * r
-
-    loop(enter, cond)
-    mod[...] = matmul(signal[...], ada_w[...])
-
-    def modulate(at):
-        normed = hat[at, :] * bias(3) + bias(4)
-        shift = mod[at, :HW] + ada_b[0:1, :HW]
-        scale = 1.0 + (mod[at, HW : 2 * HW] + ada_b[0:1, HW : 2 * HW])
-        mod[at, HW : 2 * HW] = scale
-        modulated[at, :] = (normed * scale + shift).astype(NARROW)
-
-    loop(modulate)
-    inner[...] = matmul(modulated[...], inner_w[...])
-
-    def activate(at):
-        value, slope = silu_and_slope(inner[at, :] + bias(5))
-        inner[at, :] = slope
-        active[at, :] = value.astype(NARROW)
-
-    loop(activate)
-    outer[...] = matmul(active[...], outer_w[...])
-
-    def leave(at):
-        out = outer[at, :] + bias(6)
-        outer[at, :] = out
-        gate = mod[at, 2 * HW :] + ada_b[0:1, 2 * HW :]
-        mod[at, 2 * HW :] = gate
-        value = hidden[at, :] + gate * out
-        centered = value - jnp.mean(value, -1, keepdims=True)
-        r = lax.rsqrt(jnp.mean(centered * centered, -1, keepdims=True) + NORM_EPS)
-        spread[at, 1:2] = r
-        value = centered * r
-        top[at, :] = value
-        final[at, :] = value.astype(NARROW)
-
-    loop(leave)
-    off = matmul(final[...], final_w[...]) + final_b[0:1, :] - noise[...]
-    error[...] = off
-    pred_low = (2.0 * off * marks[...] / divisor[0]).astype(NARROW)
-    grad[...] = matmul_turned(pred_low, final_w[...])
-
-    def enter_back(at):
-        g, value = grad[at, :], top[at, :]
-        g = spread[at, 1:2] * (g - jnp.mean(g, -1, keepdims=True) - value * jnp.mean(g * value, -1, keepdims=True))
-        grad[at, :] = g
-        gate_grad = g * outer[at, :]
-        mod_low[at, 2 * HW :] = gate_grad.astype(NARROW)
-        add_sum(0, gate_grad)
-        out_grad = g * mod[at, 2 * HW :]
-        outer_low[at, :] = out_grad.astype(NARROW)
-        add_sum(1, out_grad)
-
-    loop(enter_back)
-    outer[...] = matmul_turned(outer_low[...], outer_w[...])
-
-    def activate_back(at):
-        g = outer[at, :] * inner[at, :]
-        inner_low[at, :] = g.astype(NARROW)
-        add_sum(2, g)
-
-    loop(activate_back)
-    inner[...] = matmul_turned(inner_low[...], inner_w[...])
-
-    def modulate_back(at):
-        g, value = inner[at, :], hat[at, :]
-        mod_low[at, :HW] = g.astype(NARROW)
-        add_sum(3, g)
-        scale_grad = g * (value * bias(3) + bias(4))
-        mod_low[at, HW : 2 * HW] = scale_grad.astype(NARROW)
-        add_sum(4, scale_grad)
-        g = g * mod[at, HW : 2 * HW]
-        add_sum(5, g)
-        add_sum(6, g * value)
-        g = g * bias(3)
-        g = spread[at, 0:1] * (g - jnp.mean(g, -1, keepdims=True) - value * jnp.mean(g * value, -1, keepdims=True))
-        g = grad[at, :] + g
-        hidden_low[at, :] = g.astype(NARROW)
-        add_sum(7, g)
-
-    loop(modulate_back)
-    top[...] = matmul_turned(mod_low[...], ada_w[...])
-
-    def enter_last(at, slot):
-        g = top[at, :] * joined[at, :]
-        joined_low[at, :] = g.astype(NARROW)
-        add_sum(8, g)
-        total[slot, :] = total[slot, :] + g
-
-    loop(enter_last, total)
-
-    @pl.when(step == pl.num_programs(0) - 1)
-    def _():
-        found = total[...].astype(NARROW)
-        cond_low[...] = found
-        cond_back[...] = matmul_turned(found, cond_w[...]).astype(NARROW)
-        acc = jnp.zeros((8, HW), WIDE)
-        for i in range(slots // 8):
-            acc = acc + total[i * 8 : (i + 1) * 8, :]
-        cond_sum[...] = acc
-
-
-def head_pass(p, conditions, clean, filled, steps, noise, divisor):
-    slots = conditions.shape[0]
-    times = steps.astype(WIDE)
-    features = time_features(times).astype(NARROW).reshape(-1, FREQ)
-    level = alpha_level(times)[..., None]
-    noisy = (jnp.sqrt(level) * clean.astype(WIDE) + jnp.sqrt(1.0 - level) * noise).astype(NARROW).reshape(-1, TOK_CH)
-    flat_noise = noise.reshape(-1, TOK_CH)
-    marks = jnp.tile(filled.astype(WIDE)[:, None], (COPIES, 1))
-    wide_b = jnp.stack(
-        [p.cond_bias, p.time_bias, p.input_bias, p.head_gain, p.head_shift, p.inner_bias, p.outer_bias, p.outer_bias]
-    ).astype(WIDE)
-    total = COPIES * slots
-
-    def tiled(width):
-        return pl.BlockSpec((TOGETHER * slots, width), lambda i: (i, 0))
-
-    def whole(x):
-        return pl.BlockSpec(x, lambda i: (0, 0), pipeline_mode=pl.Buffered(1))
-
-    weights = (p.cond_weight, p.time_weight, p.input_weight, p.ada_weight, p.inner_weight, p.outer_weight, p.final_weight)
-    biases = (wide_b, p.ada_bias.astype(WIDE)[None], p.final_bias.astype(WIDE)[None])
-    widths = (HW, 3 * HW, HW, HW, HW, HW, HW, HW, HW)
-    kept = [((total, w), NARROW, tiled(w)) for w in widths] + [((total, TOK_CH), WIDE, tiled(TOK_CH))]
-    kept += [(s, t, whole(s)) for s, t in (((SUMS * 8, HW), WIDE), ((slots, HW), NARROW), ((8, HW), WIDE), ((slots, D), NARROW))]
-    flops = 4 * total * (FREQ * HW // 2 + 5 * HW * HW) + 4 * slots * D * HW
-    found = pl.pallas_call(
-        head_kernel,
-        grid=(COPIES // TOGETHER,),
-        out_shape=[jax.ShapeDtypeStruct(s, t) for s, t, _ in kept],
-        in_specs=[pl.BlockSpec(memory_space=pltpu.SMEM), whole(conditions.shape), tiled(FREQ), tiled(TOK_CH), tiled(TOK_CH), tiled(1)]
-        + [whole(x.shape) for x in weights + biases],
-        out_specs=[spec for _, _, spec in kept],
-        scratch_shapes=[
-            pltpu.VMEM((n * slots, w), WIDE)
-            for n, w in [(1, HW)] + [(TOGETHER, w) for w in (HW, HW, 3 * HW, HW, HW, HW, HW)] + [(1, HW), (TOGETHER, LANES)]
-        ],
-        compiler_params=pltpu.CompilerParams(vmem_limit_bytes=60 * 1000 * 1000),
-        cost_estimate=pl.CostEstimate(flops=flops, bytes_accessed=26 * total * HW, transcendentals=3 * total * HW),
-    )(divisor[None], conditions, features, noisy, flat_noise, marks, *weights, *biases)
-    signal, mod_low, modulated, inner_low, active, outer_low, final, hidden_low, joined_low, error, sums, cond_low, cond_sum, cond_back = found
-    sums = jnp.sum(sums.reshape(SUMS, 8, HW), 1)
-    loss_part = jnp.sum(jnp.sum(error * error, -1) * marks[:, 0])
-    pred_grad = 2.0 * error * marks / divisor
-    grads = dict(
-        final_weight=weight_grad(final, pred_grad.astype(NARROW)), final_bias=rows_sum(pred_grad),
-        outer_weight=weight_grad(active, outer_low), outer_bias=sums[1],
-        inner_weight=weight_grad(modulated, inner_low), inner_bias=sums[2],
-        head_gain=sums[6], head_shift=sums[5],
-        ada_weight=weight_grad(signal, mod_low), ada_bias=jnp.concatenate([sums[3], sums[4], sums[0]]),
-        time_weight=weight_grad(features, joined_low), time_bias=sums[8],
-        cond_weight=weight_grad(conditions, cond_low), cond_bias=rows_sum(cond_sum),
-        input_weight=weight_grad(noisy, hidden_low), input_bias=sums[7],
-    )
-    return loss_part, grads, cond_back
 
 
 def exchange(payload, parts):
@@ -1221,58 +1333,47 @@
     masked = route < rows
     own = jnp.sum(masked.astype(WIDE))
     low = weights.reshape(size, LANES).astype(NARROW)
-    extra = jnp.full((padded - size, LANES), own).astype(NARROW)
-    block = jnp.concatenate([low, extra], 0)
+    block = jnp.concatenate([low, jnp.full((padded - size, LANES), own).astype(NARROW)], 0)
     gathered = spread(block) if meshed else lax.all_gather(block, BOTH, axis=0)
-    base, enc, mid, dec, head = unpack(gathered, size)
+    base, enc, mid, dec, head = groups = [types.SimpleNamespace() for _ in GROUPS]
+    unpack(gathered, size, groups)
     count = jnp.sum(gathered[:, size, 0].astype(WIDE))
-    keep = jnp.concatenate([jnp.ones((BUF,), bool), ~masked])
-    tokens = dense(latents, base.embed_weight) + base.embed_bias.astype(WIDE)
+    keep = jnp.concatenate([jnp.ones((BUF,), WIDE), 1.0 - masked.astype(WIDE)])
+    keep_row, keep_column = keep[None], keep[:, None]
     at = next(e.start for e in ENTRIES if e.sparse) + labels[0] * (D // LANES) + jnp.arange(D // LANES, dtype=jnp.int32)
-    classes = gathered[at // size, at % size].reshape(1, D).astype(WIDE)
-    stream = jnp.concatenate([jnp.broadcast_to(classes, (BUF, D)), tokens], 0) + base.encoder_pos.astype(WIDE)
-    stream, enc_stored = block_forward(stream, keep, enc)
-    encoded = layer_norm(stream, mid.enc_gain.astype(WIDE), mid.enc_shift.astype(WIDE)).astype(NARROW)
-    decoded = dense(encoded, mid.dec_weight) + mid.dec_bias.astype(WIDE)
-    decoded = jnp.where(keep[:, None], decoded, mid.mask_token.astype(WIDE))
-    before = decoded + mid.decoder_pos.astype(WIDE)
-    flow_out, dec_stored = block_forward(before, None, dec)
-    after = layer_norm(flow_out, head.dec_gain.astype(WIDE), head.dec_shift.astype(WIDE))
-    conditions = (after[BUF:] + head.diffusion_pos.astype(WIDE)).astype(NARROW)
+    classes = gathered[at // size, at % size].reshape(D)
+    table, attn_b, fc_b = block_vectors(base, enc, mid, dec, head, classes)
+    enc_stored, (stream, encoded, leaving, before) = encode(
+        latents, keep_row, keep_column, table, attn_b[0], fc_b[0], base, enc, mid
+    )
     token_weight = jnp.broadcast_to(image_weight.astype(NARROW)[:, None], (rows, 1))
-    payload = jnp.concatenate([conditions, latents, token_weight, jnp.zeros((rows, LANES - TOK_CH - 1), NARROW)], 1)
-    picks = (jnp.arange(rows, dtype=jnp.int32)[:, None] == route[None, :]).astype(NARROW)
-    arrived = exchange(dense(picks, payload).astype(NARROW), ranks_dp)
+    extra = jnp.concatenate([latents, token_weight, jnp.zeros((rows, LANES - TOK_CH - 1), NARROW)], 1)
+    dec_stored, flow_out, payload = decode(before, route, extra, table, attn_b[1], fc_b[1], dec, head)
+    arrived = exchange(payload, ranks_dp)
     divisor = TOK_CH * COPIES * count
-    loss_part, head_grads, cond_back = head_pass(
-        head, arrived[:, :D], arrived[:, D : D + TOK_CH], arrived[:, D + TOK_CH], timesteps, noise, divisor
+    loss_part, head_grads, cond_back = head_pass(head, arrived, timesteps, noise, divisor)
+    returned = exchange(cond_back, ranks_dp)
+    height = -(-((ranks - 1) * size + padded) // 8) * 8
+    full = fold({(4, name): value for name, value in head_grads.items()}, labels, height)
+    dec_found, (token_grad, before_grad, decoded_low, leaving_grad) = decode_back(
+        returned, route, flow_out, before, leaving, keep_column, table, dec_stored, dec, mid
     )
-    returned = exchange(cond_back.astype(NARROW), ranks_dp)
-    token_grad = lax.dot_general(picks, returned, (((0,), (0,)), ((), ())), preferred_element_type=WIDE)
-    after_grad = jnp.concatenate([jnp.zeros((BUF, D), WIDE), token_grad], 0)
-    flow_grad, dec_gain, dec_shift = norm_pull(flow_out, head.dec_gain, head.dec_shift)(after_grad)
-    head_grads.update(diffusion_pos=token_grad, dec_gain=dec_gain, dec_shift=dec_shift)
-    before_grad, dec_grads = block_backward(flow_grad, None, dec, dec_stored)
-    decoded_grad = jnp.where(keep[:, None], before_grad, 0.0)
-    decoded_low = decoded_grad.astype(NARROW)
-    pull = norm_pull(stream, mid.enc_gain, mid.enc_shift)
-    stream_grad, enc_gain, enc_shift = pull(back_input(decoded_low, mid.dec_weight))
+    enc_found, (stream_grad, embed_grad) = encode_back(leaving_grad, latents, stream, keep_row, table, enc_stored, enc)
+
+    def row(found, k):
+        return Vector(found[4], (MORE + k, 0, D))
+
+    head_grads = dict(diffusion_pos=token_grad, dec_gain=row(dec_found, 0), dec_shift=row(dec_found, 1))
     mid_grads = dict(
-        enc_gain=enc_gain, enc_shift=enc_shift, dec_weight=weight_grad(encoded, decoded_low), dec_bias=rows_sum(decoded_grad),
-        mask_token=rows_sum(jnp.where(keep[:, None], 0.0, before_grad)), decoder_pos=before_grad,
+        enc_gain=row(dec_found, 4), enc_shift=row(dec_found, 5), dec_weight=(encoded, decoded_low), dec_bias=row(dec_found, 2),
+        mask_token=row(dec_found, 3), decoder_pos=before_grad,
     )
-    stream_grad, enc_grads = block_backward(stream_grad, keep, enc, enc_stored)
-    token_in = stream_grad[BUF:]
-    base_grads = dict(
-        encoder_pos=stream_grad,
-        class_table=jnp.sum(stream_grad[:BUF], 0, keepdims=True),
-        embed_weight=weight_grad(latents, token_in.astype(NARROW)), embed_bias=rows_sum(token_in),
-    )
+    base_grads = dict(encoder_pos=stream_grad, class_table=row(enc_found, 0), embed_weight=embed_grad, embed_bias=row(enc_found, 1))
     grads = {}
-    for group, found in enumerate((base_grads, enc_grads, mid_grads, dec_grads, head_grads)):
+    parts = (base_grads, block_grads(enc_stored, enc_found), mid_grads, block_grads(dec_stored, dec_found), head_grads)
+    for group, found in enumerate(parts):
         grads.update({(group, name): value for name, value in found.items()})
-    height = -(-((ranks - 1) * size + padded) // 8) * 8
-    full = fold(grads, labels, height)
+    full = fold(grads, labels, height, full)
     if meshed:
         lane = lax.broadcasted_iota(jnp.int32, (8, LANES), 1)
         mark = jnp.where(lane == lax.axis_index("dp") * ranks_rep + lax.axis_index("rep"), loss_part, 0.0)

time: 827 us -> 787 us (0.952)
  other arithmetic: 51.8 us -> 22.5 us
  matrix products: 11.8 us -> 0 us
    reduce_sum x15 -> x0, other arithmetic: 17.9 us -> none  [the longest x3 5.16 us: rows_sum(): return jnp.sum(values.reshape(-1, values.shape[-1]), 0)]
    pallas_call x6 -> x7, Pallas kernels: 173 us -> 185 us  [the longest x2 57.6 us: fold(): pl.pallas_call(functools.partial(fold_kernel, products, items, plain, vec...]
    dot_general x8 -> x0, matrix products: 11.8 us -> none  [the longest x3 7.24 us: weight_grad(): lax.dot_general(flat_in, flat_grad, (((0,), (0,)), ((), ())), preferred_e...]
  transfers between devices with their start and end apart: 2 -> 2, of which waited for: 2 -> 0; matrix products, arithmetic and copies ran while one was open for 2% -> 2% of each run, Pallas kernels for 0% -> 3%
where the time goes in v3:
time: 787 us; the launch traced here: 778 us
  Pallas kernels  709 us (90%)
  local copies, waits for them, and re-layouts  25.9 us (3%)
  other arithmetic  22.5 us (3%)
  starting transfers between devices  15.5 us (2%)
    pallas_call x1, Pallas kernels, collect(): pl.pallas_call(functools.partial(collect_kernel, size), out_shape=(jax.Sh...  329 us
    pallas_call x1, Pallas kernels, spread(): pl.pallas_call(spread_kernel, out_shape=jax.ShapeDtypeStruct((32,) + own....  162 us
    pallas_call x2, Pallas kernels, fold(): pl.pallas_call(functools.partial(fold_kernel, products, items, plain, vec...  57.6 us
    pallas_call x1, Pallas kernels, head_pass(): pl.pallas_call(head_kernel, grid=(COPIES,), out_shape=[jax.ShapeDtypeStru...  45.4 us
    pallas_call x1, Pallas kernels, unfold(): pl.pallas_call(functools.partial(unfold_kernel, rows, padded, items), out...  33.6 us
    pallas_call x1, Pallas kernels, decode_back(): pl.pallas_call(decode_back_kernel, out_shape=backward_shapes(length, 16)...  23.6 us
    pallas_call x1, Pallas kernels, encode_back(): pl.pallas_call(encode_back_kernel, out_shape=backward_shapes(length, 8) +...  21.6 us
    pallas_call x1, Pallas kernels, encode(): pl.pallas_call(encode_kernel, out_shape=forward_shapes(length) + [jax.Sha...  19.8 us
  transfers between devices with their start and end apart: 2, of which 0 were waited for; matrix products, arithmetic and copies ran while one was open for 2% of the time, Pallas kernels for 3%

profile of v3, /device:TPU:21, one launch (start us, length us, event | category | flops | bytes accessed | tf_op | source)
XLA Modules:
  0.0 778.0 jit_solution(6544710975381601795)
XLA Ops:
  0.6 1.3 fusion.8
  1.9 0.1 concatenate.49
  2.0 0.6 broadcast_in_dim.50.keep_row
  2.6 0.8 broadcast_in_dim.60.keep_column
  3.4 1.9 convert_bitcast_fusion
  5.3 1.8 concatenate.48.own
  7.1 161.8 %shard_map.120.g_ref = bf16[32,5520,128]{2,1,0:T(8,128)(2,1)} custom-call(bf16[5520,128]{1,0:T(8,128)(2,1)} %concatenate.48.own), custom_call_target="tpu_custom_call" | custom-call | tf_op jit(solution)/shard_map/pallas_call | solution.py:578
  169.0 0.8 slice_bitcast_fusion.26
  169.7 1.3 slice_convert_fusion
  171.1 0.8 slice_bitcast_fusion.8
  171.9 0.0 copy-start.16
  171.9 33.6 %shard_map.121 = (bf16[16,768]{1,0:T(8,128)(2,1)S(1)}, bf16[320,768]{1,0:T(8,128)(2,1)S(1)}, bf16[768,2304]{1,0:T(8,128)(2,1)}, bf16[768,768]{1,0:T(8,128)(2,1)S...) custom-call(bf16[32,5520,128]{2,1,0:T(8,128)(2,1)} %shard_map.120.g_ref), custom_call_target="tpu_custom_call" | custom-call | flops 21753856 | bytes 87015424 | tf_op jit(solution)/shard_map/pallas_call | solution.py:232
  205.5 1.0 copy-done
  206.5 1.1 copy-done.1
  207.6 1.0 copy-done.2
  208.6 1.1 copy-done.3
  209.8 0.8 copy-done.4
  210.6 0.8 copy-done.5
  211.3 0.8 copy-done.6
  212.2 0.8 copy-done.7
  212.9 0.6 copy-done.8
  213.5 0.6 copy-done.9
  215.5 0.1 pad.10.clone
  215.6 0.1 pad.11.clone
  215.7 0.1 copy.27.latents
  215.8 1.3 gather_fusion
  217.2 0.2 stack.6
  217.4 0.6 convert_element_type.109.table
  218.0 0.7 maximum_maximum_fusion.extra
  218.7 0.6 fusion.7
  219.3 19.8 %shard_map.122 = (bf16[320,768]{1,0:T(8,128)(2,1)}, bf16[320,2304]{1,0:T(8,128)(2,1)}, f32[320,128]{1,0:T(8,128)}, bf16[320,768]{1,0:T(8,128)(2,1)}, f32[320,768...) custom-call(bf16[256,16]{1,0:T(8,128)(2,1)} %copy-done.13, ...), custom_call_target="tpu_custom_call" | custom-call | flops 4907335680 | bytes 24182784 | tf_op jit(solution)/shard_map/pallas_call | solution.py:898
  239.1 0.0 copy-start.15
  239.1 0.0 copy-start.17
  239.1 17.1 %shard_map.123 = (bf16[320,768]{1,0:T(8,128)(2,1)}, bf16[320,2304]{1,0:T(8,128)(2,1)}, f32[320,128]{1,0:T(8,128)}, bf16[320,768]{1,0:T(8,128)(2,1)}, f32[320,768...) custom-call(f32[320,768]{1,0:T(8,128)} %get-tuple-element.87.before,, ...), custom_call_target="tpu_custom_call" | custom-call | flops 4529848320 | bytes 23003136 | tf_op jit(solution)/shard_map/pallas_call | solution.py:932
  256.2 10.1 %all-to-all-start = ((bf16[8,32,896]{2,1,0:T(8,128)(2,1)}), bf16[8,32,896]{2,1,0:T(8,128)(2,1)S(1)}, u32[]{:S(2)}, u32[]{:S(2)}) async-start(bf16[8,32,896]{2,1,0:T(8,128)(2,1)} %bitcast.172), calls=%async_computation | async-start | bytes 917504 | tf_op jit(solution)/shard_map/all_to_all | solution.py:1320
  266.3 0.1 sqrt_bitcast_fusion.1
  266.4 0.8 slice_bitcast_fusion
  267.2 0.8 slice.156
  268.0 0.8 copy.32.route
  268.8 1.0 copy.31.levels
  269.9 1.0 copy.30
  270.9 0.1 stack.7
  271.0 0.6 convert_element_type.118.wide_b
  271.6 0.9 reshape_reshape_squeeze.3.final_w
  272.5 1.5 convert_reduce_fusion
  274.6 2.2 fusion.2
  276.9 0.9 pad_maximum_fusion.features.refs_2_
  277.7 1.2 bitcast_convert_fusion.final_b
  278.9 0.8 copy-done.11
  279.7 45.4 %shard_map.124 = (bf16[1024,1024]{1,0:T(8,128)(2,1)}, bf16[1024,3072]{1,0:T(8,128)(2,1)}, bf16[1024,1024]{1,0:T(8,128)(2,1)}, bf16[1024,1024]{1,0:T(8,128)(2,1)}...) custom-call(f32[1]{0:T(128)} %bitcast.1.divisor, ...), custom_call_target="tpu_custom_call" | custom-call | flops 22817013760 | bytes 27262976 | tf_op jit(solution)/shard_map/pallas_call | solution.py:1279
  325.1 1.2 slice.166
  326.3 5.4 all-to-all-start.1
  331.7 1.9 reshape.279.refs_13_
  333.6 0.6 compare_select_fusion.2
  334.2 21.9 %shard_map.127.refs_28_ = f32[176368,128]{1,0:T(8,128)} custom-call(s32[1]{0:T(128)S(6)} %copy.102.label, f32[16,1024]{1,0:T(8,128)} %get-tuple-element.141.refs_0_, f32[8,128]{1,0:T(8,128)} %get-tuple-element.142.refs_1_, bf16[1024,256]{1,0:T(8,128)(2,1)} %pad_maximum_fusion.features.refs_2_, bf16[1024,1024]{1,0:T(8,128)(2,1)} %get-tuple-element.143.refs_3_, ...), custom_call_target="tpu_custom_call" | custom-call | flops 11676942336 | bytes 25338368 | tf_op jit(solution)/shard_map/pallas_call | solution.py:418
  356.2 0.0 copy-start.12
  356.2 0.7 copy-done.12
  356.9 23.6 %shard_map.125 = (bf16[320,768]{1,0:T(8,128)(2,1)}, bf16[320,3072]{1,0:T(8,128)(2,1)}, bf16[320,768]{1,0:T(8,128)(2,1)}, bf16[320,2304]{1,0:T(8,128)(2,1)}, f32[...) custom-call(bf16[256,768]{1,0:T(8,128)(2,1)} %bitcast.170, ...), custom_call_target="tpu_custom_call" | custom-call | flops 4907335680 | bytes 24182784 | tf_op jit(solution)/shard_map/pallas_call | solution.py:1057
  380.5 21.6 %shard_map.126 = (bf16[320,768]{1,0:T(8,128)(2,1)}, bf16[320,3072]{1,0:T(8,128)(2,1)}, bf16[320,768]{1,0:T(8,128)(2,1)}, bf16[320,2304]{1,0:T(8,128)(2,1)}, f32[...) custom-call(f32[320,768]{1,0:T(8,128)} %get-tuple-element.107.leaving_grad,, ...), custom_call_target="tpu_custom_call" | custom-call | flops 4529848320 | bytes 23003136 | tf_op jit(solution)/shard_map/pallas_call | solution.py:1093
  402.1 35.7 %shard_map.128.refs_0_ = f32[176368,128]{1,0:T(8,128)} custom-call(s32[1]{0:T(128)S(6)} %copy.102.label, f32[8,768]{1,0:T(8,128)} %get-tuple-element.113.refs_0_, f32[1,2304]{1,0:T(1,128)} %get-tuple-element.114.refs_1_, f32[1,3072]{1,0:T(1,128)} %get-tuple-element.115.refs_2_, ...), custom_call_target="tpu_custom_call", output_to_operand_aliasing={{}: (29, {})} | custom-call | flops 9437184000 | bytes 64951296 | tf_op jit(solution)/shard_map/pallas_call | solution.py:418
  437.8 0.6 iota.19.refs_1_
  438.4 328.5 %shard_map.129 = (f32[5520,128]{1,0:T(8,128)}, f32[96,920,128]{2,1,0:T(8,128)}) custom-call(f32[176368,128]{1,0:T(8,128)} %shard_map.128.refs_0_, f32[8,128]{1,0:T(8,128)} %iota.19.refs_1_), custom_call_target="tpu_custom_call" | custom-call | tf_op jit(solution)/shard_map/pallas_call | solution.py:756
  766.9 1.3 slice_reduce_fusion
  768.9 7.6 multiply_add_fusion
  (48 shorter events, 0.2 us)
Async XLA Ops:
  171.9 43.8 %copy-start.16 = (bf16[256,16]{0,1:T(8,128)(2,1)S(1)}, bf16[256,16]{0,1:T(8,128)(2,1)}, u32[]{:S(2)}) copy-start(bf16[256,16]{0,1:T(8,128)(2,1)} %param.9) | copy-start | bytes 24580
  205.5 1.0 copy-start
  206.5 1.1 copy-start.1
  207.6 1.0 copy-start.2
  208.6 1.1 copy-start.3
  209.8 0.8 copy-start.4
  210.6 0.8 copy-start.5
  211.3 0.8 copy-start.6
  212.2 0.8 copy-start.7
  212.9 0.6 copy-start.8
  213.5 0.6 copy-start.9
  215.8 3.5 copy-start.13
  239.1 27.2 %copy-start.15 = (s32[4,256]{1,0:T(4,128)S(1)}, s32[4,256]{1,0:T(4,128)}, u32[]{:S(2)}) copy-start(s32[4,256]{1,0:T(4,128)} %param.12) | copy-start | bytes 12292
  239.1 28.9 %copy-start.17 = (s32[256]{0:T(256)S(1)}, s32[256]{0:T(256)}, u32[]{:S(2)}) copy-start(s32[256]{0:T(256)} %param.10) | copy-start | bytes 3076
  239.1 30.8 %copy-start.14 = (f32[4,256,16]{1,2,0:T(8,128)S(1)}, f32[4,256,16]{1,2,0:T(8,128)}, u32[]{:S(2)}) copy-start(f32[4,256,16]{1,2,0:T(8,128)} %param.13) | copy-start | bytes 196612
  256.2 22.7 %all-to-all-start = ((bf16[8,32,896]{2,1,0:T(8,128)(2,1)}), bf16[8,32,896]{2,1,0:T(8,128)(2,1)S(1)}, u32[]{:S(2)}, u32[]{:S(2)}) async-start(bf16[8,32,896]{2,1,0:T(8,128)(2,1)} %bitcast.172), calls=%async_computation | async-start | bytes 917504 | tf_op jit(solution)/shard_map/all_to_all | solution.py:1320
  278.9 0.8 copy-start.11
  326.3 29.9 %all-to-all-start.1 = ((bf16[8,32,768]{2,1,0:T(8,128)(2,1)}), bf16[8,32,768]{2,1,0:T(8,128)(2,1)S(1)}, u32[]{:S(2)}, u32[]{:S(2)}) async-start(bf16[8,32,768]{2,1,0:T(8,128)(2,1)} %bitcast.173), calls=%async_computation.1 | async-start | bytes 786432 | tf_op jit(solution)/shard_map/all_to_all | solution.py:1320
  356.2 0.7 copy-start.12
  438.4 330.5 %copy-start.10 = (f32[705408]{0:T(1024)S(1)}, f32[705408]{0:T(1024)}, u32[]{:S(2)}) copy-start(f32[705408]{0:T(1024)} %param.15) | copy-start | bytes 8464900

commit v4 on v3

--- a/solution.py
+++ b/solution.py
@@ -82,6 +82,24 @@
 USED = ENTRIES[-1].start + ENTRIES[-1].rows
 
 
+STACKS = ((D, D), (HW, HW))
+PLACES = [types.SimpleNamespace() for _ in GROUPS]
+STACK_OF = {}
+STACK_ROWS = []
+for number, (width, tallest) in enumerate(STACKS):
+    top = 0
+    for e in ENTRIES:
+        if e.matrix and not e.sparse and e.shape[1] == width and e.shape[0] <= tallest:
+            setattr(PLACES[e.group], e.name, (top, e.shape[0]))
+            STACK_OF[e] = number, top
+            top += e.shape[0]
+    STACK_ROWS.append(top)
+
+
+def placed(stack, place):
+    return stack.at[pl.ds(*place)]
+
+
 def block_height(entry, limit):
     best = 0
     for height in range(8, entry.shape[0] + 1, 8):
@@ -127,10 +145,12 @@
 
 def unfold_kernel(rows, padded, items, g_ref, *refs):
     count = len(items)
-    outs = refs[:count]
-    first, second, wide, first_sem, second_sem, out_sem = refs[count : count + 6]
+    total = len(STACKS) + sum(e not in STACK_OF for e, _ in items)
+    stacks, alone = refs[: len(STACKS)], iter(refs[len(STACKS) : total])
+    outs = [(stacks[STACK_OF[e][0]], STACK_OF[e][1]) if e in STACK_OF else (next(alone), 0) for e, _ in items]
+    first, second, wide, first_sem, second_sem, out_sem = refs[total : total + 6]
     kinds = sorted({(h, e.across) for e, h in items})
-    stages = dict(zip(kinds, refs[count + 6 :]))
+    stages = dict(zip(kinds, refs[total + 6 :]))
     turns = {kind: Slots(OUT) for kind in kinds}
     bases = [0]
     for entry, height in items:
@@ -183,8 +203,9 @@
 
         def put(b, t=t, stage=stage, height=height, place=turn.base, kind=kind):
             slot = (place + b) % OUT
+            into, top = outs[t]
             return pltpu.make_async_copy(
-                stage.at[slot], outs[t].at[pl.ds(pl.multiple_of(b * height, 8), height)], out_sem.at[kinds.index(kind), slot]
+                stage.at[slot], into.at[pl.ds(pl.multiple_of(top + b * height, 8), height)], out_sem.at[kinds.index(kind), slot]
             )
 
         def body(b, carry, t=t, entry=entry, height=height, window=window, blocks=blocks, stage=stage, turn=turn, put=put):
@@ -229,11 +250,13 @@
     tall = max(e.across * h for e, h in items) + 8
     kinds = sorted({(h, e.across) for e, h in items})
     total = sum(math.prod(e.shape) for e, _ in items)
+    alone = [e for e, _ in items if e not in STACK_OF]
+    shapes = [(n, width) for n, (width, _) in zip(STACK_ROWS, STACKS)] + [e.shape for e in alone]
     outs = pl.pallas_call(
         functools.partial(unfold_kernel, rows, padded, items),
-        out_shape=[jax.ShapeDtypeStruct(e.shape, NARROW) for e, _ in items],
+        out_shape=[jax.ShapeDtypeStruct(s, NARROW) for s in shapes],
         in_specs=[ANY],
-        out_specs=[ANY] * len(items),
+        out_specs=[ANY] * len(shapes),
         scratch_shapes=[
             pltpu.VMEM((SLOTS, tall, LANES), NARROW), pltpu.VMEM((SLOTS, tall, LANES), NARROW),
             pltpu.VMEM((2 * tall, LANES), WIDE), DMA((SLOTS,)), DMA((SLOTS,)), DMA((len(kinds), OUT)),
@@ -242,7 +265,7 @@
         compiler_params=pltpu.CompilerParams(vmem_limit_bytes=48 * 1000 * 1000),
         cost_estimate=pl.CostEstimate(flops=total, bytes_accessed=4 * total, transcendentals=0),
     )(gathered)
-    return {(e.group, e.name): out for (e, _), out in zip(items, outs)}
+    return outs[: len(STACKS)], {(e.group, e.name): out for e, out in zip(alone, outs[len(STACKS) :])}
 
 
 def rows_at(gathered, rows, start, number):
@@ -256,15 +279,16 @@
 
 
 def unpack(gathered, rows, groups):
-    matrices = unfold(gathered, rows)
+    stacks, matrices = unfold(gathered, rows)
     for e in ENTRIES:
-        if e.sparse:
+        if e.sparse or e in STACK_OF:
             continue
         if e.matrix:
             value = matrices[(e.group, e.name)]
         else:
             value = rows_at(gathered, rows, e.start, e.rows).reshape(-1)[: math.prod(e.shape)].reshape(e.shape)
         setattr(groups[e.group], e.name, value)
+    return stacks
 
 
 DEPTH = 3
@@ -514,11 +538,17 @@
         pl.when(condition)(action)
 
 
-def spread_kernel(own, out, keep_sem, send_sem, link_sem, core_send, core_sem):
+def spread_kernel(flat, route, out, wide, own, load_sem, keep_sem, send_sem, link_sem, core_send, core_sem):
     dp, rep = lax.axis_index("dp"), lax.axis_index("rep")
     z, x, y, c = dp // 2, dp % 2, rep // 2, rep % 2
-    unit = own.shape[0] // SHARES
+    size, padded = flat.shape[0], own.shape[0]
+    unit = padded // SHARES
     sibling = (dp, y * 2 + 1 - c)
+    loads = []
+    for u in range(SHARES):
+        part = pl.ds(u * unit, min(unit, size - u * unit))
+        loads.append(pltpu.make_async_copy(flat.at[part], wide.at[part], load_sem.at[u]))
+        loads[u].start()
 
     def device(dz, dx, dy):
         return ((z + dz) * 2 + (x + dx) % 2, (y + dy) % 2 * 2 + c)
@@ -534,9 +564,8 @@
     inner = z * (FAR - z)
     only(inner == 0, lambda: pl.semaphore_wait(barrier, len(near)))
     only(inner > 0, lambda: pl.semaphore_wait(barrier, len(near) + 1))
-    keep = pltpu.make_async_copy(own, out.at[dp * 4 + rep], keep_sem)
-    keep.start()
-    ends, number = [], 0
+    masked = jnp.sum(jnp.where(route[...] < SEQ, 1.0, 0.0))
+    keeps, ends, number = [], [], 0
     for u, dz, dx, dy in spread_order():
         part = pl.ds(u * unit, unit)
         q = ((z + dz) * 2 + (x + dx) % 2) * 2 + (y + dy) % 2
@@ -564,25 +593,36 @@
                 only(exists(hop[0]), lambda: copy(device(*hop), send_sem.at[n], link_sem.at[i]).wait_send())
             copy(sibling, core_send.at[i], core_sem.at[i]).wait()
 
+        if mine:
+            loads[u].wait()
+            if u == SHARES - 1:
+                wide[size:padded, :] = jnp.broadcast_to(masked, (padded - size, LANES))
+            own[part, :] = wide[part, :].astype(NARROW)
+            keeps.append(pltpu.make_async_copy(own.at[part], out.at[dp * 4 + rep, part], keep_sem.at[u]))
+            keeps[-1].start()
         there = None if dz == 0 else jnp.logical_and(z + dz >= 0, z + dz <= FAR)
         only(there, run)
         ends.append((there, finish))
     for there, finish in ends:
         only(there, finish)
-    keep.wait()
-
-
-def spread(own):
+    for keep in keeps:
+        keep.wait()
+
+
+def spread(flat, route, padded):
     pieces = SHARES * 16
     sends = sum(len(hops(*key)) for key in spread_order())
     return pl.pallas_call(
         spread_kernel,
-        out_shape=jax.ShapeDtypeStruct((32,) + own.shape, own.dtype),
-        in_specs=[ANY],
+        out_shape=jax.ShapeDtypeStruct((32, padded, LANES), NARROW),
+        in_specs=[ANY, VMEM],
         out_specs=ANY,
-        scratch_shapes=[DMA, DMA((sends,)), DMA((pieces,)), DMA((pieces,)), DMA((pieces,))],
+        scratch_shapes=[
+            pltpu.VMEM((padded, LANES), WIDE), pltpu.VMEM((padded, LANES), NARROW), DMA((SHARES,)), DMA((SHARES,)),
+            DMA((sends,)), DMA((pieces,)), DMA((pieces,)), DMA((pieces,)),
+        ],
         compiler_params=pltpu.CompilerParams(collective_id=0, has_side_effects=True),
-    )(own)
+    )(flat, route.reshape(-1, LANES))
 
 
 class Chip:
@@ -870,10 +910,16 @@
     return [jax.ShapeDtypeStruct((length, w), t) for w, t in widths]
 
 
-def encode_kernel(latents, keep_row, keep_column, table, attn_b, fc_b, embed_w, enc_pos, dec_pos, *refs):
-    sources, outs, (stream, encoded, leaving, before) = refs[:5], refs[5:13], refs[13:17]
-    held, sem = refs[17:22], refs[22]
-    moves = start_all(sources, held, sem)
+def encode_kernel(latents, keep_row, keep_column, table, attn_b, fc_b, stack, *refs):
+    (attn_src, one_src, two_src), outs, (stream, encoded, leaving, before) = refs[:3], refs[3:11], refs[11:15]
+    held, (embed_w, enc_pos, dec_pos), sem = refs[15:20], refs[20:23], refs[23]
+    base, enc, mid = PLACES[:3]
+    early = [placed(stack, place) for place in (base.embed_weight, base.encoder_pos, mid.decoder_pos)]
+    sources = [attn_src, placed(stack, enc.proj_weight), one_src, two_src, placed(stack, mid.dec_weight)]
+    moves = start_all(early + sources, (embed_w, enc_pos, dec_pos) + tuple(held), sem)
+    for move in moves[:3]:
+        move.wait()
+    moves = moves[3:]
     pos = enc_pos[...].astype(WIDE)
     stream[:BUF, :] = table[CLASS : CLASS + 1, :] + pos[:BUF]
     stream[BUF:, :] = matmul(latents[...], embed_w[...]) + table[EMBED_B : EMBED_B + 1, :] + pos[BUF:]
@@ -892,32 +938,33 @@
     return pl.CostEstimate(flops=2 * length * work, bytes_accessed=2 * work + 36 * length * D, transcendentals=4 * length * MLP)
 
 
-def encode(latents, keep_row, keep_column, table, attn_b, fc_b, base, enc, mid):
+def encode(latents, keep_row, keep_column, table, attn_b, fc_b, stack, enc):
     length = BUF + SEQ
     weights = BLOCK_WEIGHTS + ((D, D),)
     found = pl.pallas_call(
         encode_kernel,
         out_shape=forward_shapes(length)
         + [jax.ShapeDtypeStruct((length, D), t) for t in (WIDE, NARROW, WIDE, WIDE)],
-        in_specs=[VMEM] * 9 + [HBM] * 5,
+        in_specs=[VMEM] * 6 + [HBM] * 4,
         out_specs=[VMEM] * 12,
-        scratch_shapes=[pltpu.VMEM(s, NARROW) for s in weights] + [DMA((5,))],
+        scratch_shapes=[pltpu.VMEM(s, NARROW) for s in weights + ((TOK_CH, D), (length, D), (length, D))] + [DMA((8,))],
         compiler_params=BIG,
         cost_estimate=block_cost(length, weights),
     )(
-        latents, keep_row, keep_column, table, attn_b, fc_b, base.embed_weight, base.encoder_pos, mid.decoder_pos,
-        enc.attn_weight, enc.proj_weight, enc.fc_one_weight, enc.fc_two_weight, mid.dec_weight,
+        latents, keep_row, keep_column, table, attn_b, fc_b, stack, enc.attn_weight, enc.fc_one_weight, enc.fc_two_weight,
     )
     return found[:8], found[8:]
 
 
-def decode_kernel(before, route, extra, table, attn_b, fc_b, diff_pos, *refs):
-    sources, outs, (flow_out, payload) = refs[:4], refs[4:12], refs[12:14]
-    held, sem = refs[14:18], refs[18]
-    moves = start_all(sources, held, sem)
+def decode_kernel(before, route, extra, table, attn_b, fc_b, stack, *refs):
+    (attn_src, one_src, two_src), outs, (flow_out, payload) = refs[:3], refs[3:11], refs[11:13]
+    held, diff_pos, sem = refs[13:17], refs[17], refs[18]
+    sources = [attn_src, placed(stack, PLACES[DEC].proj_weight), one_src, two_src, placed(stack, PLACES[-1].diffusion_pos)]
+    moves = start_all(sources, tuple(held) + (diff_pos,), sem)
     value = forward_block(before[...], DEC_ROWS, None, table, attn_b, fc_b, outs, held, moves)
     flow_out[...] = value
     hat, _ = whiten(flow_out[BUF:, :])
+    moves[4].wait()
     value = hat * table[DEC_G : DEC_G + 1, :] + table[DEC_S : DEC_S + 1, :]
     conditions = (value + diff_pos[...].astype(WIDE)).astype(NARROW)
     slots = payload.shape[0]
@@ -927,20 +974,19 @@
     payload[:, D:] = matmul(picks, extra[...]).astype(NARROW)
 
 
-def decode(before, route, extra, table, attn_b, fc_b, dec, head):
+def decode(before, route, extra, table, attn_b, fc_b, stack, dec):
     length = BUF + SEQ
     found = pl.pallas_call(
         decode_kernel,
         out_shape=forward_shapes(length)
         + [jax.ShapeDtypeStruct((length, D), WIDE), jax.ShapeDtypeStruct((SEQ, D + LANES), NARROW)],
-        in_specs=[VMEM] * 7 + [HBM] * 4,
+        in_specs=[VMEM] * 6 + [HBM] * 4,
         out_specs=[VMEM] * 10,
-        scratch_shapes=[pltpu.VMEM(s, NARROW) for s in BLOCK_WEIGHTS] + [DMA((4,))],
+        scratch_shapes=[pltpu.VMEM(s, NARROW) for s in BLOCK_WEIGHTS + ((SEQ, D),)] + [DMA((5,))],
         compiler_params=BIG,
         cost_estimate=block_cost(length, BLOCK_WEIGHTS),
     )(
-        before, route[None], extra, table, attn_b, fc_b, head.diffusion_pos,
-        dec.attn_weight, dec.proj_weight, dec.fc_one_weight, dec.fc_two_weight,
+        before, route[None], extra, table, attn_b, fc_b, stack, dec.attn_weight, dec.fc_one_weight, dec.fc_two_weight,
     )
     return found[:8], found[8], found[9]
 
@@ -1016,9 +1062,10 @@
 
 
 def decode_back_kernel(returned, route, flow_out, before, leaving, keep_column, table, mixed, totals, middle, *refs):
-    slope_src, attn_src, proj_src, one_src, two_src, dec_src = refs[:6]
-    outs, (token_grad, before_grad, decoded_low, leaving_grad) = refs[6:13], refs[13:17]
-    attn_w, proj_w, one_w, two_w, dec_w, slope, attended_grad, sem = refs[17:]
+    slope_src, attn_src, one_src, two_src, stack = refs[:5]
+    proj_src, dec_src = placed(stack, PLACES[DEC].proj_weight), placed(stack, PLACES[2].dec_weight)
+    outs, (token_grad, before_grad, decoded_low, leaving_grad) = refs[5:12], refs[12:16]
+    attn_w, proj_w, one_w, two_w, dec_w, slope, attended_grad, sem = refs[16:]
     moves = start_all(
         (two_src, slope_src, one_src, proj_src, attn_src, dec_src), (two_w, slope, one_w, proj_w, attn_w, dec_w), sem
     )
@@ -1050,7 +1097,7 @@
     leaving_grad[...] = whiten_back(part * table[ENC_G : ENC_G + 1, :], hat, r)
 
 
-def decode_back(returned, route, flow_out, before, leaving, keep_column, table, stored, dec, mid):
+def decode_back(returned, route, flow_out, before, leaving, keep_column, table, stored, stack, dec):
     length = BUF + SEQ
     weights = BLOCK_WEIGHTS + ((D, D),)
     normed, mixed, totals, attended, middle, second, slope, active = stored
@@ -1058,20 +1105,21 @@
         decode_back_kernel,
         out_shape=backward_shapes(length, 16)
         + [jax.ShapeDtypeStruct((n, D), t) for n, t in ((SEQ, WIDE), (length, WIDE), (length, NARROW), (length, WIDE))],
-        in_specs=[VMEM] * 10 + [HBM] * 6,
+        in_specs=[VMEM] * 10 + [HBM] * 5,
         out_specs=[VMEM] * 11,
         scratch_shapes=backward_scratch(length, weights),
         compiler_params=BIG,
         cost_estimate=block_cost(length, weights),
     )(
         returned, route[:, None], flow_out, before, leaving, keep_column, table, mixed, totals, middle,
-        slope, dec.attn_weight, dec.proj_weight, dec.fc_one_weight, dec.fc_two_weight, mid.dec_weight,
+        slope, dec.attn_weight, dec.fc_one_weight, dec.fc_two_weight, stack,
     )
     return found[:7], found[7:]
 
 
 def encode_back_kernel(leaving_grad, latents, stream, keep_row, table, mixed, totals, middle, *refs):
-    slope_src, attn_src, proj_src, one_src, two_src = refs[:5]
+    slope_src, attn_src, one_src, two_src, stack = refs[:5]
+    proj_src = placed(stack, PLACES[ENC].proj_weight)
     outs, (stream_grad, embed_grad) = refs[5:12], refs[12:14]
     attn_w, proj_w, one_w, two_w, slope, attended_grad, sem = refs[14:]
     moves = start_all((two_src, slope_src, one_src, proj_src, attn_src), (two_w, slope, one_w, proj_w, attn_w), sem)
@@ -1087,7 +1135,7 @@
     embed_grad[...] = lax.dot_general(latents[...], tokens.astype(NARROW), (((0,), (0,)), ((), ())), preferred_element_type=WIDE)
 
 
-def encode_back(leaving_grad, latents, stream, keep_row, table, stored, enc):
+def encode_back(leaving_grad, latents, stream, keep_row, table, stored, stack, enc):
     length = BUF + SEQ
     normed, mixed, totals, attended, middle, second, slope, active = stored
     found = pl.pallas_call(
@@ -1101,7 +1149,7 @@
         cost_estimate=block_cost(length, BLOCK_WEIGHTS),
     )(
         leaving_grad, latents, stream, keep_row, table, mixed, totals, middle,
-        slope, enc.attn_weight, enc.proj_weight, enc.fc_one_weight, enc.fc_two_weight,
+        slope, enc.attn_weight, enc.fc_one_weight, enc.fc_two_weight, stack,
     )
     return found[:7], found[7:]
 
@@ -1151,13 +1199,15 @@
 
 
 def head_kernel(
-    divisor, arrived, features, levels, noise, input_w, final_w, wide_b, ada_b, final_b,
-    cond_src, time_src, ada_src, inner_src, outer_src,
+    divisor, arrived, features, levels, noise, final_w, wide_b, ada_b, final_b, ada_src, stack,
     signal, mod_low, modulated, inner_low, active, outer_low, joined_low, cond_low, cond_back, wide_sums, final_grad, input_grad, last,
-    cond, joined, hidden, mod, hat, inner, outer, top, total, sums, cond_w, time_w, ada_w, inner_w, outer_w, weight_sem,
+    cond, joined, hidden, mod, hat, inner, outer, top, total, sums, cond_w, time_w, input_w, ada_w, inner_w, outer_w, weight_sem,
 ):
     step = pl.program_id(0)
-    sources, held = (cond_src, time_src, ada_src, inner_src, outer_src), (cond_w, time_w, ada_w, inner_w, outer_w)
+    own = PLACES[-1]
+    sources = [placed(stack, place) for place in (own.cond_weight, own.time_weight, own.input_weight)]
+    sources += [ada_src, placed(stack, own.inner_weight), placed(stack, own.outer_weight)]
+    held = (cond_w, time_w, input_w, ada_w, inner_w, outer_w)
     moves = [pltpu.make_async_copy(s, t, weight_sem.at[i]) for i, (s, t) in enumerate(zip(sources, held))]
 
     def need(*which):
@@ -1178,8 +1228,8 @@
             move.start()
         for ref in (sums, total, final_grad, input_grad, last):
             ref[...] = jnp.zeros_like(ref)
-        moves[0].wait()
-        moves[1].wait()
+        for move in moves[:3]:
+            move.wait()
         cond[...] = matmul(arrived[:, :D], cond_w[...]) + bias(0)
 
     clean = arrived[:, D : D + TOK_CH].astype(WIDE)
@@ -1192,7 +1242,7 @@
     hidden[...] = h
     value, first_r = whiten(h)
     hat[...] = value
-    need(2, 3, 4)
+    need(3, 4, 5)
     mod[...] = matmul(signal[...], ada_w[...])
     normed = hat[...] * bias(3) + bias(4)
     scale = 1.0 + (mod[:, HW : 2 * HW] + ada_b[0:1, HW : 2 * HW])
@@ -1252,7 +1302,7 @@
             wide_sums[k : k + 1, :] = column_sum(sums[k * 8 : (k + 1) * 8, :])
 
 
-def head_pass(p, arrived, steps, noise, divisor):
+def head_pass(p, stack, arrived, steps, noise, divisor):
     slots = arrived.shape[0]
     times = steps.astype(WIDE)
     features = time_features(times).astype(NARROW).reshape(-1, FREQ)
@@ -1270,8 +1320,9 @@
     def whole(x):
         return pl.BlockSpec(x, lambda i: (0, 0), pipeline_mode=pl.Buffered(1))
 
-    weights = (p.cond_weight, p.time_weight, p.ada_weight, p.inner_weight, p.outer_weight)
-    small = (p.input_weight, p.final_weight, wide_b, p.ada_bias.astype(WIDE)[None], p.final_bias.astype(WIDE)[None])
+    heights = (D, FREQ, TOK_CH, None, HW, HW)
+    weights = [(h, HW) if h else (HW, 3 * HW) for h in heights]
+    small = (p.final_weight, wide_b, p.ada_bias.astype(WIDE)[None], p.final_bias.astype(WIDE)[None])
     kept = [((total, w), NARROW, tiled(w)) for w in (HW, 3 * HW, HW, HW, HW, HW, HW)]
     once = (((slots, HW), NARROW), ((slots, D), NARROW), ((16, HW), WIDE), ((HW, TOK_CH), WIDE), ((TOK_CH, HW), WIDE), ((8, LANES), WIDE))
     kept += [(s, t, whole(s)) for s, t in once]
@@ -1281,13 +1332,13 @@
         grid=(COPIES,),
         out_shape=[jax.ShapeDtypeStruct(s, t) for s, t, _ in kept],
         in_specs=[pl.BlockSpec(memory_space=pltpu.SMEM), whole(arrived.shape), tiled(FREQ), tiled(2), tiled(TOK_CH)]
-        + [whole(x.shape) for x in small] + [HBM] * len(weights),
+        + [whole(x.shape) for x in small] + [HBM] * 2,
         out_specs=[spec for _, _, spec in kept],
         scratch_shapes=[pltpu.VMEM((slots, w), WIDE) for w in (HW, HW, HW, 3 * HW, HW, HW, HW, HW, HW)]
-        + [pltpu.VMEM((SUMS * 8, HW), WIDE)] + [pltpu.VMEM(x.shape, NARROW) for x in weights] + [DMA((len(weights),))],
+        + [pltpu.VMEM((SUMS * 8, HW), WIDE)] + [pltpu.VMEM(s, NARROW) for s in weights] + [DMA((len(weights),))],
         compiler_params=BIG,
         cost_estimate=pl.CostEstimate(flops=flops, bytes_accessed=26 * total * HW, transcendentals=3 * total * HW),
-    )(divisor[None], arrived, features, levels, flat_noise, *small, *weights)
+    )(divisor[None], arrived, features, levels, flat_noise, *small, p.ada_weight, stack)
     signal, mod_low, modulated, inner_low, active, outer_low, joined_low, cond_low, cond_back, sums, final_grad, input_grad, last = found
 
     def row(k):
@@ -1331,12 +1382,14 @@
     size = weights.shape[0] // LANES
     padded = -(-(size + 1) // 48) * 48
     masked = route < rows
-    own = jnp.sum(masked.astype(WIDE))
-    low = weights.reshape(size, LANES).astype(NARROW)
-    block = jnp.concatenate([low, jnp.full((padded - size, LANES), own).astype(NARROW)], 0)
-    gathered = spread(block) if meshed else lax.all_gather(block, BOTH, axis=0)
+    flat = weights.reshape(size, LANES)
+    if meshed:
+        gathered = spread(flat, route, padded)
+    else:
+        extra = jnp.full((padded - size, LANES), jnp.sum(masked.astype(WIDE)))
+        gathered = lax.all_gather(jnp.concatenate([flat, extra], 0).astype(NARROW), BOTH, axis=0)
     base, enc, mid, dec, head = groups = [types.SimpleNamespace() for _ in GROUPS]
-    unpack(gathered, size, groups)
+    stack, head_stack = unpack(gathered, size, groups)
     count = jnp.sum(gathered[:, size, 0].astype(WIDE))
     keep = jnp.concatenate([jnp.ones((BUF,), WIDE), 1.0 - masked.astype(WIDE)])
     keep_row, keep_column = keep[None], keep[:, None]
@@ -1344,21 +1397,21 @@
     classes = gathered[at // size, at % size].reshape(D)
     table, attn_b, fc_b = block_vectors(base, enc, mid, dec, head, classes)
     enc_stored, (stream, encoded, leaving, before) = encode(
-        latents, keep_row, keep_column, table, attn_b[0], fc_b[0], base, enc, mid
+        latents, keep_row, keep_column, table, attn_b[0], fc_b[0], stack, enc
     )
     token_weight = jnp.broadcast_to(image_weight.astype(NARROW)[:, None], (rows, 1))
     extra = jnp.concatenate([latents, token_weight, jnp.zeros((rows, LANES - TOK_CH - 1), NARROW)], 1)
-    dec_stored, flow_out, payload = decode(before, route, extra, table, attn_b[1], fc_b[1], dec, head)
+    dec_stored, flow_out, payload = decode(before, route, extra, table, attn_b[1], fc_b[1], stack, dec)
     arrived = exchange(payload, ranks_dp)
     divisor = TOK_CH * COPIES * count
-    loss_part, head_grads, cond_back = head_pass(head, arrived, timesteps, noise, divisor)
+    loss_part, head_grads, cond_back = head_pass(head, head_stack, arrived, timesteps, noise, divisor)
     returned = exchange(cond_back, ranks_dp)
     height = -(-((ranks - 1) * size + padded) // 8) * 8
     full = fold({(4, name): value for name, value in head_grads.items()}, labels, height)
     dec_found, (token_grad, before_grad, decoded_low, leaving_grad) = decode_back(
-        returned, route, flow_out, before, leaving, keep_column, table, dec_stored, dec, mid
+        returned, route, flow_out, before, leaving, keep_column, table, dec_stored, stack, dec
     )
-    enc_found, (stream_grad, embed_grad) = encode_back(leaving_grad, latents, stream, keep_row, table, enc_stored, enc)
+    enc_found, (stream_grad, embed_grad) = encode_back(leaving_grad, latents, stream, keep_row, table, enc_stored, stack, enc)
 
     def row(found, k):
         return Vector(found[4], (MORE + k, 0, D))

time: 787 us -> 780 us (level)
  no operation moved by 1% of the time
where the time goes in v4:
time: 780 us; the launch traced here: 771 us
  Pallas kernels  711 us (91%)
  other arithmetic  20 us (3%)
  local copies, waits for them, and re-layouts  19.2 us (2%)
  starting transfers between devices  15.4 us (2%)
    pallas_call x1, Pallas kernels, collect(): pl.pallas_call(functools.partial(collect_kernel, size), out_shape=(jax.Sh...  329 us
    pallas_call x1, Pallas kernels, spread(): pl.pallas_call(spread_kernel, out_shape=jax.ShapeDtypeStruct((32, padded,...  162 us
    pallas_call x2, Pallas kernels, fold(): pl.pallas_call(functools.partial(fold_kernel, products, items, plain, vec...  57.5 us
    pallas_call x1, Pallas kernels, head_pass(): pl.pallas_call(head_kernel, grid=(COPIES,), out_shape=[jax.ShapeDtypeStru...  45.4 us
    pallas_call x1, Pallas kernels, unfold(): pl.pallas_call(functools.partial(unfold_kernel, rows, padded, items), out...  33 us
    pallas_call x1, Pallas kernels, decode_back(): pl.pallas_call(decode_back_kernel, out_shape=backward_shapes(length, 16)...  23.6 us
    pallas_call x1, Pallas kernels, encode_back(): pl.pallas_call(encode_back_kernel, out_shape=backward_shapes(length, 8) +...  21.5 us
    pallas_call x1, Pallas kernels, encode(): pl.pallas_call(encode_kernel, out_shape=forward_shapes(length) + [jax.Sha...  19.6 us
  transfers between devices with their start and end apart: 2, of which 0 were waited for; matrix products, arithmetic and copies ran while one was open for 2% of the time, Pallas kernels for 3%

profile of v4, /device:TPU:21, one launch (start us, length us, event | category | flops | bytes accessed | tf_op | source)
XLA Modules:
  0.0 770.8 jit_solution(5170198570261724064)
XLA Ops:
  0.6 0.7 fusion.8
  1.3 0.1 concatenate.45
  1.4 0.6 broadcast_in_dim.49.keep_row
  2.0 0.8 broadcast_in_dim.59.keep_column
  2.7 162.5 %shard_map.120.g_ref = bf16[32,5520,128]{2,1,0:T(8,128)(2,1)} custom-call(f32[5511,128]{1,0:T(8,128)} %bitcast.168, s32[2,128]{1,0:T(2,128)} %bitcast.177), custom_call_target="tpu_custom_call" | custom-call | tf_op jit(solution)/shard_map/pallas_call | solution.py:615
  165.2 0.8 slice_bitcast_fusion.26
  166.0 1.3 slice_convert_fusion
  167.3 0.8 slice_bitcast_fusion.8
  168.2 0.0 copy-start.9
  168.2 33.0 %shard_map.121 = (bf16[3216,768]{1,0:T(8,128)(2,1)}, bf16[3088,1024]{1,0:T(8,128)(2,1)}, bf16[768,2304]{1,0:T(8,128)(2,1)S(1)}, bf16[768,3072]{1,0:T(8,128)(2,1)...) custom-call(bf16[32,5520,128]{2,1,0:T(8,128)(2,1)} %shard_map.120.g_ref), custom_call_target="tpu_custom_call" | custom-call | flops 21753856 | bytes 87015424 | tf_op jit(solution)/shard_map/pallas_call | solution.py:255
  201.2 0.0 copy-start
  201.2 1.8 copy-done
  202.9 1.9 copy-done.1
  206.1 0.1 pad.9.clone
  206.2 0.1 pad.10.clone
  206.3 0.0 copy-done.9
  206.3 0.1 copy.27.latents
  206.4 1.4 gather_fusion
  207.9 0.2 stack.6
  208.1 0.6 convert_element_type.95.table
  208.7 0.7 maximum_maximum_fusion.extra
  209.4 0.6 fusion.7
  210.0 0.0 copy-done.5
  210.0 19.6 %shard_map.122 = (bf16[320,768]{1,0:T(8,128)(2,1)}, bf16[320,2304]{1,0:T(8,128)(2,1)}, f32[320,128]{1,0:T(8,128)}, bf16[320,768]{1,0:T(8,128)(2,1)}, f32[320,768...) custom-call(bf16[256,16]{1,0:T(8,128)(2,1)} %copy-done.5, ...), custom_call_target="tpu_custom_call" | custom-call | flops 4907335680 | bytes 24182784 | tf_op jit(solution)/shard_map/pallas_call | solution.py:944
  229.6 0.0 copy-start.8
  229.6 0.0 copy-start.7
  229.7 0.0 copy-start.6
  229.7 19.4 %shard_map.123 = (bf16[320,768]{1,0:T(8,128)(2,1)}, bf16[320,2304]{1,0:T(8,128)(2,1)}, f32[320,128]{1,0:T(8,128)}, bf16[320,768]{1,0:T(8,128)(2,1)}, f32[320,768...) custom-call(f32[320,768]{1,0:T(8,128)} %get-tuple-element.73.before,, ...), custom_call_target="tpu_custom_call" | custom-call | flops 4529848320 | bytes 23003136 | tf_op jit(solution)/shard_map/pallas_call | solution.py:979
  249.0 10.0 %all-to-all-start = ((bf16[8,32,896]{2,1,0:T(8,128)(2,1)}), bf16[8,32,896]{2,1,0:T(8,128)(2,1)S(1)}, u32[]{:S(2)}, u32[]{:S(2)}) async-start(bf16[8,32,896]{2,1,0:T(8,128)(2,1)} %bitcast.173), calls=%async_computation | async-start | bytes 917504 | tf_op jit(solution)/shard_map/all_to_all | solution.py:1371
  259.1 0.0 copy-done.8
  259.1 0.1 sqrt_bitcast_fusion.1
  259.1 0.8 slice_bitcast_fusion
  259.9 0.8 slice.156
  260.7 0.0 copy-done.7
  260.7 0.8 copy.32.route
  261.6 1.1 copy.31.levels
  262.6 0.0 copy-done.6
  262.6 1.0 copy.30
  263.7 0.1 stack.7
  263.8 0.6 convert_element_type.104.wide_b
  264.4 0.9 reshape_reshape_squeeze.3.final_w
  265.3 1.5 convert_reduce_fusion
  267.4 2.2 fusion.2
  269.7 0.9 pad_maximum_fusion.features.refs_2_
  270.5 1.2 bitcast_convert_fusion.final_b
  271.8 0.0 all-to-all-done
  271.8 0.8 copy-done.3
  272.6 45.4 %shard_map.124 = (bf16[1024,1024]{1,0:T(8,128)(2,1)}, bf16[1024,3072]{1,0:T(8,128)(2,1)}, bf16[1024,1024]{1,0:T(8,128)(2,1)}, bf16[1024,1024]{1,0:T(8,128)(2,1)}...) custom-call(f32[1]{0:T(128)} %bitcast.2.divisor, ...), custom_call_target="tpu_custom_call" | custom-call | flops 22817013760 | bytes 27262976 | tf_op jit(solution)/shard_map/pallas_call | solution.py:1330
  318.0 1.2 slice.166
  319.2 5.4 all-to-all-start.1
  324.6 1.8 reshape.285.refs_13_
  326.5 0.6 compare_select_fusion.2
  327.1 21.9 %shard_map.127.refs_28_ = f32[176368,128]{1,0:T(8,128)} custom-call(s32[1]{0:T(128)S(6)} %copy.102.label, f32[16,1024]{1,0:T(8,128)} %get-tuple-element.121.refs_0_, f32[8,128]{1,0:T(8,128)} %get-tuple-element.122.refs_1_, bf16[1024,256]{1,0:T(8,128)(2,1)} %pad_maximum_fusion.features.refs_2_, bf16[1024,1024]{1,0:T(8,128)(2,1)} %get-tuple-element.123.refs_3_, ...), custom_call_target="tpu_custom_call" | custom-call | flops 11676942336 | bytes 25338368 | tf_op jit(solution)/shard_map/pallas_call | solution.py:442
  349.0 0.0 all-to-all-done.1
  349.0 0.0 copy-start.4
  349.0 0.7 copy-done.4
  349.7 23.6 %shard_map.125 = (bf16[320,768]{1,0:T(8,128)(2,1)}, bf16[320,3072]{1,0:T(8,128)(2,1)}, bf16[320,768]{1,0:T(8,128)(2,1)}, bf16[320,2304]{1,0:T(8,128)(2,1)}, f32[...) custom-call(bf16[256,768]{1,0:T(8,128)(2,1)} %bitcast.171, ...), custom_call_target="tpu_custom_call" | custom-call | flops 4907335680 | bytes 24182784 | tf_op jit(solution)/shard_map/pallas_call | solution.py:1104
  373.3 21.5 %shard_map.126 = (bf16[320,768]{1,0:T(8,128)(2,1)}, bf16[320,3072]{1,0:T(8,128)(2,1)}, bf16[320,768]{1,0:T(8,128)(2,1)}, bf16[320,2304]{1,0:T(8,128)(2,1)}, f32[...) custom-call(f32[320,768]{1,0:T(8,128)} %get-tuple-element.87.leaving_grad, ...), custom_call_target="tpu_custom_call" | custom-call | flops 4529848320 | bytes 23003136 | tf_op jit(solution)/shard_map/pallas_call | solution.py:1141
  394.8 35.6 %shard_map.128.refs_0_ = f32[176368,128]{1,0:T(8,128)} custom-call(s32[1]{0:T(128)S(6)} %copy.102.label, f32[8,768]{1,0:T(8,128)} %get-tuple-element.93.refs_0_, f32[1,2304]{1,0:T(1,128)} %get-tuple-element.94.refs_1_, f32[1,3072]{1,0:T(1,128)} %get-tuple-element.95.refs_2_, f32[16,768]{1,0:T(8,128)} %get-tuple-element.96.refs_3_, ...), custom_call_target="tpu_custom_call", output_to_operand_aliasing={{}: (29, {})} | custom-call | flops 9437184000 | bytes 64951296 | tf_op jit(solution)/shard_map/pallas_call | solution.py:442
  430.4 0.6 iota.19.refs_1_
  431.0 328.6 %shard_map.129 = (f32[5520,128]{1,0:T(8,128)}, f32[96,920,128]{2,1,0:T(8,128)}) custom-call(f32[176368,128]{1,0:T(8,128)} %shard_map.128.refs_0_, f32[8,128]{1,0:T(8,128)} %iota.19.refs_1_), custom_call_target="tpu_custom_call" | custom-call | tf_op jit(solution)/shard_map/pallas_call | solution.py:796
  759.7 1.3 slice_reduce_fusion
  761.6 0.0 copy-done.2
  761.6 7.6 multiply_add_fusion
  (30 shorter events, 0.2 us)
Async XLA Ops:
  168.2 38.1 %copy-start.9 = (bf16[256,16]{0,1:T(8,128)(2,1)S(1)}, bf16[256,16]{0,1:T(8,128)(2,1)}, u32[]{:S(2)}) copy-start(bf16[256,16]{0,1:T(8,128)(2,1)} %param.9) | copy-start | bytes 24580
  201.2 1.8 copy-start
  202.9 1.9 copy-start.1
  206.4 3.6 copy-start.5
  229.6 29.4 %copy-start.8 = (s32[4,256]{1,0:T(4,128)S(1)}, s32[4,256]{1,0:T(4,128)}, u32[]{:S(2)}) copy-start(s32[4,256]{1,0:T(4,128)} %param.12) | copy-start | bytes 12292
  229.6 31.1 %copy-start.7 = (s32[256]{0:T(256)S(1)}, s32[256]{0:T(256)}, u32[]{:S(2)}) copy-start(s32[256]{0:T(256)} %param.10) | copy-start | bytes 3076
  229.7 33.0 %copy-start.6 = (f32[4,256,16]{1,2,0:T(8,128)S(1)}, f32[4,256,16]{1,2,0:T(8,128)}, u32[]{:S(2)}) copy-start(f32[4,256,16]{1,2,0:T(8,128)} %param.13) | copy-start | bytes 196612
  249.0 22.7 %all-to-all-start = ((bf16[8,32,896]{2,1,0:T(8,128)(2,1)}), bf16[8,32,896]{2,1,0:T(8,128)(2,1)S(1)}, u32[]{:S(2)}, u32[]{:S(2)}) async-start(bf16[8,32,896]{2,1,0:T(8,128)(2,1)} %bitcast.173), calls=%async_computation | async-start | bytes 917504 | tf_op jit(solution)/shard_map/all_to_all | solution.py:1371
  271.8 0.8 copy-start.3
  319.2 29.8 %all-to-all-start.1 = ((bf16[8,32,768]{2,1,0:T(8,128)(2,1)}), bf16[8,32,768]{2,1,0:T(8,128)(2,1)S(1)}, u32[]{:S(2)}, u32[]{:S(2)}) async-start(bf16[8,32,768]{2,1,0:T(8,128)(2,1)} %bitcast.174), calls=%async_computation.1 | async-start | bytes 786432 | tf_op jit(solution)/shard_map/all_to_all | solution.py:1371
  349.0 0.7 copy-start.4
  431.0 330.6 %copy-start.2 = (f32[705408]{0:T(1024)S(1)}, f32[705408]{0:T(1024)}, u32[]{:S(2)}) copy-start(f32[705408]{0:T(1024)} %param.15) | copy-start | bytes 8464900

commit v5 on v4

--- a/solution.py
+++ b/solution.py
@@ -864,6 +864,11 @@
     return jnp.stack(rows).astype(WIDE), attn_b, [p.fc_one_bias.astype(WIDE)[None] for p in (enc, dec)]
 
 
+class Here:
+    def wait(self):
+        pass
+
+
 def forward_block(value, first, keep, table, attn_b, fc_b, outs, weights, moves):
     normed, mixed, totals, attended, middle, second, slope, active = outs
     attn_w, proj_w, one_w, two_w = weights
@@ -912,14 +917,12 @@
 
 def encode_kernel(latents, keep_row, keep_column, table, attn_b, fc_b, stack, *refs):
     (attn_src, one_src, two_src), outs, (stream, encoded, leaving, before) = refs[:3], refs[3:11], refs[11:15]
-    held, (embed_w, enc_pos, dec_pos), sem = refs[15:20], refs[20:23], refs[23]
+    attn_w, one_w, two_w, sem = refs[15:]
     base, enc, mid = PLACES[:3]
-    early = [placed(stack, place) for place in (base.embed_weight, base.encoder_pos, mid.decoder_pos)]
-    sources = [attn_src, placed(stack, enc.proj_weight), one_src, two_src, placed(stack, mid.dec_weight)]
-    moves = start_all(early + sources, (embed_w, enc_pos, dec_pos) + tuple(held), sem)
-    for move in moves[:3]:
-        move.wait()
-    moves = moves[3:]
+    embed_w, enc_pos, dec_pos = (placed(stack, place) for place in (base.embed_weight, base.encoder_pos, mid.decoder_pos))
+    held = attn_w, placed(stack, enc.proj_weight), one_w, two_w, placed(stack, mid.dec_weight)
+    moves = start_all((attn_src, one_src, two_src), (attn_w, one_w, two_w), sem)
+    moves.insert(1, Here())
     pos = enc_pos[...].astype(WIDE)
     stream[:BUF, :] = table[CLASS : CLASS + 1, :] + pos[:BUF]
     stream[BUF:, :] = matmul(latents[...], embed_w[...]) + table[EMBED_B : EMBED_B + 1, :] + pos[BUF:]
@@ -927,7 +930,6 @@
     leaving[...] = value
     hat, _ = whiten(value)
     encoded[...] = (hat * table[ENC_G : ENC_G + 1, :] + table[ENC_S : ENC_S + 1, :]).astype(NARROW)
-    moves[4].wait()
     value = matmul(encoded[...], held[4][...]) + table[DEC_B : DEC_B + 1, :]
     value = jnp.where(keep_column[...] > 0.0, value, table[MASK_T : MASK_T + 1, :])
     before[...] = value + dec_pos[...].astype(WIDE)
@@ -945,9 +947,9 @@
         encode_kernel,
         out_shape=forward_shapes(length)
         + [jax.ShapeDtypeStruct((length, D), t) for t in (WIDE, NARROW, WIDE, WIDE)],
-        in_specs=[VMEM] * 6 + [HBM] * 4,
+        in_specs=[VMEM] * 7 + [HBM] * 3,
         out_specs=[VMEM] * 12,
-        scratch_shapes=[pltpu.VMEM(s, NARROW) for s in weights + ((TOK_CH, D), (length, D), (length, D))] + [DMA((8,))],
+        scratch_shapes=[pltpu.VMEM(s, NARROW) for s in BLOCK_WEIGHTS if s != (D, D)] + [DMA((3,))],
         compiler_params=BIG,
         cost_estimate=block_cost(length, weights),
     )(
@@ -958,13 +960,14 @@
 
 def decode_kernel(before, route, extra, table, attn_b, fc_b, stack, *refs):
     (attn_src, one_src, two_src), outs, (flow_out, payload) = refs[:3], refs[3:11], refs[11:13]
-    held, diff_pos, sem = refs[13:17], refs[17], refs[18]
-    sources = [attn_src, placed(stack, PLACES[DEC].proj_weight), one_src, two_src, placed(stack, PLACES[-1].diffusion_pos)]
-    moves = start_all(sources, tuple(held) + (diff_pos,), sem)
+    attn_w, one_w, two_w, sem = refs[13:]
+    held = attn_w, placed(stack, PLACES[DEC].proj_weight), one_w, two_w
+    diff_pos = placed(stack, PLACES[-1].diffusion_pos)
+    moves = start_all((attn_src, one_src, two_src), (attn_w, one_w, two_w), sem)
+    moves.insert(1, Here())
     value = forward_block(before[...], DEC_ROWS, None, table, attn_b, fc_b, outs, held, moves)
     flow_out[...] = value
     hat, _ = whiten(flow_out[BUF:, :])
-    moves[4].wait()
     value = hat * table[DEC_G : DEC_G + 1, :] + table[DEC_S : DEC_S + 1, :]
     conditions = (value + diff_pos[...].astype(WIDE)).astype(NARROW)
     slots = payload.shape[0]
@@ -980,9 +983,9 @@
         decode_kernel,
         out_shape=forward_shapes(length)
         + [jax.ShapeDtypeStruct((length, D), WIDE), jax.ShapeDtypeStruct((SEQ, D + LANES), NARROW)],
-        in_specs=[VMEM] * 6 + [HBM] * 4,
+        in_specs=[VMEM] * 7 + [HBM] * 3,
         out_specs=[VMEM] * 10,
-        scratch_shapes=[pltpu.VMEM(s, NARROW) for s in BLOCK_WEIGHTS + ((SEQ, D),)] + [DMA((5,))],
+        scratch_shapes=[pltpu.VMEM(s, NARROW) for s in BLOCK_WEIGHTS if s != (D, D)] + [DMA((3,))],
         compiler_params=BIG,
         cost_estimate=block_cost(length, BLOCK_WEIGHTS),
     )(
@@ -1298,6 +1301,7 @@
         found = total[...].astype(NARROW)
         cond_low[...] = found
         cond_back[...] = matmul_turned(found, cond_w[...]).astype(NARROW)
+        last[1:2, :] = jnp.broadcast_to(last[1:2, 0:1], (1, LANES))
         for k in range(SUMS):
             wide_sums[k : k + 1, :] = column_sum(sums[k * 8 : (k + 1) * 8, :])
 
@@ -1351,7 +1355,7 @@
         ada_bias=Vector(sums, (3, 0, HW), (4, 0, HW), (0, 0, HW)), time_weight=(features, joined_low), time_bias=row(8),
         cond_weight=(arrived, cond_low), cond_bias=row(8), input_weight=input_grad, input_bias=row(7),
     )
-    return last[1, 0], grads, cond_back
+    return last[1:2], grads, cond_back
 
 
 def time_features(times):
@@ -1434,7 +1438,7 @@
         loss = jnp.sum(owned[padded - 8, :ranks]) / divisor
         owned = owned[:size]
     else:
-        loss = lax.psum(loss_part, BOTH) / divisor
+        loss = lax.psum(loss_part[0, 0], BOTH) / divisor
         owned = lax.psum_scatter(full[: ranks * size].reshape(ranks, size, LANES), BOTH, scatter_dimension=0, tiled=False)
     owned = owned.reshape(-1)
     rate = 0.05 * math.sqrt(images * ranks * SEQ)

time: 780 us -> 776 us (level)
  no operation moved by 1% of the time
where the time goes in v5:
time: 776 us; the launch traced here: 768 us
  Pallas kernels  709 us (91%)
  other arithmetic  20 us (3%)
  local copies, waits for them, and re-layouts  18 us (2%)
  starting transfers between devices  15.4 us (2%)
    pallas_call x1, Pallas kernels, collect(): pl.pallas_call(functools.partial(collect_kernel, size), out_shape=(jax.Sh...  329 us
    pallas_call x1, Pallas kernels, spread(): pl.pallas_call(spread_kernel, out_shape=jax.ShapeDtypeStruct((32, padded,...  162 us
    pallas_call x2, Pallas kernels, fold(): pl.pallas_call(functools.partial(fold_kernel, products, items, plain, vec...  57.5 us
    pallas_call x1, Pallas kernels, head_pass(): pl.pallas_call(head_kernel, grid=(COPIES,), out_shape=[jax.ShapeDtypeStru...  45.4 us
    pallas_call x1, Pallas kernels, unfold(): pl.pallas_call(functools.partial(unfold_kernel, rows, padded, items), out...  33 us
    pallas_call x1, Pallas kernels, decode_back(): pl.pallas_call(decode_back_kernel, out_shape=backward_shapes(length, 16)...  23.6 us
    pallas_call x1, Pallas kernels, encode_back(): pl.pallas_call(encode_back_kernel, out_shape=backward_shapes(length, 8) +...  21.5 us
    pallas_call x1, Pallas kernels, encode(): pl.pallas_call(encode_kernel, out_shape=forward_shapes(length) + [jax.Sha...  18.6 us
  transfers between devices with their start and end apart: 2, of which 0 were waited for; matrix products, arithmetic and copies ran while one was open for 2% of the time, Pallas kernels for 3%

profile of v5, /device:TPU:21, one launch (start us, length us, event | category | flops | bytes accessed | tf_op | source)
XLA Modules:
  0.0 767.6 jit_solution(15286154978339397685)
XLA Ops:
  0.6 0.7 fusion.8
  1.3 0.1 concatenate.45
  1.4 0.6 broadcast_in_dim.55.keep_row
  2.0 0.8 broadcast_in_dim.66.keep_column
  2.7 162.5 %shard_map.120.g_ref = bf16[32,5520,128]{2,1,0:T(8,128)(2,1)} custom-call(f32[5511,128]{1,0:T(8,128)} %bitcast.169, s32[2,128]{1,0:T(2,128)} %bitcast.178), custom_call_target="tpu_custom_call" | custom-call | tf_op jit(solution)/shard_map/pallas_call | solution.py:615
  165.2 0.8 slice_bitcast_fusion.26
  166.0 1.3 slice_convert_fusion
  167.3 0.8 slice_bitcast_fusion.8
  168.2 0.0 copy-start.9
  168.2 33.0 %shard_map.121 = (bf16[3216,768]{1,0:T(8,128)(2,1)}, bf16[3088,1024]{1,0:T(8,128)(2,1)}, bf16[768,2304]{1,0:T(8,128)(2,1)S(1)}, bf16[768,3072]{1,0:T(8,128)(2,1)...) custom-call(bf16[32,5520,128]{2,1,0:T(8,128)(2,1)} %shard_map.120.g_ref), custom_call_target="tpu_custom_call" | custom-call | flops 21753856 | bytes 87015424 | tf_op jit(solution)/shard_map/pallas_call | solution.py:255
  201.2 0.0 copy-start
  201.2 1.8 copy-done
  202.9 1.9 copy-done.1
  206.1 0.1 pad.9.clone
  206.2 0.1 pad.10.clone
  206.3 0.0 copy-done.9
  206.3 0.1 copy.27.latents
  206.4 1.3 gather_fusion
  207.9 0.2 stack.6
  208.1 0.6 convert_element_type.95.table
  208.7 0.7 maximum_maximum_fusion.extra
  209.4 0.6 fusion.7
  210.0 0.0 copy-done.5
  210.0 18.6 %shard_map.122 = (bf16[320,768]{1,0:T(8,128)(2,1)}, bf16[320,2304]{1,0:T(8,128)(2,1)}, f32[320,128]{1,0:T(8,128)}, bf16[320,768]{1,0:T(8,128)(2,1)}, f32[320,768...) custom-call(bf16[256,16]{1,0:T(8,128)(2,1)} %copy-done.5, ...), custom_call_target="tpu_custom_call" | custom-call | flops 4907335680 | bytes 24182784 | tf_op jit(solution)/shard_map/pallas_call | solution.py:946
  228.6 0.0 copy-start.8
  228.6 0.0 copy-start.7
  228.6 0.0 copy-start.6
  228.6 18.2 %shard_map.123 = (bf16[320,768]{1,0:T(8,128)(2,1)}, bf16[320,2304]{1,0:T(8,128)(2,1)}, f32[320,128]{1,0:T(8,128)}, bf16[320,768]{1,0:T(8,128)(2,1)}, f32[320,768...) custom-call(f32[320,768]{1,0:T(8,128)} %get-tuple-element.73.before,, ...), custom_call_target="tpu_custom_call" | custom-call | flops 4529848320 | bytes 23003136 | tf_op jit(solution)/shard_map/pallas_call | solution.py:982
  246.9 10.0 %all-to-all-start = ((bf16[8,32,896]{2,1,0:T(8,128)(2,1)}), bf16[8,32,896]{2,1,0:T(8,128)(2,1)S(1)}, u32[]{:S(2)}, u32[]{:S(2)}) async-start(bf16[8,32,896]{2,1,0:T(8,128)(2,1)} %bitcast.174), calls=%async_computation | async-start | bytes 917504 | tf_op jit(solution)/shard_map/all_to_all | solution.py:1375
  256.9 0.0 copy-done.8
  256.9 0.1 sqrt_bitcast_fusion.1
  257.0 1.5 convert_reduce_fusion
  258.4 0.8 slice_bitcast_fusion
  259.2 0.8 slice.156
  260.0 0.0 copy-done.7
  260.0 0.8 copy.32.route
  260.9 1.1 copy.31.levels
  261.9 0.0 copy-done.6
  261.9 1.0 copy.30
  263.0 0.1 stack.7
  263.1 0.6 convert_element_type.104.wide_b
  263.7 0.9 reshape_reshape_squeeze.3.final_w
  265.3 2.2 fusion.2
  267.5 0.9 pad_maximum_fusion.features.refs_2_
  268.4 1.2 bitcast_convert_fusion.final_b
  269.6 0.0 all-to-all-done
  269.6 0.8 copy-done.3
  270.4 45.4 %shard_map.124 = (bf16[1024,1024]{1,0:T(8,128)(2,1)}, bf16[1024,3072]{1,0:T(8,128)(2,1)}, bf16[1024,1024]{1,0:T(8,128)(2,1)}, bf16[1024,1024]{1,0:T(8,128)(2,1)}...) custom-call(f32[1]{0:T(128)} %bitcast.2.divisor, ...), custom_call_target="tpu_custom_call" | custom-call | flops 22817013760 | bytes 27262976 | tf_op jit(solution)/shard_map/pallas_call | solution.py:1334
  315.8 0.7 slice_bitcast_fusion.30
  316.5 5.4 all-to-all-start.1
  321.9 1.8 reshape.285.refs_13_
  323.8 0.6 broadcast_select_fusion.refs_1_
  324.4 21.9 %shard_map.127.refs_28_ = f32[176368,128]{1,0:T(8,128)} custom-call(s32[1]{0:T(128)S(6)} %copy.102.label, f32[16,1024]{1,0:T(8,128)} %get-tuple-element.121.refs_0_, f32[8,128]{1,0:T(8,128)} %get-tuple-element.122.refs_1_, bf16[1024,256]{1,0:T(8,128)(2,1)} %pad_maximum_fusion.features.refs_2_, bf16[1024,1024]{1,0:T(8,128)(2,1)} %get-tuple-element.123.refs_3_, ...), custom_call_target="tpu_custom_call" | custom-call | flops 11676942336 | bytes 25338368 | tf_op jit(solution)/shard_map/pallas_call | solution.py:442
  346.2 0.0 all-to-all-done.1
  346.3 0.0 copy-start.4
  346.3 0.7 copy-done.4
  347.0 23.6 %shard_map.125 = (bf16[320,768]{1,0:T(8,128)(2,1)}, bf16[320,3072]{1,0:T(8,128)(2,1)}, bf16[320,768]{1,0:T(8,128)(2,1)}, bf16[320,2304]{1,0:T(8,128)(2,1)}, f32[...) custom-call(bf16[256,768]{1,0:T(8,128)(2,1)} %bitcast.172, ...), custom_call_target="tpu_custom_call" | custom-call | flops 4907335680 | bytes 24182784 | tf_op jit(solution)/shard_map/pallas_call | solution.py:1107
  370.6 21.5 %shard_map.126 = (bf16[320,768]{1,0:T(8,128)(2,1)}, bf16[320,3072]{1,0:T(8,128)(2,1)}, bf16[320,768]{1,0:T(8,128)(2,1)}, bf16[320,2304]{1,0:T(8,128)(2,1)}, f32[...) custom-call(f32[320,768]{1,0:T(8,128)} %get-tuple-element.87.leaving_grad, ...), custom_call_target="tpu_custom_call" | custom-call | flops 4529848320 | bytes 23003136 | tf_op jit(solution)/shard_map/pallas_call | solution.py:1144
  392.1 35.6 %shard_map.128.refs_0_ = f32[176368,128]{1,0:T(8,128)} custom-call(s32[1]{0:T(128)S(6)} %copy.102.label, f32[8,768]{1,0:T(8,128)} %get-tuple-element.93.refs_0_, f32[1,2304]{1,0:T(1,128)} %get-tuple-element.94.refs_1_, f32[1,3072]{1,0:T(1,128)} %get-tuple-element.95.refs_2_, f32[16,768]{1,0:T(8,128)} %get-tuple-element.96.refs_3_, ...), custom_call_target="tpu_custom_call", output_to_operand_aliasing={{}: (29, {})} | custom-call | flops 9437184000 | bytes 64951296 | tf_op jit(solution)/shard_map/pallas_call | solution.py:442
  427.7 0.0 copy-start.2
  427.7 328.8 %shard_map.129 = (f32[5520,128]{1,0:T(8,128)}, f32[96,920,128]{2,1,0:T(8,128)}) custom-call(f32[176368,128]{1,0:T(8,128)} %shard_map.128.refs_0_, f32[8,128]{1,0:T(8,128)} %broadcast_select_fusion.refs_1_), custom_call_target="tpu_custom_call" | custom-call | tf_op jit(solution)/shard_map/pallas_call | solution.py:796
  756.5 1.3 slice_reduce_fusion
  758.5 0.0 copy-done.2
  758.5 7.6 multiply_add_fusion
  (30 shorter events, 0.2 us)
Async XLA Ops:
  168.2 38.1 %copy-start.9 = (bf16[256,16]{0,1:T(8,128)(2,1)S(1)}, bf16[256,16]{0,1:T(8,128)(2,1)}, u32[]{:S(2)}) copy-start(bf16[256,16]{0,1:T(8,128)(2,1)} %param.9) | copy-start | bytes 24580
  201.2 1.8 copy-start
  202.9 1.9 copy-start.1
  206.4 3.6 copy-start.5
  228.6 28.3 %copy-start.8 = (s32[4,256]{1,0:T(4,128)S(1)}, s32[4,256]{1,0:T(4,128)}, u32[]{:S(2)}) copy-start(s32[4,256]{1,0:T(4,128)} %param.12) | copy-start | bytes 12292
  228.6 31.4 %copy-start.7 = (s32[256]{0:T(256)S(1)}, s32[256]{0:T(256)}, u32[]{:S(2)}) copy-start(s32[256]{0:T(256)} %param.10) | copy-start | bytes 3076
  228.6 33.3 %copy-start.6 = (f32[4,256,16]{1,2,0:T(8,128)S(1)}, f32[4,256,16]{1,2,0:T(8,128)}, u32[]{:S(2)}) copy-start(f32[4,256,16]{1,2,0:T(8,128)} %param.13) | copy-start | bytes 196612
  246.9 22.7 %all-to-all-start = ((bf16[8,32,896]{2,1,0:T(8,128)(2,1)}), bf16[8,32,896]{2,1,0:T(8,128)(2,1)S(1)}, u32[]{:S(2)}, u32[]{:S(2)}) async-start(bf16[8,32,896]{2,1,0:T(8,128)(2,1)} %bitcast.174), calls=%async_computation | async-start | bytes 917504 | tf_op jit(solution)/shard_map/all_to_all | solution.py:1375
  269.6 0.8 copy-start.3
  316.5 29.8 %all-to-all-start.1 = ((bf16[8,32,768]{2,1,0:T(8,128)(2,1)}), bf16[8,32,768]{2,1,0:T(8,128)(2,1)S(1)}, u32[]{:S(2)}, u32[]{:S(2)}) async-start(bf16[8,32,768]{2,1,0:T(8,128)(2,1)} %bitcast.175), calls=%async_computation.1 | async-start | bytes 786432 | tf_op jit(solution)/shard_map/all_to_all | solution.py:1375
  346.3 0.7 copy-start.4
  427.7 330.7 %copy-start.2 = (f32[705408]{0:T(1024)S(1)}, f32[705408]{0:T(1024)}, u32[]{:S(2)}) copy-start(f32[705408]{0:T(1024)} %param.15) | copy-start | bytes 8464900

commit v6 on v5

--- a/solution.py
+++ b/solution.py
@@ -291,7 +291,7 @@
     return stacks
 
 
-DEPTH = 3
+DEPTH = 5
 TALL = 256
 CHUNK = 512
 NEXT = 3

time: 776 us -> 773 us (level)
  no operation moved by 1% of the time
where the time goes in v6:
time: 773 us; the launch traced here: 764 us
  Pallas kernels  705 us (91%)
  other arithmetic  20 us (3%)
  local copies, waits for them, and re-layouts  18 us (2%)
  starting transfers between devices  15.4 us (2%)
    pallas_call x1, Pallas kernels, collect(): pl.pallas_call(functools.partial(collect_kernel, size), out_shape=(jax.Sh...  329 us
    pallas_call x1, Pallas kernels, spread(): pl.pallas_call(spread_kernel, out_shape=jax.ShapeDtypeStruct((32, padded,...  162 us
    pallas_call x2, Pallas kernels, fold(): pl.pallas_call(functools.partial(fold_kernel, products, items, plain, vec...  54.1 us
    pallas_call x1, Pallas kernels, head_pass(): pl.pallas_call(head_kernel, grid=(COPIES,), out_shape=[jax.ShapeDtypeStru...  45.4 us
    pallas_call x1, Pallas kernels, unfold(): pl.pallas_call(functools.partial(unfold_kernel, rows, padded, items), out...  33 us
    pallas_call x1, Pallas kernels, decode_back(): pl.pallas_call(decode_back_kernel, out_shape=backward_shapes(length, 16)...  23.6 us
    pallas_call x1, Pallas kernels, encode_back(): pl.pallas_call(encode_back_kernel, out_shape=backward_shapes(length, 8) +...  21.5 us
    pallas_call x1, Pallas kernels, encode(): pl.pallas_call(encode_kernel, out_shape=forward_shapes(length) + [jax.Sha...  18.6 us
  transfers between devices with their start and end apart: 2, of which 0 were waited for; matrix products, arithmetic and copies ran while one was open for 2% of the time, Pallas kernels for 3%

profile of v6, /device:TPU:21, one launch (start us, length us, event | category | flops | bytes accessed | tf_op | source)
XLA Modules:
  0.0 764.1 jit_solution(17996498803351698271)
XLA Ops:
  0.6 0.7 fusion.8
  1.3 0.1 concatenate.45
  1.4 0.6 broadcast_in_dim.55.keep_row
  2.0 0.8 broadcast_in_dim.66.keep_column
  2.7 162.5 %shard_map.120.g_ref = bf16[32,5520,128]{2,1,0:T(8,128)(2,1)} custom-call(f32[5511,128]{1,0:T(8,128)} %bitcast.169, s32[2,128]{1,0:T(2,128)} %bitcast.178), custom_call_target="tpu_custom_call" | custom-call | tf_op jit(solution)/shard_map/pallas_call | solution.py:615
  165.2 0.8 slice_bitcast_fusion.26
  166.0 1.3 slice_convert_fusion
  167.3 0.8 slice_bitcast_fusion.8
  168.2 0.0 copy-start.9
  168.2 33.0 %shard_map.121 = (bf16[3216,768]{1,0:T(8,128)(2,1)}, bf16[3088,1024]{1,0:T(8,128)(2,1)}, bf16[768,2304]{1,0:T(8,128)(2,1)S(1)}, bf16[768,3072]{1,0:T(8,128)(2,1)...) custom-call(bf16[32,5520,128]{2,1,0:T(8,128)(2,1)} %shard_map.120.g_ref), custom_call_target="tpu_custom_call" | custom-call | flops 21753856 | bytes 87015424 | tf_op jit(solution)/shard_map/pallas_call | solution.py:255
  201.2 0.0 copy-start
  201.2 1.8 copy-done
  202.9 1.9 copy-done.1
  206.1 0.1 pad.9.clone
  206.2 0.1 pad.10.clone
  206.3 0.0 copy-done.9
  206.3 0.1 copy.27.latents
  206.4 1.3 gather_fusion
  207.9 0.2 stack.6
  208.0 0.6 convert_element_type.95.table
  208.7 0.7 maximum_maximum_fusion.extra
  209.4 0.6 fusion.7
  210.0 0.0 copy-done.5
  210.0 18.6 %shard_map.122 = (bf16[320,768]{1,0:T(8,128)(2,1)}, bf16[320,2304]{1,0:T(8,128)(2,1)}, f32[320,128]{1,0:T(8,128)}, bf16[320,768]{1,0:T(8,128)(2,1)}, f32[320,768...) custom-call(bf16[256,16]{1,0:T(8,128)(2,1)} %copy-done.5, ...), custom_call_target="tpu_custom_call" | custom-call | flops 4907335680 | bytes 24182784 | tf_op jit(solution)/shard_map/pallas_call | solution.py:946
  228.6 0.0 copy-start.8
  228.6 0.0 copy-start.7
  228.6 0.0 copy-start.6
  228.6 18.2 %shard_map.123 = (bf16[320,768]{1,0:T(8,128)(2,1)}, bf16[320,2304]{1,0:T(8,128)(2,1)}, f32[320,128]{1,0:T(8,128)}, bf16[320,768]{1,0:T(8,128)(2,1)}, f32[320,768...) custom-call(f32[320,768]{1,0:T(8,128)} %get-tuple-element.73.before,, ...), custom_call_target="tpu_custom_call" | custom-call | flops 4529848320 | bytes 23003136 | tf_op jit(solution)/shard_map/pallas_call | solution.py:982
  246.8 10.0 %all-to-all-start = ((bf16[8,32,896]{2,1,0:T(8,128)(2,1)}), bf16[8,32,896]{2,1,0:T(8,128)(2,1)S(1)}, u32[]{:S(2)}, u32[]{:S(2)}) async-start(bf16[8,32,896]{2,1,0:T(8,128)(2,1)} %bitcast.174), calls=%async_computation | async-start | bytes 917504 | tf_op jit(solution)/shard_map/all_to_all | solution.py:1375
  256.9 0.0 copy-done.8
  256.9 0.1 sqrt_bitcast_fusion.1
  256.9 1.5 convert_reduce_fusion
  258.4 0.8 slice_bitcast_fusion
  259.2 0.8 slice.156
  260.0 0.0 copy-done.7
  260.0 0.8 copy.32.route
  260.8 1.1 copy.31.levels
  261.9 0.0 copy-done.6
  261.9 1.0 copy.30
  263.0 0.1 stack.7
  263.0 0.6 convert_element_type.104.wide_b
  263.7 0.9 reshape_reshape_squeeze.3.final_w
  265.3 2.2 fusion.2
  267.5 0.9 pad_maximum_fusion.features.refs_2_
  268.4 1.2 bitcast_convert_fusion.final_b
  269.6 0.0 all-to-all-done
  269.6 0.8 copy-done.3
  270.4 45.4 %shard_map.124 = (bf16[1024,1024]{1,0:T(8,128)(2,1)}, bf16[1024,3072]{1,0:T(8,128)(2,1)}, bf16[1024,1024]{1,0:T(8,128)(2,1)}, bf16[1024,1024]{1,0:T(8,128)(2,1)}...) custom-call(f32[1]{0:T(128)} %bitcast.2.divisor, ...), custom_call_target="tpu_custom_call" | custom-call | flops 22817013760 | bytes 27262976 | tf_op jit(solution)/shard_map/pallas_call | solution.py:1334
  315.8 0.7 slice_bitcast_fusion.30
  316.5 5.4 all-to-all-start.1
  321.9 1.8 reshape.285.refs_13_
  323.8 0.6 broadcast_select_fusion.refs_1_
  324.4 21.8 %shard_map.127.refs_28_ = f32[176368,128]{1,0:T(8,128)} custom-call(s32[1]{0:T(128)S(6)} %copy.102.label, f32[16,1024]{1,0:T(8,128)} %get-tuple-element.121.refs_0_, f32[8,128]{1,0:T(8,128)} %get-tuple-element.122.refs_1_, bf16[1024,256]{1,0:T(8,128)(2,1)} %pad_maximum_fusion.features.refs_2_, bf16[1024,1024]{1,0:T(8,128)(2,1)} %get-tuple-element.123.refs_3_, ...), custom_call_target="tpu_custom_call" | custom-call | flops 11676942336 | bytes 25338368 | tf_op jit(solution)/shard_map/pallas_call | solution.py:442
  346.2 0.0 all-to-all-done.1
  346.2 0.0 copy-start.4
  346.2 0.7 copy-done.4
  346.9 23.6 %shard_map.125 = (bf16[320,768]{1,0:T(8,128)(2,1)}, bf16[320,3072]{1,0:T(8,128)(2,1)}, bf16[320,768]{1,0:T(8,128)(2,1)}, bf16[320,2304]{1,0:T(8,128)(2,1)}, f32[...) custom-call(bf16[256,768]{1,0:T(8,128)(2,1)} %bitcast.172, ...), custom_call_target="tpu_custom_call" | custom-call | flops 4907335680 | bytes 24182784 | tf_op jit(solution)/shard_map/pallas_call | solution.py:1107
  370.5 21.5 %shard_map.126 = (bf16[320,768]{1,0:T(8,128)(2,1)}, bf16[320,3072]{1,0:T(8,128)(2,1)}, bf16[320,768]{1,0:T(8,128)(2,1)}, bf16[320,2304]{1,0:T(8,128)(2,1)}, f32[...) custom-call(f32[320,768]{1,0:T(8,128)} %get-tuple-element.87.leaving_grad, ...), custom_call_target="tpu_custom_call" | custom-call | flops 4529848320 | bytes 23003136 | tf_op jit(solution)/shard_map/pallas_call | solution.py:1144
  392.1 32.3 %shard_map.128.refs_0_ = f32[176368,128]{1,0:T(8,128)} custom-call(s32[1]{0:T(128)S(6)} %copy.102.label, f32[8,768]{1,0:T(8,128)} %get-tuple-element.93.refs_0_, f32[1,2304]{1,0:T(1,128)} %get-tuple-element.94.refs_1_, f32[1,3072]{1,0:T(1,128)} %get-tuple-element.95.refs_2_, f32[16,768]{1,0:T(8,128)} %get-tuple-element.96.refs_3_, ...), custom_call_target="tpu_custom_call", output_to_operand_aliasing={{}: (29, {})} | custom-call | flops 9437184000 | bytes 64951296 | tf_op jit(solution)/shard_map/pallas_call | solution.py:442
  424.3 0.0 copy-start.2
  424.3 328.6 %shard_map.129 = (f32[5520,128]{1,0:T(8,128)}, f32[96,920,128]{2,1,0:T(8,128)}) custom-call(f32[176368,128]{1,0:T(8,128)} %shard_map.128.refs_0_, f32[8,128]{1,0:T(8,128)} %broadcast_select_fusion.refs_1_), custom_call_target="tpu_custom_call" | custom-call | tf_op jit(solution)/shard_map/pallas_call | solution.py:796
  753.0 1.3 slice_reduce_fusion
  754.9 0.0 copy-done.2
  754.9 7.6 multiply_add_fusion
  (30 shorter events, 0.2 us)
Async XLA Ops:
  168.2 38.1 %copy-start.9 = (bf16[256,16]{0,1:T(8,128)(2,1)S(1)}, bf16[256,16]{0,1:T(8,128)(2,1)}, u32[]{:S(2)}) copy-start(bf16[256,16]{0,1:T(8,128)(2,1)} %param.9) | copy-start | bytes 24580
  201.2 1.8 copy-start
  202.9 1.9 copy-start.1
  206.4 3.5 copy-start.5
  228.6 28.3 %copy-start.8 = (s32[4,256]{1,0:T(4,128)S(1)}, s32[4,256]{1,0:T(4,128)}, u32[]{:S(2)}) copy-start(s32[4,256]{1,0:T(4,128)} %param.12) | copy-start | bytes 12292
  228.6 31.4 %copy-start.7 = (s32[256]{0:T(256)S(1)}, s32[256]{0:T(256)}, u32[]{:S(2)}) copy-start(s32[256]{0:T(256)} %param.10) | copy-start | bytes 3076
  228.6 33.3 %copy-start.6 = (f32[4,256,16]{1,2,0:T(8,128)S(1)}, f32[4,256,16]{1,2,0:T(8,128)}, u32[]{:S(2)}) copy-start(f32[4,256,16]{1,2,0:T(8,128)} %param.13) | copy-start | bytes 196612
  246.8 22.7 %all-to-all-start = ((bf16[8,32,896]{2,1,0:T(8,128)(2,1)}), bf16[8,32,896]{2,1,0:T(8,128)(2,1)S(1)}, u32[]{:S(2)}, u32[]{:S(2)}) async-start(bf16[8,32,896]{2,1,0:T(8,128)(2,1)} %bitcast.174), calls=%async_computation | async-start | bytes 917504 | tf_op jit(solution)/shard_map/all_to_all | solution.py:1375
  269.6 0.8 copy-start.3
  316.5 29.7 %all-to-all-start.1 = ((bf16[8,32,768]{2,1,0:T(8,128)(2,1)}), bf16[8,32,768]{2,1,0:T(8,128)(2,1)S(1)}, u32[]{:S(2)}, u32[]{:S(2)}) async-start(bf16[8,32,768]{2,1,0:T(8,128)(2,1)} %bitcast.175), calls=%async_computation.1 | async-start | bytes 786432 | tf_op jit(solution)/shard_map/all_to_all | solution.py:1375
  346.2 0.7 copy-start.4
  424.3 330.6 %copy-start.2 = (f32[705408]{0:T(1024)S(1)}, f32[705408]{0:T(1024)}, u32[]{:S(2)}) copy-start(f32[705408]{0:T(1024)} %param.15) | copy-start | bytes 8464900
